TPU v7x, 32 devices: a whole 2x2x4 slice. The times are simulated.
32 devices in a mesh: dp: 4 (over y, x), ctx: 8 (over z, core).
Axes of the slice: x: 2, y: 2, z: 4, core: 2. Of those that a mesh axis runs over, the one named last changes fastest.
Arguments:
- tokens: bfloat16 [8, 2560, 1024], P('dp', 'ctx'), may hold values from -6 to 6
- cotangent: bfloat16 [8, 2560, 1024], P('dp', 'ctx'), may hold values from -6 to 6
- segment_ids: int32 [8, 2560], P('dp'), may hold values from 0 to 12, as said below
- positions: int32 [8, 2560], P('dp'), may hold values from 0 to 1279, as said below
- parents: int32 [8, 13], P('dp'), may hold values from 0 to 4, as said below
- input_norm: bfloat16 [1024], P(('dp', 'ctx')), may hold values from 0.25 to 1.75
- query_proj: bfloat16 [1024, 2048], P(('dp', 'ctx')), may hold values from -0.1875 to 0.1875
- key_proj: bfloat16 [1024, 1024], P(('dp', 'ctx')), may hold values from -0.1875 to 0.1875
- value_proj: bfloat16 [1024, 1024], P(('dp', 'ctx')), may hold values from -0.1875 to 0.1875
- query_norm: bfloat16 [128], P(('dp', 'ctx')), may hold values from 0.25 to 1.75
- key_norm: bfloat16 [128], P(('dp', 'ctx')), may hold values from 0.25 to 1.75
- out_proj: bfloat16 [2048, 1024], P(None, ('dp', 'ctx')), may hold values from -1 to 1
- post_norm: bfloat16 [1024], P(('dp', 'ctx')), may hold values from 0.25 to 1.75
- gate_proj: bfloat16 [1024, 3072], P(('dp', 'ctx')), may hold values from -0.1875 to 0.1875
- up_proj: bfloat16 [1024, 3072], P(('dp', 'ctx')), may hold values from -0.1875 to 0.1875
- down_proj: bfloat16 [3072, 1024], P(None, ('dp', 'ctx')), may hold values from -0.109375 to 0.109375
Outputs:
- output: bfloat16 [8, 2560, 1024], P('dp', 'ctx')
- input_grad: float32 [8, 2560, 1024], P('dp', 'ctx')
- input_norm_grad: float32 [1024], P(('dp', 'ctx'))
- query_proj_grad: float32 [1024, 2048], P(('dp', 'ctx'))
- key_proj_grad: float32 [1024, 1024], P(('dp', 'ctx'))
- value_proj_grad: float32 [1024, 1024], P(('dp', 'ctx'))
- query_norm_grad: float32 [128], P(('dp', 'ctx'))
- key_norm_grad: float32 [128], P(('dp', 'ctx'))
- out_proj_grad: float32 [2048, 1024], P(None, ('dp', 'ctx'))
- post_norm_grad: float32 [1024], P(('dp', 'ctx'))
- gate_proj_grad: float32 [1024, 3072], P(('dp', 'ctx'))
- up_proj_grad: float32 [1024, 3072], P(('dp', 'ctx'))
- down_proj_grad: float32 [3072, 1024], P(None, ('dp', 'ctx'))
Inputs may be any that keep to these rules, and one draw needn't show every extreme that they name: `parents`: in every tree segment 0 is the trunk and its own parent; segments 1 to 4 have parent 0; each later segment has a parent among 1 to 4, and each of these has exactly 2 children. `segment_ids`: in every tree tokens 0 to 1023 are segment 0; the other tokens form aligned runs of 128, one run for each other segment, in an order that varies from tree to tree. `positions`: trunk token t has position t; the k-th token of a branch segment has 1024 + k, of a leaf segment 1024 + 128 + k.
All inputs are finite; a program needn't handle non-finite values.
Results may differ from a plain program's by a relative error of at most 0.018.
Values may be sent and summed in bfloat16 or wider, within the bound.
A program may use at most 448 MiB of HBM per device.

v0:
```python
import jax
import jax.numpy as jnp
from jax import lax
from jax.sharding import PartitionSpec as P

D = 1024
HEADS = 16
KV_HEADS = 8
HEAD_DIM = 128
FF = 3072
MICRO = 2
TR = 1


eps_norm = 1e-06
rope_base = 1000000.0
path_levels = 3
masked_score = -1e30


def matmul(left_side, right_side):
    return jnp.dot(left_side, right_side, preferred_element_type=jnp.float32)


def contract_rows(left_side, right_side):
    return lax.dot_general(
        left_side, right_side, (((0,), (0,)), ((), ())), preferred_element_type=jnp.float32
    )


def norm_forward(values, weight):
    factor = lax.rsqrt(jnp.mean(values * values, axis=-1, keepdims=True) + eps_norm)
    normed = values * factor
    return (normed * weight, normed, factor)


def norm_backward(grad_out, weight, normed, factor):
    weighted = grad_out * weight
    grad_in = factor * (weighted - normed * jnp.mean(weighted * normed, axis=-1, keepdims=True))
    return (grad_in, grad_out * normed)


def rotate(values, cosine, sine_table):
    middle = values.shape[-1] // 2
    turned = jnp.concatenate([-values[..., middle:], values[..., :middle]], axis=-1)
    return values * cosine + turned * sine_table


def rotate_back(gradient, cosine, sine_table):
    middle = gradient.shape[-1] // 2
    moved = gradient * sine_table
    return gradient * cosine + jnp.concatenate([moved[..., middle:], -moved[..., :middle]], axis=-1)


def rope_tables(positions):
    steps_half = jnp.arange(HEAD_DIM // 2, dtype=jnp.float32)
    inverse = rope_base ** (-(steps_half * 2.0 / HEAD_DIM))
    angles = positions.astype(jnp.float32)[:, None] * inverse[None, :]
    angles = jnp.concatenate([angles, angles], axis=-1)
    return (jnp.cos(angles)[:, None, :], jnp.sin(angles)[:, None, :])


def ancestor_table(parent_tree):
    seg_count = parent_tree.shape[0]
    seg_index = jnp.arange(seg_count, dtype=jnp.int32)
    current = seg_index
    ancestry = jnp.zeros((seg_count, seg_count), jnp.float32)
    for level_index in range(path_levels):
        matches = current[:, None] == seg_index[None, :]
        ancestry = jnp.maximum(ancestry, matches.astype(jnp.float32))
        current = jnp.sum(jnp.where(matches, parent_tree[None, :], 0), axis=1)
    return ancestry


def visible_keys(ancestry, seg_rows, pos_rows, seg_cols, pos_cols):
    seg_count = ancestry.shape[0]
    seg_index = jnp.arange(seg_count, dtype=jnp.int32)
    rows_onehot = (seg_rows[:, None] == seg_index[None, :]).astype(jnp.float32)
    cols_onehot = (seg_cols[:, None] == seg_index[None, :]).astype(jnp.float32)
    reaches = jnp.dot(jnp.dot(rows_onehot, ancestry), cols_onehot.T)
    return (reaches > 0.5) & (pos_cols[None, :] <= pos_rows[:, None])


def attend_forward(tree_item):
    queries, key_block, value_block, allowed = tree_item
    raw_scores = jnp.einsum(
        "rkgd,tkd->kgrt", queries, key_block, preferred_element_type=jnp.float32
    )
    scores = jnp.where(allowed, raw_scores * HEAD_DIM ** (-0.5), masked_score)
    top_score = jnp.max(scores, axis=-1, keepdims=True)
    exponent = jnp.exp(scores - top_score)
    totals = jnp.sum(exponent, axis=-1, keepdims=True)
    weights_low = (exponent / totals).astype(jnp.bfloat16)
    mixed_heads = jnp.einsum(
        "kgrt,tkd->rkgd", weights_low, value_block, preferred_element_type=jnp.float32
    )
    return (mixed_heads, top_score + jnp.log(totals))


def attend_backward(tree_item):
    queries, key_block, value_block, allowed, log_total, grad_mixed = tree_item
    raw_scores = jnp.einsum(
        "rkgd,tkd->kgrt", queries, key_block, preferred_element_type=jnp.float32
    )
    scores = jnp.where(allowed, raw_scores * HEAD_DIM ** (-0.5), masked_score)
    weights_soft = jnp.exp(scores - log_total)
    grad_soft = jnp.einsum(
        "rkgd,tkd->kgrt", grad_mixed, value_block, preferred_element_type=jnp.float32
    )
    inner_sum = jnp.sum(weights_soft * grad_soft, axis=-1, keepdims=True)
    grad_raw = (weights_soft * (grad_soft - inner_sum) * HEAD_DIM ** (-0.5)).astype(jnp.bfloat16)
    grad_queries = jnp.einsum(
        "kgrt,tkd->rkgd", grad_raw, key_block, preferred_element_type=jnp.float32
    )
    grad_keys = jnp.einsum("kgrt,rkgd->tkd", grad_raw, queries, preferred_element_type=jnp.float32)
    grad_values = jnp.einsum(
        "kgrt,rkgd->tkd",
        weights_soft.astype(jnp.bfloat16),
        grad_mixed,
        preferred_element_type=jnp.float32,
    )
    return (grad_queries, grad_keys, grad_values)


def shards(
    tokens,
    cotangent,
    segment_ids,
    positions,
    parents,
    input_norm,
    query_proj,
    key_proj,
    value_proj,
    query_norm,
    key_norm,
    out_proj,
    post_norm,
    gate_proj,
    up_proj,
    down_proj,
):
    tree_rows = tokens.shape[1]
    row_start = lax.axis_index("ctx") * tree_rows
    shard_rows = query_proj.shape[0]
    groups = HEADS // KV_HEADS
    query_width = HEADS * HEAD_DIM
    kv_width = KV_HEADS * HEAD_DIM
    count_rows = TR * tree_rows
    attention_width = 2 * query_width + 2 * kv_width

    def attention_weights():
        return (
            lax.all_gather(input_norm, ("dp", "ctx"), axis=0, tiled=True),
            lax.all_gather(query_proj, ("dp", "ctx"), axis=0, tiled=True),
            lax.all_gather(key_proj, ("dp", "ctx"), axis=0, tiled=True),
            lax.all_gather(value_proj, ("dp", "ctx"), axis=0, tiled=True),
            lax.all_gather(query_norm, ("dp", "ctx"), axis=0, tiled=True),
            lax.all_gather(key_norm, ("dp", "ctx"), axis=0, tiled=True),
            lax.all_gather(out_proj, ("dp", "ctx"), axis=1, tiled=True),
        )

    def feed_weights():
        return (
            lax.all_gather(post_norm, ("dp", "ctx"), axis=0, tiled=True),
            lax.all_gather(gate_proj, ("dp", "ctx"), axis=0, tiled=True),
            lax.all_gather(up_proj, ("dp", "ctx"), axis=0, tiled=True),
            lax.all_gather(down_proj, ("dp", "ctx"), axis=1, tiled=True),
        )

    attention_whole = jnp.zeros((D, attention_width), jnp.float32)
    feed_whole = jnp.zeros((D, 3 * FF), jnp.float32)
    in_gain_sum = jnp.zeros((D,), jnp.float32)
    post_gain_sum = jnp.zeros((D,), jnp.float32)
    query_gain_sum = jnp.zeros((HEAD_DIM,), jnp.float32)
    key_gain_sum = jnp.zeros((HEAD_DIM,), jnp.float32)
    outputs_list = []
    input_grads = []
    for batch_index in range(MICRO):
        tree_first = batch_index * TR
        inputs = tokens[tree_first : tree_first + TR].reshape(count_rows, D).astype(jnp.float32)
        seg_trees = segment_ids[tree_first : tree_first + TR]
        pos_trees = positions[tree_first : tree_first + TR]
        seg_local = lax.dynamic_slice_in_dim(seg_trees, row_start, tree_rows, 1)
        pos_local = lax.dynamic_slice_in_dim(pos_trees, row_start, tree_rows, 1)
        ancestries = jax.vmap(ancestor_table)(parents[tree_first : tree_first + TR])
        allowed = jax.vmap(visible_keys)(ancestries, seg_local, pos_local, seg_trees, pos_trees)
        cosine_table, sine_table = rope_tables(pos_local.reshape(count_rows))
        in_gain, query_full, key_full, value_full, query_gain, key_gain, out_full = (
            attention_weights()
        )
        in_weight = in_gain.astype(jnp.float32)
        query_weight = query_gain.astype(jnp.float32)
        key_weight = key_gain.astype(jnp.float32)
        normed_in, in_hat, in_factor = norm_forward(inputs, in_weight)
        normed_low = normed_in.astype(jnp.bfloat16)
        query_pre = matmul(normed_low, query_full).reshape(count_rows, HEADS, HEAD_DIM)
        key_pre = matmul(normed_low, key_full).reshape(count_rows, KV_HEADS, HEAD_DIM)
        value_low = matmul(normed_low, value_full).astype(jnp.bfloat16)
        query_normed, query_hat, query_factor = norm_forward(query_pre, query_weight)
        key_normed, key_hat, key_factor = norm_forward(key_pre, key_weight)
        query_low = rotate(query_normed, cosine_table, sine_table).astype(jnp.bfloat16)
        key_low = rotate(key_normed, cosine_table, sine_table).astype(jnp.bfloat16)
        tree_keys, tree_values = (
            lax.all_gather(
                key_low.reshape(TR, tree_rows, KV_HEADS, HEAD_DIM), "ctx", axis=1, tiled=True
            ),
            lax.all_gather(
                value_low.reshape(TR, tree_rows, KV_HEADS, HEAD_DIM), "ctx", axis=1, tiled=True
            ),
        )
        query_trees = query_low.reshape(TR, tree_rows, KV_HEADS, groups, HEAD_DIM)
        mixed_heads, log_total = lax.map(
            attend_forward, (query_trees, tree_keys, tree_values, allowed)
        )
        mixed_low = mixed_heads.reshape(count_rows, query_width).astype(jnp.bfloat16)
        hidden = inputs + matmul(mixed_low, out_full)
        post_gain, gate_full, up_full, down_full = feed_weights()
        post_weight = post_gain.astype(jnp.float32)
        normed_post, post_hat, post_factor = norm_forward(hidden, post_weight)
        second_low = normed_post.astype(jnp.bfloat16)
        gate_pre = matmul(second_low, gate_full)
        up_pre = matmul(second_low, up_full)
        activated = jax.nn.silu(gate_pre)
        inner_low = (activated * up_pre).astype(jnp.bfloat16)
        result = hidden + matmul(inner_low, down_full)
        outputs_list.append(result.astype(jnp.bfloat16).reshape(TR, tree_rows, D))
        post_gain, gate_full, up_full, down_full = feed_weights()
        grad_out = cotangent[tree_first : tree_first + TR].reshape(count_rows, D)
        grad_inner = matmul(grad_out, down_full.T)
        sigmoid_gate = jax.nn.sigmoid(gate_pre)
        grad_gate = (
            grad_inner * up_pre * sigmoid_gate * (1.0 + gate_pre * (1.0 - sigmoid_gate))
        ).astype(jnp.bfloat16)
        grad_up = (grad_inner * activated).astype(jnp.bfloat16)
        grad_gate_up = jnp.concatenate([grad_gate, grad_up], axis=1)
        grad_second = matmul(grad_gate, gate_full.T) + matmul(grad_up, up_full.T)
        grad_post_in, post_part = norm_backward(grad_second, post_weight, post_hat, post_factor)
        grad_hidden = grad_out.astype(jnp.float32) + grad_post_in
        post_gain_sum = post_gain_sum + jnp.sum(post_part, axis=0)
        in_gain, query_full, key_full, value_full, query_gain, key_gain, out_full = (
            attention_weights()
        )
        grad_branch = grad_hidden.astype(jnp.bfloat16)
        grad_mixed = matmul(grad_branch, out_full.T).astype(jnp.bfloat16)
        grad_queries, grad_keys, grad_values = lax.map(
            attend_backward,
            (
                query_trees,
                tree_keys,
                tree_values,
                allowed,
                log_total,
                grad_mixed.reshape(TR, tree_rows, KV_HEADS, groups, HEAD_DIM),
            ),
        )
        key_grad_local, value_grad_local = (
            lax.psum_scatter(
                grad_keys.astype(jnp.bfloat16), "ctx", scatter_dimension=1, tiled=True
            ).astype(jnp.float32),
            lax.psum_scatter(
                grad_values.astype(jnp.bfloat16), "ctx", scatter_dimension=1, tiled=True
            ).astype(jnp.float32),
        )
        grad_query_normed = rotate_back(
            grad_queries.reshape(count_rows, HEADS, HEAD_DIM), cosine_table, sine_table
        )
        grad_query_pre, query_part = norm_backward(
            grad_query_normed, query_weight, query_hat, query_factor
        )
        grad_key_normed = rotate_back(
            key_grad_local.reshape(count_rows, KV_HEADS, HEAD_DIM), cosine_table, sine_table
        )
        grad_key_pre, key_part = norm_backward(grad_key_normed, key_weight, key_hat, key_factor)
        query_gain_sum = query_gain_sum + jnp.sum(query_part, axis=(0, 1))
        key_gain_sum = key_gain_sum + jnp.sum(key_part, axis=(0, 1))
        grad_query_low = grad_query_pre.reshape(count_rows, query_width).astype(jnp.bfloat16)
        grad_key_low = grad_key_pre.reshape(count_rows, kv_width).astype(jnp.bfloat16)
        grad_value_low = value_grad_local.reshape(count_rows, kv_width).astype(jnp.bfloat16)
        grad_projected = jnp.concatenate([grad_query_low, grad_key_low, grad_value_low], axis=1)
        grad_normed = (
            matmul(grad_query_low, query_full.T)
            + matmul(grad_key_low, key_full.T)
            + matmul(grad_value_low, value_full.T)
        )
        grad_in_norm, in_part = norm_backward(grad_normed, in_weight, in_hat, in_factor)
        in_gain_sum = in_gain_sum + jnp.sum(in_part, axis=0)
        input_grads.append((grad_hidden + grad_in_norm).reshape(TR, tree_rows, D))
        left_part = contract_rows(normed_low, grad_projected)
        right_part = contract_rows(grad_branch, mixed_low)
        attention_whole = attention_whole + jnp.concatenate([left_part, right_part], axis=1)
        feed_left_part = contract_rows(second_low, grad_gate_up)
        feed_right_part = contract_rows(grad_out, inner_low)
        feed_whole = feed_whole + jnp.concatenate([feed_left_part, feed_right_part], axis=1)
    attention_shard = lax.psum_scatter(
        (lambda first_row, row_count: attention_whole)(
            jnp.int32(0), shard_rows * lax.axis_size(("dp", "ctx"))
        ),
        ("dp", "ctx"),
        scatter_dimension=0,
        tiled=True,
    )
    feed_shard = lax.psum_scatter(
        (lambda first_row, row_count: feed_whole)(
            jnp.int32(0), shard_rows * lax.axis_size(("dp", "ctx"))
        ),
        ("dp", "ctx"),
        scatter_dimension=0,
        tiled=True,
    )
    in_grad, post_grad, query_gain_grad, key_gain_grad = (
        lax.psum_scatter(in_gain_sum, ("dp", "ctx"), scatter_dimension=0, tiled=True),
        lax.psum_scatter(post_gain_sum, ("dp", "ctx"), scatter_dimension=0, tiled=True),
        lax.psum_scatter(query_gain_sum, ("dp", "ctx"), scatter_dimension=0, tiled=True),
        lax.psum_scatter(key_gain_sum, ("dp", "ctx"), scatter_dimension=0, tiled=True),
    )
    query_grad = attention_shard[:, :query_width]
    key_grad = attention_shard[:, query_width : query_width + kv_width]
    value_grad = attention_shard[:, query_width + kv_width : query_width + 2 * kv_width]
    out_grad = attention_shard[:, query_width + 2 * kv_width :].T
    gate_grad = feed_shard[:, :FF]
    up_grad = feed_shard[:, FF : 2 * FF]
    down_grad = feed_shard[:, 2 * FF :].T
    output = jnp.concatenate(outputs_list, axis=0)
    input_grad = jnp.concatenate(input_grads, axis=0)
    return (
        output,
        input_grad,
        in_grad,
        query_grad,
        key_grad,
        value_grad,
        query_gain_grad,
        key_gain_grad,
        out_grad,
        post_grad,
        gate_grad,
        up_grad,
        down_grad,
    )


def solution(mesh):
    return jax.shard_map(
        shards,
        mesh=mesh,
        in_specs=(
            P("dp", "ctx", None),
            P("dp", "ctx", None),
            P("dp", None),
            P("dp", None),
            P("dp", None),
            P(("dp", "ctx")),
            P(("dp", "ctx"), None),
            P(("dp", "ctx"), None),
            P(("dp", "ctx"), None),
            P(("dp", "ctx")),
            P(("dp", "ctx")),
            P(None, ("dp", "ctx")),
            P(("dp", "ctx")),
            P(("dp", "ctx"), None),
            P(("dp", "ctx"), None),
            P(None, ("dp", "ctx")),
        ),
        out_specs=(
            P("dp", "ctx", None),
            P("dp", "ctx", None),
            P(("dp", "ctx")),
            P(("dp", "ctx"), None),
            P(("dp", "ctx"), None),
            P(("dp", "ctx"), None),
            P(("dp", "ctx")),
            P(("dp", "ctx")),
            P(None, ("dp", "ctx")),
            P(("dp", "ctx")),
            P(("dp", "ctx"), None),
            P(("dp", "ctx"), None),
            P(None, ("dp", "ctx")),
        ),
        check_vma=False,
    )
```

profile of v0, /device:TPU:0, one launch (start us, length us, event | category | flops | bytes accessed | tf_op | source)
XLA Modules:
  0.0 1877.2 jit_solution(12937188276462766737)
XLA Ops:
  12.8 42.3 %all-reduce.9 = (bf16[1024]{0:T(1024)(128)(2,1)S(1)}, bf16[128]{0:T(256)(128)(2,1)S(1)}, bf16[128]{0:T(256)(128)(2,1)S(1)}, bf16[1024]{0:T(1024)(128)(2,1)S(1)}) all-reduce(bf16[1024]{0:T(1024)(128)(2,1)S(1)} %dynamic-update-slice, bf16[128]{0:T(256)(128)(2,1)S(1)} %dynamic-update-slice.2, ...), channel_id=1, replica_groups=mesh['dp'=4,'ctx'=8] {'dp','ctx'}, use_global_device_ids=true, to_apply=%add | all-reduce | flops 2304 | bytes 9216
  81.2 47.4 %all-gather.14.cloned.1.call-done = bf16[1024,1024]{1,0:T(8,128)(2,1)} async-done(((bf16[32,1024]{1,0:T(8,128)(2,1)}), bf16[1024,1024]{1,0:T(8,128)(2,1)}) %all-gather.14.cloned.1.call-update) | async-done | bytes 2097168 | tf_op jit(solution)/shard_map/all_gather | solution.py:157
  145.8 46.9 %all-gather.20.cloned.1.call-done = bf16[1024,2048]{1,0:T(8,128)(2,1)} async-done(((bf16[32,2048]{1,0:T(8,128)(2,1)}), bf16[1024,2048]{1,0:T(8,128)(2,1)}) %all-gather.20.cloned.1.call-update) | async-done | bytes 4194320 | tf_op jit(solution)/shard_map/all_gather | solution.py:155
  211.9 37.4 %all-gather.34.cloned.1.call-done = bf16[2560,8,128]{2,0,1:T(8,128)(2,1)} async-done(((bf16[320,8,128]{2,0,1:T(8,128)(2,1)}), bf16[2560,8,128]{2,0,1:T(8,128)(2,1)}) %all-gather.34.cloned.1.call-update) | async-done | bytes 5242896 | tf_op jit(solution)/shard_map/all_gather | solution.py:205
  249.3 22.8 %fusion.228 = (f32[8,2,320]{2,1,0:T(2,128)S(1)}, f32[8,2,320,2560]{3,2,1,0:T(8,128)}) fusion(bf16[320,8,2,128]{3,0,2,1:T(8,128)(2,1)S(1)} %bitcast.418, bf16[2560,8,128]{2,0,1:T(8,128)(2,1)} %all-gather.34.cloned.1.call-done, pred[320,2560]{1,0:T(8,128)(4,1)S(1)} %fusion.59), kind=kOutput, calls=%fused_computation.343 | convolution fusion | flops 3394759680 | bytes 59822080 | tf_op jit(solution)/shard_map/while/body/eval_jaxpr/rkgd,tkd->kgrt/dot_general | solution.py:86
  305.6 21.3 %fusion.99 = bf16[320,8,2,128]{3,0,2,1:T(8,128)(2,1)S(1)} fusion(f32[8,2,320,2560]{3,2,1,0:T(8,128)} %get-tuple-element.210, f32[8,2,320]{2,1,0:T(2,128)S(1)} %fusion.9, f32[8,2,320]{2,1,0:T(2,128)S(1)} %get-tuple-element.209, bf16[1,2560,8,128]{3,1,2,0:T(8,128)(2,1)} %all-gather.30.cloned.1.call-done), kind=kOutput, calls=%fused_computation.150 | convolution fusion | flops 3395420160 | bytes 59023360 | tf_op jit(solution)/shard_map/while/body/eval_jaxpr/kgrt,tkd->rkgd/dot_general | solution.py:94
  326.9 35.0 %all-gather.32.cloned.1.call-done = bf16[2560,8,128]{2,0,1:T(8,128)(2,1)} async-done(((bf16[320,8,128]{2,0,1:T(8,128)(2,1)}), bf16[2560,8,128]{2,0,1:T(8,128)(2,1)}) %all-gather.32.cloned.1.call-update) | async-done | bytes 5242896 | tf_op jit(solution)/shard_map/all_gather | solution.py:205
  361.9 22.9 %fusion.229 = (f32[8,2,320]{2,1,0:T(2,128)S(1)}, f32[8,2,320,2560]{3,2,1,0:T(8,128)}) fusion(bf16[320,8,2,128]{3,0,2,1:T(8,128)(2,1)S(1)} %bitcast.421, bf16[2560,8,128]{2,0,1:T(8,128)(2,1)} %all-gather.32.cloned.1.call-done, pred[320,2560]{1,0:T(8,128)(4,1)S(1)} %fusion.58), kind=kOutput, calls=%fused_computation.344 | convolution fusion | flops 3394759680 | bytes 59822080 | tf_op jit(solution)/shard_map/while/body/eval_jaxpr/rkgd,tkd->kgrt/dot_general | solution.py:86
  444.2 38.1 %all-gather.22.cloned.1.call-done = bf16[2048,1024]{0,1:T(8,128)(2,1)} async-done(((bf16[2048,32]{0,1:T(8,128)(2,1)}), bf16[2048,1024]{0,1:T(8,128)(2,1)}) %all-gather.22.cloned.1.call-update) | async-done | bytes 4194320 | tf_op jit(solution)/shard_map/all_gather | solution.py:160
  489.6 63.7 %all-gather.24.cloned.1.call-done = bf16[1024,3072]{1,0:T(8,128)(2,1)} async-done(((bf16[32,3072]{1,0:T(8,128)(2,1)}), bf16[1024,3072]{1,0:T(8,128)(2,1)}) %all-gather.24.cloned.1.call-update) | async-done | bytes 6291472 | tf_op jit(solution)/shard_map/all_gather | solution.py:166
  560.2 64.0 %all-gather.26.cloned.1.call-done = bf16[1024,3072]{1,0:T(8,128)(2,1)} async-done(((bf16[32,3072]{1,0:T(8,128)(2,1)}), bf16[1024,3072]{1,0:T(8,128)(2,1)}) %all-gather.26.cloned.1.call-update) | async-done | bytes 6291472 | tf_op jit(solution)/shard_map/all_gather | solution.py:167
  631.0 64.1 %all-gather.28.cloned.1.call-done = bf16[3072,1024]{0,1:T(8,128)(2,1)} async-done(((bf16[3072,32]{0,1:T(8,128)(2,1)}), bf16[3072,1024]{0,1:T(8,128)(2,1)}) %all-gather.28.cloned.1.call-update) | async-done | bytes 6291472 | tf_op jit(solution)/shard_map/all_gather | solution.py:168
  748.0 21.8 %fusion.40 = bf16[1,2560,8,128]{1,3,2,0:T(8,128)(2,1)} fusion(f32[8,2,320,2560]{3,2,1,0:T(8,128)} %get-tuple-element.212, f32[8,2,320]{2,1,0:T(2,128)S(1)} %bitcast.438, bf16[320,8,2,128]{3,2,1,0:T(2,128)(2,1)S(1)} %squeeze.66), kind=kOutput, calls=%fused_computation.54 | convolution fusion | flops 3384279040 | bytes 59002880 | tf_op jit(solution)/shard_map/while/body/eval_jaxpr/kgrt,rkgd->tkd/dot_general | solution.py:116
  778.2 21.3 %fusion.35 = f32[8,2560,320,2]{1,2,3,0:T(8,128)} fusion(bf16[1,2560,8,128]{3,1,2,0:T(8,128)(2,1)} %all-gather.16.cloned.1.call-done, bf16[320,8,2,128]{3,2,1,0:T(2,128)(2,1)S(1)} %squeeze.66), kind=kOutput, calls=%fused_computation.49 | convolution fusion | flops 3355443200 | bytes 58982400 | tf_op jit(solution)/shard_map/while/body/eval_jaxpr/rkgd,tkd->kgrt/dot_general | solution.py:107
  799.5 92.5 %fusion.46 = bf16[1,2560,8,128]{3,1,2,0:T(8,128)(2,1)} fusion(bf16[320,8,2,128]{3,0,2,1:T(8,128)(2,1)} %bitcast.420, f32[8,2560,320,2]{1,2,3,0:T(8,128)} %fusion.35, f32[8,2,320,2560]{3,2,1,0:T(8,128)} %get-tuple-element.212, f32[8,2,320]{2,1,0:T(2,128)S(1)} %bitcast.439), kind=kOutput, calls=%fused_computation.56 | convolution fusion | flops 3449822720 | bytes 111431680 | tf_op jit(solution)/shard_map/while/body/eval_jaxpr/kgrt,rkgd->tkd/dot_general | solution.py:115
  918.3 92.1 %fusion.47 = bf16[1,2560,8,128]{3,1,2,0:T(8,128)(2,1)} fusion(bf16[320,8,2,128]{3,0,2,1:T(8,128)(2,1)S(1)} %bitcast.419, f32[8,2560,320,2]{1,2,3,0:T(8,128)} %fusion.30, f32[8,2,320,2560]{3,2,1,0:T(8,128)} %get-tuple-element.210, f32[8,2,320]{2,1,0:T(2,128)S(1)} %bitcast.441), kind=kOutput, calls=%fused_computation.57 | convolution fusion | flops 3449822720 | bytes 111431680 | tf_op jit(solution)/shard_map/while/body/eval_jaxpr/kgrt,rkgd->tkd/dot_general | solution.py:115
  1010.5 22.2 %fusion.43 = bf16[1,2560,8,128]{1,3,2,0:T(8,128)(2,1)} fusion(f32[8,2,320,2560]{3,2,1,0:T(8,128)} %get-tuple-element.210, f32[8,2,320]{2,1,0:T(2,128)S(1)} %bitcast.442, bf16[320,8,2,128]{3,2,1,0:T(2,128)(2,1)S(1)} %squeeze.67), kind=kOutput, calls=%fused_computation.55 | convolution fusion | flops 3384279040 | bytes 59002880 | tf_op jit(solution)/shard_map/while/body/eval_jaxpr/kgrt,rkgd->tkd/dot_general | solution.py:116
  1041.1 67.3 %fusion.22 = f32[8,128,2,320]{1,3,2,0:T(8,128)S(1)} fusion(f32[8,2560,320,2]{1,2,3,0:T(8,128)} %fusion.35, f32[8,2,320,2560]{3,2,1,0:T(8,128)} %get-tuple-element.212, f32[8,2,320]{2,1,0:T(2,128)S(1)} %bitcast.440, bf16[2560,8,128]{2,0,1:T(8,128)(2,1)} %all-gather.32.cloned.1.call-done), kind=kOutput, calls=%fused_computation.34 | convolution fusion | flops 3447201280 | bytes 112742400 | tf_op jit(solution)/shard_map/while/body/eval_jaxpr/kgrt,tkd->rkgd/dot_general | solution.py:112
  1113.7 66.4 %fusion.25 = f32[8,128,2,320]{1,3,2,0:T(8,128)S(1)} fusion(f32[8,2560,320,2]{1,2,3,0:T(8,128)} %fusion.30, f32[8,2,320,2560]{3,2,1,0:T(8,128)} %get-tuple-element.210, f32[8,2,320]{2,1,0:T(2,128)S(1)} %bitcast.443, bf16[2560,8,128]{2,0,1:T(8,128)(2,1)} %all-gather.34.cloned.1.call-done), kind=kOutput, calls=%fused_computation.37 | convolution fusion | flops 3447201280 | bytes 112742400 | tf_op jit(solution)/shard_map/while/body/eval_jaxpr/kgrt,tkd->rkgd/dot_general | solution.py:112
  1242.1 24.8 %maximum_add_fusion.1 = f32[1024,6144]{1,0:T(8,128)} fusion(f32[1024,2048]{1,0:T(8,128)} %fusion.161, f32[1024,4096]{1,0:T(8,128)} %fusion.64, f32[1024,2048]{1,0:T(8,128)} %fusion.158, f32[1024,4096]{1,0:T(8,128)} %fusion.70), kind=kLoop, calls=%fused_computation.31 | loop fusion | flops 18874368 | bytes 75497472 | tf_op jit(solution)/shard_map/add | solution.py:291
  1313.2 35.5 %maximum_add_fusion = f32[1024,9216]{1,0:T(8,128)} fusion(f32[1024,3072]{1,0:T(8,128)S(1)} %convolution_bitcast_fusion.1, f32[1024,6144]{1,0:T(8,128)} %fusion.48, f32[1024,3072]{1,0:T(8,128)} %convolution_bitcast_fusion, f32[1024,6144]{1,0:T(8,128)} %fusion.52), kind=kLoop, calls=%fused_computation.24 | loop fusion | flops 28311552 | bytes 113246208 | tf_op jit(solution)/shard_map/add | solution.py:294
  1373.7 42.7 %all-reduce.8 = (f32[1024]{0:T(1024)S(1)}, f32[128]{0:T(128)S(1)}, f32[128]{0:T(128)S(1)}, f32[1024]{0:T(1024)S(1)}) all-reduce(f32[1024]{0:T(1024)S(1)} %add.252, f32[128]{0:T(128)S(1)} %add.254, f32[128]{0:T(128)S(1)} %add.255, f32[1024]{0:T(1024)S(1)} %add.256), channel_id=8, replica_groups=mesh['dp'=4,'ctx'=8] {'dp','ctx'}, use_global_device_ids=true, to_apply=%region_32.33.clone | all-reduce | flops 2304 | bytes 18432
  1423.2 89.6 %reduce-scatter.15.cloned.1.call-done = f32[32,6144]{1,0:T(8,128)} async-done(((f32[1024,6144]{1,0:T(8,128)}), f32[32,6144]{1,0:T(8,128)}) %reduce-scatter.15.cloned.1.call-update) | async-done | bytes 786448 | tf_op jit(solution)/shard_map/reduce_scatter | solution.py:295
  1516.3 351.9 %reduce-scatter.17.cloned.1.call-done = f32[32,9216]{1,0:T(8,128)} async-done(((f32[1024,9216]{1,0:T(8,128)}), f32[32,9216]{1,0:T(8,128)}) %reduce-scatter.17.cloned.1.call-update) | async-done | bytes 1179664 | tf_op jit(solution)/shard_map/reduce_scatter | solution.py:303
  (410 shorter events, 427.2 us)
Async XLA Ops:
  7.2 63.1 %all-gather.18.cloned.1.call-start = ((), (), s32[]{:S(2)}) async-start(), calls=%async_computation.8 | async-start | bytes 2162688 | tf_op jit(solution)/shard_map/all_gather | solution.py:156
  7.9 120.7 %all-gather.14.cloned.1.call-start = ((), (), s32[]{:S(2)}) async-start(), calls=%async_computation.6 | async-start | bytes 2162688 | tf_op jit(solution)/shard_map/all_gather | solution.py:157
  8.7 184.0 %all-gather.20.cloned.1.call-start = ((), (), s32[]{:S(2)}) async-start(), calls=%async_computation.9 | async-start | bytes 4325376 | tf_op jit(solution)/shard_map/all_gather | solution.py:155
  9.4 239.9 %all-gather.34.cloned.1.call-start = ((), (), s32[]{:S(2)}) async-start(), calls=%async_computation.22 | async-start | bytes 5898240 | tf_op jit(solution)/shard_map/all_gather | solution.py:205
  55.1 148.2 %copy-start.71 = (f32[1024]{0:T(1024)}, f32[1024]{0:T(1024)S(1)}, u32[]{:S(2)}) copy-start(f32[1024]{0:T(1024)S(1)} %convert_element_type.363) | copy-start | bytes 12292
  57.1 151.9 %copy-start.46 = (f32[320,128]{1,0:T(8,128)}, f32[320,128]{1,0:T(8,128)S(1)}, u32[]{:S(2)}) copy-start(f32[320,128]{1,0:T(8,128)S(1)} %get-tuple-element.185) | copy-start | bytes 491524
  58.9 140.2 %copy-start.87 = (f32[320]{0:T(512)}, f32[320]{0:T(512)S(1)}, u32[]{:S(2)}) copy-start(f32[320]{0:T(512)S(1)} %get-tuple-element.221) | copy-start | bytes 3844
  58.9 144.4 %copy-start.85 = (f32[320]{0:T(512)}, f32[320]{0:T(512)S(1)}, u32[]{:S(2)}) copy-start(f32[320]{0:T(512)S(1)} %get-tuple-element.220) | copy-start | bytes 3844
  81.1 224.4 %all-gather.30.cloned.1.call-start = ((), (), s32[]{:S(2)}) async-start(), calls=%async_computation.14 | async-start | bytes 5898240 | tf_op jit(solution)/shard_map/all_gather | solution.py:208
  132.2 229.6 %all-gather.32.cloned.1.call-start = ((), (), s32[]{:S(2)}) async-start(), calls=%async_computation.21 | async-start | bytes 5898240 | tf_op jit(solution)/shard_map/all_gather | solution.py:205
  134.7 283.6 %all-gather.16.cloned.1.call-start = ((), (), s32[]{:S(2)}) async-start(), calls=%async_computation.7 | async-start | bytes 5898240 | tf_op jit(solution)/shard_map/all_gather | solution.py:208
  138.4 343.9 %all-gather.22.cloned.1.call-start = ((), (), s32[]{:S(2)}) async-start(), calls=%async_computation.10 | async-start | bytes 4325376 | tf_op jit(solution)/shard_map/all_gather | solution.py:160
  139.1 414.2 %all-gather.24.cloned.1.call-start = ((), (), s32[]{:S(2)}) async-start(), calls=%async_computation.11 | async-start | bytes 6488064 | tf_op jit(solution)/shard_map/all_gather | solution.py:166
  139.8 484.3 %all-gather.26.cloned.1.call-start = ((), (), s32[]{:S(2)}) async-start(), calls=%async_computation.12 | async-start | bytes 6488064 | tf_op jit(solution)/shard_map/all_gather | solution.py:167
  140.4 554.7 %all-gather.28.cloned.1.call-start = ((), (), s32[]{:S(2)}) async-start(), calls=%async_computation.13 | async-start | bytes 6488064 | tf_op jit(solution)/shard_map/all_gather | solution.py:168
  141.2 1066.1 %reduce-scatter.9.cloned.1.call-start = ((), (), s32[]{:S(2)}) async-start(), calls=%async_computation.16 | async-start | bytes 5898240 | tf_op jit(solution)/shard_map/reduce_scatter | solution.py:261
  486.7 252.0 %copy-start.30 = (f32[320,1024]{1,0:T(8,128)}, f32[320,1024]{1,0:T(8,128)S(1)}, u32[]{:S(2)}) copy-start(f32[320,1024]{1,0:T(8,128)S(1)} %get-tuple-element.214) | copy-start | bytes 3932164
  560.2 134.9 %copy-start.38 = (bf16[2,320,1024]{2,1,0:T(8,128)(2,1)S(1)}, bf16[2,320,1024]{2,1,0:T(8,128)(2,1)}, u32[]{:S(2)}) copy-start(bf16[2,320,1024]{2,1,0:T(8,128)(2,1)} %param.17) | copy-start | bytes 3932164
  739.4 152.7 %copy-start.24 = (f32[320,1024]{1,0:T(8,128)}, f32[320,1024]{1,0:T(8,128)S(1)}, u32[]{:S(2)}) copy-start(f32[320,1024]{1,0:T(8,128)S(1)} %get-tuple-element.166) | copy-start | bytes 3932164
  778.1 431.2 %reduce-scatter.7.cloned.1.call-start = ((), (), s32[]{:S(2)}) async-start(), calls=%async_computation.15 | async-start | bytes 5898240 | tf_op jit(solution)/shard_map/reduce_scatter | solution.py:258
  892.0 321.8 %reduce-scatter.11.cloned.1.call-start = ((), (), s32[]{:S(2)}) async-start(), calls=%async_computation.17 | async-start | bytes 5898240 | tf_op jit(solution)/shard_map/reduce_scatter | solution.py:258
  1010.5 210.6 %reduce-scatter.13.cloned.1.call-start = ((), (), s32[]{:S(2)}) async-start(), calls=%async_computation.18 | async-start | bytes 5898240 | tf_op jit(solution)/shard_map/reduce_scatter | solution.py:261
  1041.0 471.7 %reduce-scatter.15.cloned.1.call-start = ((), (), s32[]{:S(2)}) async-start(), calls=%async_computation.19 | async-start | bytes 25952256 | tf_op jit(solution)/shard_map/reduce_scatter | solution.py:295
  1267.0 601.3 %reduce-scatter.17.cloned.1.call-start = ((), (), s32[]{:S(2)}) async-start(), calls=%async_computation.20 | async-start | bytes 38928384 | tf_op jit(solution)/shard_map/reduce_scatter | solution.py:303
  (102 other events, 1156.6 us)
Sparse Core Ops, SparseCore 0:
  11.0 59.2 all-gather.17
  73.2 55.3 all-gather.13
  131.6 60.9 all-gather.19
  194.7 54.5 all-gather.33
  250.7 54.8 all-gather.29
  307.0 54.7 all-gather.31
  363.5 54.7 all-gather.15
  421.3 60.9 all-gather.21
  485.3 67.9 all-gather.23
  556.2 67.9 all-gather.25
  627.1 67.9 all-gather.27
  778.2 58.4 reduce-scatter.8
  892.1 58.6 reduce-scatter.6
  1010.6 59.1 reduce-scatter.10
  1071.9 58.2 reduce-scatter.12
  1267.1 245.6 reduce-scatter.14
  1520.2 347.9 reduce-scatter.16
where the time goes:
time: 1890 us; the launch traced here: 1880 us
  waiting for transfers between devices  883 us (47%)
  matrix products  676 us (36%)
  other arithmetic  142 us (8%)
  blocking collectives  84.9 us (4%)
  local copies, waits for them, and re-layouts  73.8 us (4%)
    reduce_scatter x1, waiting for transfers between devices, shards(): lax.psum_scatter((lambda first_row, row_count: feed_whole)(jnp.int32(0),...  352 us
    dot_general x2, matrix products, attend_backward(): jnp.einsum('kgrt,rkgd->tkd', grad_raw, queries, preferred_element_type=jn...  185 us
    dot_general x2, matrix products, attend_backward(): jnp.einsum('kgrt,tkd->rkgd', grad_raw, key_block, preferred_element_type=...  134 us
    dot_general x28, matrix products, matmul(): return jnp.dot(left_side, right_side, preferred_element_type=jnp.float32)  106 us
    reduce_scatter x1, waiting for transfers between devices, shards(): lax.psum_scatter((lambda first_row, row_count: attention_whole)(jnp.int32...  89.6 us
    unnamed x2, blocking collectives  84.9 us
    dot_general x8, matrix products, contract_rows(): lax.dot_general(left_side, right_side, (((0,), (0,)), ((), ())), preferre...  74.8 us
    all_gather x2, waiting for transfers between devices, shards(): lax.all_gather(key_low.reshape(TR, tree_rows, KV_HEADS, HEAD_DIM), 'ctx',...  72.4 us
  transfers between devices with their start and end apart: 17, of which 13 were waited for; matrix products, arithmetic and copies ran while one was open for 40% of the time, Pallas kernels for 0%

commit v1 on v0

v1 whole, which is shorter than its diff:
```python
import functools
import math

import jax
import jax.numpy as jnp
from jax import lax
from jax.experimental import pallas as pl
from jax.experimental.pallas import tpu as pltpu
from jax.sharding import PartitionSpec as P

D = 1024
HEADS = 16
KV_HEADS = 8
HEAD_DIM = 128
FF = 3072
TRUNK = 1024
SEG = 128
TREE = 2560
QD = HEADS * HEAD_DIM
KVD = KV_HEADS * HEAD_DIM
SUBS = 5
CHUNK = 256
GAIN_COLS = 128

eps_norm = 1e-06
rope_base = 1000000.0
exp2_scale = math.log2(math.e) / math.sqrt(HEAD_DIM)
score_scale = HEAD_DIM ** (-0.5)

MESH = pl.DeviceIdType.MESH
ANY = pl.BlockSpec(memory_space=pl.ANY)
AXES = ("dp", "ctx")


def matmul(left_side, right_side):
    return jnp.dot(left_side, right_side, preferred_element_type=jnp.float32)


def matmul_t(left_side, right_side):
    return lax.dot_general(
        left_side, right_side, (((1,), (1,)), ((), ())), preferred_element_type=jnp.float32
    )


def contract_rows(left_side, right_side):
    return lax.dot_general(
        left_side, right_side, (((0,), (0,)), ((), ())), preferred_element_type=jnp.float32
    )


def norm_forward(values, weight):
    factor = lax.rsqrt(jnp.mean(values * values, axis=-1, keepdims=True) + eps_norm)
    normed = values * factor
    return (normed * weight, normed, factor)


def norm_backward(grad_out, weight, normed, factor):
    weighted = grad_out * weight
    grad_in = factor * (weighted - normed * jnp.mean(weighted * normed, axis=-1, keepdims=True))
    return (grad_in, grad_out * normed)


def rotate(values, cosine, sine_table):
    middle = values.shape[-1] // 2
    turned = jnp.concatenate([-values[..., middle:], values[..., :middle]], axis=-1)
    return values * cosine + turned * sine_table


def rotate_back(gradient, cosine, sine_table):
    middle = gradient.shape[-1] // 2
    moved = gradient * sine_table
    return gradient * cosine + jnp.concatenate([moved[..., middle:], -moved[..., :middle]], axis=-1)


def rope_tables(positions):
    steps_half = jnp.arange(HEAD_DIM // 2, dtype=jnp.float32)
    inverse = rope_base ** (-(steps_half * 2.0 / HEAD_DIM))
    angles = positions.astype(jnp.float32)[:, None] * inverse[None, :]
    angles = jnp.concatenate([angles, angles], axis=-1)
    return (jnp.cos(angles)[:, None, :], jnp.sin(angles)[:, None, :])


def place(sizes):
    ny, nx, nz = sizes
    dp, ctx = lax.axis_index("dp"), lax.axis_index("ctx")
    me = (dp // nx, lax.rem(dp, nx), ctx // 2, lax.rem(ctx, 2))

    def device(y, x, z, core):
        return (y * nx + x, z * 2 + core)

    return me, device


def meet(partners):
    barrier = pltpu.get_barrier_semaphore()
    for partner in partners:
        pl.semaphore_signal(barrier, inc=1, device_id=partner, device_id_type=MESH)
    pl.semaphore_wait(barrier, len(partners))


def gather_kernel(sizes, orders, *refs):
    count = len(orders)
    shard = refs[:count]
    moved = refs[count : count + 2]
    whole = refs[count + 2 : 2 * count + 2]
    placed = refs[2 * count + 2 : 2 * count + 4]
    send_sem, recv_sem, local_sem = refs[2 * count + 4 :]
    ny, nx, nz = sizes
    (y, x, z, core), device = place(sizes)
    half = z // (nz // 2)
    used = [0]

    def others(axis):
        if axis == "z":
            return [(y, x, lax.rem(z + s, nz), core) for s in range(1, nz)]
        if axis == "x":
            return [(y, lax.rem(x + s, nx), z, core) for s in range(1, nx)]
        return [(lax.rem(y + s, ny), x, z, core) for s in range(1, ny)]

    def senders(axis):
        if axis == "z":
            return [(y, x, lax.rem(z + nz - s, nz), core) for s in range(1, nz)]
        if axis == "x":
            return [(y, lax.rem(x + nx - s, nx), z, core) for s in range(1, nx)]
        return [(lax.rem(y + ny - s, ny), x, z, core) for s in range(1, ny)]

    sibling = device(y, x, z, 1 - core)
    across = device(y, x, lax.rem(z + nz // 2, nz), core)
    meet([device(*o) for a in "zxy" for o in others(a)] + [sibling])

    def send(src, dst, target):
        k = used[0]
        used[0] += 1
        copy = pltpu.make_async_remote_copy(
            src_ref=src,
            dst_ref=dst,
            send_sem=send_sem.at[k],
            recv_sem=recv_sem.at[k],
            device_id=target,
            device_id_type=MESH,
        )
        copy.start()
        return copy

    pending = []
    locals_ = []
    for i in range(count):
        copy = pltpu.make_async_copy(shard[i], whole[i].at[y, x, z, core], local_sem.at[i])
        copy.start()
        locals_.append(copy)
    first = []
    for i in range(count):
        first.append(
            [send(shard[i], whole[i].at[y, x, z, core], device(*o)) for o in others("z")]
        )
        pending.append(send(shard[i], whole[i].at[y, x, z, core], sibling))
    for i in range(2):
        pending.append(send(moved[i].at[1 - half], placed[i].at[half], across))
        copy = pltpu.make_async_copy(
            moved[i].at[half], placed[i].at[half], local_sem.at[count + i]
        )
        copy.start()
        locals_.append(copy)

    def slab(i, stage, py, px, pz):
        order = orders[i]
        if stage == 0:
            return whole[i].at[py, px, pz, core]
        if stage == 1:
            return whole[i].at[py, px, :, core]
        if order[1] == "x":
            return whole[i].at[py, :, :, core]
        return whole[i].at[:, px, :, core]

    second = []
    for i in range(count):
        locals_[i].wait()
        for copy in first[i]:
            copy.wait()
        a = orders[i][1]
        second.append([send(slab(i, 1, y, x, z), slab(i, 1, y, x, z), device(*o)) for o in others(a)])
        for o in senders("z"):
            pending.append(send(slab(i, 0, *o[:3]), slab(i, 0, *o[:3]), sibling))
    third = []
    for i in range(count):
        for copy in second[i]:
            copy.wait()
        a, b = orders[i][1], orders[i][2]
        third.append([send(slab(i, 2, y, x, z), slab(i, 2, y, x, z), device(*o)) for o in others(b)])
        for o in senders(a):
            pending.append(send(slab(i, 1, *o[:3]), slab(i, 1, *o[:3]), sibling))
    for i in range(count):
        for copy in third[i]:
            copy.wait()
        b = orders[i][2]
        for o in senders(b):
            pending.append(send(slab(i, 2, *o[:3]), slab(i, 2, *o[:3]), sibling))
    for copy in pending:
        copy.wait()
    for copy in locals_[count:]:
        copy.wait()


def gather_weights(sizes, orders, shards_, moved, collective_id):
    ny, nx, nz = sizes
    count = len(orders)
    rounds = count * (2 * (nz - 1) + 2 * (nx - 1) + 2 * (ny - 1) + 1) + 2
    results = pl.pallas_call(
        functools.partial(gather_kernel, sizes, orders),
        out_shape=[
            jax.ShapeDtypeStruct((ny, nx, nz, 2) + s.shape, s.dtype) for s in shards_
        ]
        + [jax.ShapeDtypeStruct(s.shape, s.dtype) for s in moved],
        in_specs=[ANY] * (count + 2),
        out_specs=[ANY] * (count + 2),
        scratch_shapes=[
            pltpu.SemaphoreType.DMA((rounds,)),
            pltpu.SemaphoreType.DMA((rounds,)),
            pltpu.SemaphoreType.DMA((count + 2,)),
        ],
        compiler_params=pltpu.CompilerParams(
            collective_id=collective_id, has_side_effects=True
        ),
        name="gather_weights",
    )(*shards_, *moved)
    wholes = [r.reshape(-1, r.shape[-1]) for r in results[:count]]
    return wholes, results[count:]


def group_gather_kernel(sizes, key_ref, value_ref, keys_ref, values_ref, send_sem, recv_sem, local_sem):
    ny, nx, nz = sizes
    chips = nz // 2
    (y, x, z, core), device = place(sizes)
    base = (z // chips) * chips
    here = z - base
    sibling = device(y, x, z, 1 - core)

    def other(s):
        return device(y, x, base + lax.rem(here + s, chips), core)

    meet([other(s) for s in range(1, chips)] + [sibling])
    used = [0]

    def send(src, dst, target):
        k = used[0]
        used[0] += 1
        copy = pltpu.make_async_remote_copy(
            src_ref=src,
            dst_ref=dst,
            send_sem=send_sem.at[k],
            recv_sem=recv_sem.at[k],
            device_id=target,
            device_id_type=MESH,
        )
        copy.start()
        return copy

    mine = here * 2 + core
    pairs = ((key_ref, keys_ref), (value_ref, values_ref))
    first, pending, locals_ = [], [], []
    for src, dst in pairs:
        for s in range(1, chips):
            for half in range(2):
                first.append((s, half, dst, send(src.at[half], dst.at[half, mine], other(s))))
    for i, (src, dst) in enumerate(pairs):
        for half in range(2):
            pending.append(send(src.at[half], dst.at[half, mine], sibling))
            copy = pltpu.make_async_copy(
                src.at[half], dst.at[half, mine], local_sem.at[2 * i + half]
            )
            copy.start()
            locals_.append(copy)
    for s, half, dst, copy in first:
        copy.wait()
        came = lax.rem(here + chips - s, chips) * 2 + core
        pending.append(send(dst.at[half, came], dst.at[half, came], sibling))
    for copy in pending + locals_:
        copy.wait()


def group_gather(sizes, key, value, collective_id):
    chips = sizes[2] // 2
    rounds = 4 * (chips - 1) * 2 + 4
    shape = jax.ShapeDtypeStruct((2, 2 * chips) + key.shape[1:], key.dtype)
    return pl.pallas_call(
        functools.partial(group_gather_kernel, sizes),
        out_shape=[shape, shape],
        in_specs=[ANY] * 2,
        out_specs=[ANY] * 2,
        scratch_shapes=[
            pltpu.SemaphoreType.DMA((rounds,)),
            pltpu.SemaphoreType.DMA((rounds,)),
            pltpu.SemaphoreType.DMA((4,)),
        ],
        compiler_params=pltpu.CompilerParams(
            collective_id=collective_id, has_side_effects=True
        ),
        name="group_gather",
    )(key, value)


def group_scatter(parts, here, core, chips):
    _, _, rows, width = parts.shape
    pieces = parts.reshape(2, chips, 2, rows, width)
    size = 2 * chips
    swap = [(i, i ^ 1) for i in range(2 * size)]
    give = lax.dynamic_index_in_dim(pieces, 1 - core, 2, keepdims=False)
    keep = lax.dynamic_index_in_dim(pieces, core, 2, keepdims=False)
    got = lax.ppermute(give, "ctx", swap)
    both = (keep.astype(jnp.float32) + got.astype(jnp.float32)).astype(jnp.bfloat16)
    total = lax.dynamic_index_in_dim(both, here, 1, keepdims=False).astype(jnp.float32)
    for s in range(1, chips):
        hop = [
            (i, (i // size) * size + ((i % size) // 2 + s) % chips * 2 + i % 2)
            for i in range(2 * size)
        ]
        sent = lax.dynamic_index_in_dim(both, (here + s) % chips, 1, keepdims=False)
        total = total + lax.ppermute(sent, "ctx", hop).astype(jnp.float32)
    return total.reshape(2 * rows, width)


def nt(left_side, right_side):
    return lax.dot_general(
        left_side, right_side, (((1,), (1,)), ((), ())), preferred_element_type=jnp.float32
    )


def stacked(ref, piece, rows, sub):
    return jnp.concatenate(
        [
            ref[piece * rows + sub * s : piece * rows + sub * (s + 1), h * HEAD_DIM : (h + 1) * HEAD_DIM]
            for s in range(SUBS)
            for h in range(2)
        ],
        axis=0,
    )


def unstacked(ref, value, piece, rows, sub):
    for s in range(SUBS):
        for h in range(2):
            start = (2 * s + h) * sub
            ref[piece * rows + sub * s : piece * rows + sub * (s + 1), h * HEAD_DIM : (h + 1) * HEAD_DIM] = (
                value[start : start + sub].astype(ref.dtype)
            )


def attend_forward_kernel(rows, meta, q_ref, k_ref, v_ref, o_ref, l_ref, qs, acc, part):
    sub = rows // SUBS
    head = pl.program_id(0)

    @pl.when(head == 0)
    def _():
        l_ref[...] = jnp.zeros_like(l_ref)

    for piece in range(2):
        qs[...] = stacked(q_ref, piece, rows, sub)
        acc[...] = jnp.zeros_like(acc)
        part[...] = jnp.zeros_like(part)
        base = meta[piece]

        def trunk(step, carry):
            start = pl.multiple_of(step * CHUNK, CHUNK)
            scores = nt(qs[...], k_ref[pl.ds(start, CHUNK), :])
            weights = jnp.exp2(scores * exp2_scale)
            if piece == 0:
                at = lax.broadcasted_iota(jnp.int32, weights.shape, 0)
                at = base + (at // (2 * sub)) * sub + at % sub
                key_at = start + lax.broadcasted_iota(jnp.int32, weights.shape, 1)
                weights = jnp.where(key_at <= at, weights, 0.0)
            part[...] += weights[:, :HEAD_DIM] + weights[:, HEAD_DIM:]
            acc[...] += jnp.dot(
                weights.astype(jnp.bfloat16),
                v_ref[pl.ds(start, CHUNK), :],
                preferred_element_type=jnp.float32,
            )
            return carry

        lax.fori_loop(0, meta[32 + piece], trunk, 0)
        for s in range(SUBS):
            index = piece * SUBS + s
            block = slice(2 * sub * s, 2 * sub * (s + 1))

            def add(start, masked):
                start = pl.multiple_of(start, SEG)
                scores = nt(qs[block], k_ref[pl.ds(start, SEG), :])
                weights = jnp.exp2(scores * exp2_scale)
                if masked:
                    at = lax.broadcasted_iota(jnp.int32, weights.shape, 0)
                    at = lax.rem(base + s * sub, SEG) + at % sub
                    key_at = lax.broadcasted_iota(jnp.int32, weights.shape, 1)
                    weights = jnp.where(key_at <= at, weights, 0.0)
                part[block] += weights
                acc[block] += jnp.dot(
                    weights.astype(jnp.bfloat16),
                    v_ref[pl.ds(start, SEG), :],
                    preferred_element_type=jnp.float32,
                )

            @pl.when(meta[22 + index] > 0)
            def _():
                add(meta[2 + index], True)

            @pl.when(meta[22 + index] > 1)
            def _():
                add(meta[12 + index], False)

        total = jnp.sum(part[...], axis=-1, keepdims=True)
        unstacked(o_ref, acc[...] / total, piece, rows, sub)
        lanes = lax.broadcasted_iota(jnp.int32, (2 * rows, HEAD_DIM), 1)
        region = slice(piece * 2 * rows, (piece + 1) * 2 * rows)
        l_ref[region] = jnp.where(lanes == head, total, l_ref[region])


def attend_forward(meta, queries, keys, values):
    rows = queries.shape[0] // 2
    tree = keys.shape[0]
    return pl.pallas_call(
        functools.partial(attend_forward_kernel, rows),
        out_shape=[
            jax.ShapeDtypeStruct((2 * rows, QD), jnp.bfloat16),
            jax.ShapeDtypeStruct((4 * rows, HEAD_DIM), jnp.float32),
        ],
        grid_spec=pltpu.PrefetchScalarGridSpec(
            num_scalar_prefetch=1,
            grid=(KV_HEADS,),
            in_specs=[
                pl.BlockSpec((2 * rows, 2 * HEAD_DIM), lambda h, meta: (0, h)),
                pl.BlockSpec((tree, HEAD_DIM), lambda h, meta: (0, h)),
                pl.BlockSpec((tree, HEAD_DIM), lambda h, meta: (0, h)),
            ],
            out_specs=[
                pl.BlockSpec((2 * rows, 2 * HEAD_DIM), lambda h, meta: (0, h)),
                pl.BlockSpec((4 * rows, HEAD_DIM), lambda h, meta: (0, 0)),
            ],
            scratch_shapes=[
                pltpu.VMEM((2 * rows, HEAD_DIM), jnp.bfloat16),
                pltpu.VMEM((2 * rows, HEAD_DIM), jnp.float32),
                pltpu.VMEM((2 * rows, HEAD_DIM), jnp.float32),
            ],
        ),
        compiler_params=pltpu.CompilerParams(
            dimension_semantics=("arbitrary",), vmem_limit_bytes=48 * 1024 * 1024
        ),
        cost_estimate=pl.CostEstimate(
            flops=4 * 2 * rows * 1200 * QD, bytes_accessed=20_000_000, transcendentals=0
        ),
        name="attend_forward",
    )(meta, queries, keys, values)


def attend_backward_kernel(
    rows, meta, q_ref, g_ref, k_ref, v_ref, lse_ref, del_ref, lses_ref, dels_ref, dq_ref, dk_ref, dv_ref, qs, gs, dq, dk, dv
):
    sub = rows // SUBS
    dk[...] = jnp.zeros_like(dk)
    dv[...] = jnp.zeros_like(dv)
    for piece in range(2):
        qs[...] = stacked(q_ref, piece, rows, sub)
        gs[...] = stacked(g_ref, piece, rows, sub)
        dq[...] = jnp.zeros_like(dq)
        base = meta[piece]

        def add(start, width, block, lse, delta, mask):
            key = k_ref[pl.ds(start, width), :]
            scores = nt(key, qs[block])
            weights = jnp.exp2(scores * exp2_scale - lse)
            if mask is not None:
                weights = jnp.where(mask, weights, 0.0)
            grads = nt(v_ref[pl.ds(start, width), :], gs[block])
            grads = (weights * (grads - delta)).astype(jnp.bfloat16)
            dv[pl.ds(start, width), :] += jnp.dot(
                weights.astype(jnp.bfloat16), gs[block], preferred_element_type=jnp.float32
            )
            dk[pl.ds(start, width), :] += jnp.dot(
                grads, qs[block], preferred_element_type=jnp.float32
            )
            dq[block] += lax.dot_general(
                grads, key, (((0,), (0,)), ((), ())), preferred_element_type=jnp.float32
            )

        def trunk(step, carry):
            start = pl.multiple_of(step * CHUNK, CHUNK)
            mask = None
            if piece == 0:
                shape = (CHUNK, 2 * rows)
                at = lax.broadcasted_iota(jnp.int32, shape, 1)
                at = base + (at // (2 * sub)) * sub + at % sub
                mask = start + lax.broadcasted_iota(jnp.int32, shape, 0) <= at
            add(start, CHUNK, slice(0, 2 * rows), lse_ref[0, piece], del_ref[0, piece], mask)
            return carry

        lax.fori_loop(0, meta[32 + piece], trunk, 0)
        for s in range(SUBS):
            index = piece * SUBS + s
            block = slice(2 * sub * s, 2 * sub * (s + 1))

            @pl.when(meta[22 + index] > 0)
            def _():
                shape = (SEG, 2 * sub)
                at = lax.rem(base + s * sub, SEG) + lax.broadcasted_iota(jnp.int32, shape, 1) % sub
                mask = lax.broadcasted_iota(jnp.int32, shape, 0) <= at
                start = pl.multiple_of(meta[2 + index], SEG)
                add(start, SEG, block, lses_ref[0, index], dels_ref[0, index], mask)

            @pl.when(meta[22 + index] > 1)
            def _():
                start = pl.multiple_of(meta[12 + index], SEG)
                add(start, SEG, block, lses_ref[0, index], dels_ref[0, index], None)

        unstacked(dq_ref, dq[...] * score_scale, piece, rows, sub)
    dk_ref[...] = (dk[...] * score_scale).astype(dk_ref.dtype)
    dv_ref[...] = dv[...].astype(dv_ref.dtype)


def attend_backward(meta, queries, grads, keys, values, log_total, delta):
    rows = queries.shape[0] // 2
    tree = keys.shape[0]
    sub = rows // SUBS
    wide = pl.BlockSpec((2 * rows, 2 * HEAD_DIM), lambda h, meta: (0, h))
    tall = pl.BlockSpec((tree, HEAD_DIM), lambda h, meta: (0, h))
    line = pl.BlockSpec((1, 2, 1, 2 * rows), lambda h, meta: (h, 0, 0, 0))
    lines = pl.BlockSpec((1, 2 * SUBS, 1, 2 * sub), lambda h, meta: (h, 0, 0, 0))
    return pl.pallas_call(
        functools.partial(attend_backward_kernel, rows),
        out_shape=[
            jax.ShapeDtypeStruct((2 * rows, QD), jnp.float32),
            jax.ShapeDtypeStruct((tree, KVD), jnp.bfloat16),
            jax.ShapeDtypeStruct((tree, KVD), jnp.bfloat16),
        ],
        grid_spec=pltpu.PrefetchScalarGridSpec(
            num_scalar_prefetch=1,
            grid=(KV_HEADS,),
            in_specs=[wide, wide, tall, tall, line, line, lines, lines],
            out_specs=[wide, tall, tall],
            scratch_shapes=[
                pltpu.VMEM((2 * rows, HEAD_DIM), jnp.bfloat16),
                pltpu.VMEM((2 * rows, HEAD_DIM), jnp.bfloat16),
                pltpu.VMEM((2 * rows, HEAD_DIM), jnp.float32),
                pltpu.VMEM((tree, HEAD_DIM), jnp.float32),
                pltpu.VMEM((tree, HEAD_DIM), jnp.float32),
            ],
        ),
        compiler_params=pltpu.CompilerParams(
            dimension_semantics=("arbitrary",), vmem_limit_bytes=48 * 1024 * 1024
        ),
        cost_estimate=pl.CostEstimate(
            flops=10 * 2 * rows * 1200 * QD, bytes_accessed=40_000_000, transcendentals=0
        ),
        name="attend_backward",
    )(
        meta,
        queries,
        grads,
        keys,
        values,
        log_total.reshape(KV_HEADS, 2, 1, 2 * rows),
        delta.reshape(KV_HEADS, 2, 1, 2 * rows),
        log_total.reshape(KV_HEADS, 2 * SUBS, 1, 2 * sub),
        delta.reshape(KV_HEADS, 2 * SUBS, 1, 2 * sub),
    )


def attention_meta(seg_tree, parent_tree, rows, group_size, member):
    sub = rows // SUBS
    run_seg = seg_tree[TRUNK::SEG]
    run_parent = parent_tree[run_seg]
    parent_run = jnp.argmax(run_seg[None, :] == run_parent[:, None], axis=1).astype(jnp.int32)
    bases = jnp.stack([rows * member, rows * (group_size + member)]).astype(jnp.int32)
    starts = (bases[:, None] + sub * jnp.arange(SUBS, dtype=jnp.int32)[None, :]).reshape(-1)
    tail = starts >= TRUNK
    run = jnp.maximum(starts - TRUNK, 0) // SEG
    own = TRUNK + SEG * run
    parent = TRUNK + SEG * parent_run[run]
    kind = jnp.where(tail, jnp.where(run_parent[run] > 0, 2, 1), 0)
    chunks = jnp.minimum((bases + rows + CHUNK - 1) // CHUNK, TRUNK // CHUNK)
    return jnp.concatenate([bases, own, parent, kind, chunks]).astype(jnp.int32)


def shards(
    sizes,
    tokens,
    cotangent,
    segment_ids,
    positions,
    parents,
    input_norm,
    query_proj,
    key_proj,
    value_proj,
    query_norm,
    key_norm,
    out_proj,
    post_norm,
    gate_proj,
    up_proj,
    down_proj,
):
    nz = sizes[2]
    rows = tokens.shape[1]
    shard_rows = query_proj.shape[0]
    gain_rows = query_norm.shape[0]
    group_size = nz
    ctx = lax.axis_index("ctx")
    half = ctx // group_size
    member = ctx % group_size
    here, core = member // 2, member % 2
    count_rows = 2 * rows

    def column(gain):
        return jnp.pad(gain, (0, shard_rows - gain.shape[0]))[:, None]

    gains = jnp.concatenate(
        [column(input_norm), column(post_norm), column(query_norm), column(key_norm)], axis=1
    )
    gains = jnp.pad(gains, ((0, 0), (0, GAIN_COLS - 4)))
    key_value = jnp.concatenate([key_proj, value_proj, gains], axis=1)
    feed_shard = jnp.concatenate([out_proj.T, gate_proj, up_proj, down_proj.T], axis=1)

    (query_full, key_value_full), (inputs_low, grad_out) = gather_weights(
        sizes, ("zxy", "zyx"), [query_proj, key_value], [tokens, cotangent], 1
    )
    feed_full = lax.all_gather(feed_shard, AXES, axis=0, tiled=True)

    gain_block = key_value_full[:, 2 * KVD :].astype(jnp.float32)
    in_weight = gain_block[:, 0]
    post_weight = gain_block[:, 1]
    by_device = gain_block.reshape(-1, shard_rows, GAIN_COLS)
    query_weight = by_device[:, :gain_rows, 2].reshape(HEAD_DIM)
    key_weight = by_device[:, :gain_rows, 3].reshape(HEAD_DIM)

    seg_tree = segment_ids[half]
    pos_tree = positions[half].reshape(2, group_size, rows)
    pos_local = lax.dynamic_index_in_dim(pos_tree, member, 1, keepdims=False).reshape(count_rows)
    meta = attention_meta(seg_tree, parents[half], rows, group_size, member)
    cosine_table, sine_table = rope_tables(pos_local)

    inputs = inputs_low.reshape(count_rows, D).astype(jnp.float32)
    grad_out = grad_out.reshape(count_rows, D)

    normed_in, in_hat, in_factor = norm_forward(inputs, in_weight)
    normed_low = normed_in.astype(jnp.bfloat16)
    query_pre = matmul(normed_low, query_full).reshape(count_rows, HEADS, HEAD_DIM)
    key_pre = matmul(normed_low, key_value_full[:, :KVD]).reshape(count_rows, KV_HEADS, HEAD_DIM)
    value_low = matmul(normed_low, key_value_full[:, KVD : 2 * KVD]).astype(jnp.bfloat16)
    query_normed, query_hat, query_factor = norm_forward(query_pre, query_weight)
    key_normed, key_hat, key_factor = norm_forward(key_pre, key_weight)
    query_low = rotate(query_normed, cosine_table, sine_table).astype(jnp.bfloat16)
    key_low = rotate(key_normed, cosine_table, sine_table).astype(jnp.bfloat16)
    query_low = query_low.reshape(count_rows, QD)
    tree_keys, tree_values = group_gather(
        sizes, key_low.reshape(2, rows, KVD), value_low.reshape(2, rows, KVD), 2
    )
    tree_keys = tree_keys.reshape(TREE, KVD)
    tree_values = tree_values.reshape(TREE, KVD)
    mixed_low, totals = attend_forward(meta, query_low, tree_keys, tree_values)
    log_total = jnp.log2(totals[:, :KV_HEADS]).T

    out_t = feed_full[:, :QD]
    gate_full = feed_full[:, QD : QD + FF]
    up_full = feed_full[:, QD + FF : QD + 2 * FF]
    down_t = feed_full[:, QD + 2 * FF :]
    hidden = inputs + matmul_t(mixed_low, out_t)
    normed_post, post_hat, post_factor = norm_forward(hidden, post_weight)
    second_low = normed_post.astype(jnp.bfloat16)
    gate_pre = matmul(second_low, gate_full)
    up_pre = matmul(second_low, up_full)
    activated = jax.nn.silu(gate_pre)
    inner_low = (activated * up_pre).astype(jnp.bfloat16)
    result = (hidden + matmul_t(inner_low, down_t)).astype(jnp.bfloat16)

    grad_inner = matmul(grad_out, down_t)
    sigmoid_gate = jax.nn.sigmoid(gate_pre)
    grad_gate = (
        grad_inner * up_pre * sigmoid_gate * (1.0 + gate_pre * (1.0 - sigmoid_gate))
    ).astype(jnp.bfloat16)
    grad_up = (grad_inner * activated).astype(jnp.bfloat16)
    grad_second = matmul_t(grad_gate, gate_full) + matmul_t(grad_up, up_full)
    feed_part = jnp.concatenate(
        [
            contract_rows(second_low, grad_gate),
            contract_rows(second_low, grad_up),
            contract_rows(grad_out, inner_low),
        ],
        axis=1,
    ).astype(jnp.bfloat16)
    feed_grad = lax.psum_scatter(feed_part, AXES, scatter_dimension=0, tiled=True)

    grad_post_in, post_part = norm_backward(grad_second, post_weight, post_hat, post_factor)
    grad_hidden = grad_out.astype(jnp.float32) + grad_post_in
    grad_branch = grad_hidden.astype(jnp.bfloat16)
    grad_mixed = matmul(grad_branch, out_t).astype(jnp.bfloat16)
    delta = jnp.sum(
        (grad_mixed.astype(jnp.float32) * mixed_low.astype(jnp.float32)).reshape(
            count_rows, HEADS, HEAD_DIM
        ),
        axis=-1,
    )
    delta = delta.reshape(2, SUBS, rows // SUBS, KV_HEADS, 2).transpose(3, 0, 1, 4, 2)
    grad_queries, grad_keys, grad_values = attend_backward(
        meta, query_low, grad_mixed, tree_keys, tree_values, log_total, delta
    )
    key_grad = group_scatter(grad_keys.reshape(2, group_size, rows, KVD), here, core, nz // 2)
    value_grad = group_scatter(grad_values.reshape(2, group_size, rows, KVD), here, core, nz // 2)

    grad_query_normed = rotate_back(
        grad_queries.reshape(count_rows, HEADS, HEAD_DIM), cosine_table, sine_table
    )
    grad_query_pre, query_part = norm_backward(
        grad_query_normed, query_weight, query_hat, query_factor
    )
    grad_key_normed = rotate_back(
        key_grad.reshape(count_rows, KV_HEADS, HEAD_DIM), cosine_table, sine_table
    )
    grad_key_pre, key_part = norm_backward(grad_key_normed, key_weight, key_hat, key_factor)
    grad_query_low = grad_query_pre.reshape(count_rows, QD).astype(jnp.bfloat16)
    grad_key_low = grad_key_pre.reshape(count_rows, KVD).astype(jnp.bfloat16)
    grad_value_low = value_grad.astype(jnp.bfloat16)
    grad_key_value = jnp.concatenate([grad_key_low, grad_value_low], axis=1)
    grad_normed = matmul_t(grad_query_low, query_full) + matmul_t(
        grad_key_value, key_value_full[:, : 2 * KVD]
    )
    grad_in_norm, in_part = norm_backward(grad_normed, in_weight, in_hat, in_factor)
    input_grad = grad_hidden + grad_in_norm

    def gain_column(values):
        if values.shape[0] == D:
            return values[:, None]
        spread = jnp.pad(values.reshape(-1, gain_rows), ((0, 0), (0, shard_rows - gain_rows)))
        return spread.reshape(D, 1)

    gain_grads = jnp.concatenate(
        [
            gain_column(jnp.sum(in_part, axis=0)),
            gain_column(jnp.sum(post_part, axis=0)),
            gain_column(jnp.sum(query_part, axis=(0, 1))),
            gain_column(jnp.sum(key_part, axis=(0, 1))),
        ],
        axis=1,
    )
    gain_grads = jnp.pad(gain_grads, ((0, 0), (0, GAIN_COLS - 4)))
    attention_part = jnp.concatenate(
        [
            contract_rows(normed_low, grad_query_low),
            contract_rows(normed_low, grad_key_value),
            contract_rows(grad_branch, mixed_low),
            gain_grads,
        ],
        axis=1,
    ).astype(jnp.bfloat16)
    attention_grad = lax.psum_scatter(attention_part, AXES, scatter_dimension=0, tiled=True)

    swap = [(i, (i + group_size) % (2 * group_size)) for i in range(2 * group_size)]

    def send_back(values):
        pieces = values.reshape(2, rows, D)
        keep = pieces[half]
        got = lax.ppermute(pieces[1 - half].astype(jnp.bfloat16), "ctx", swap)
        got = got.astype(values.dtype)
        return jnp.where(half == 0, jnp.stack([keep, got]), jnp.stack([got, keep]))

    attention_grad = attention_grad.astype(jnp.float32)
    feed_grad = feed_grad.astype(jnp.float32)
    gain_grad = attention_grad[:, QD + 2 * KVD + QD :]
    return (
        send_back(result),
        send_back(input_grad),
        gain_grad[:, 0],
        attention_grad[:, :QD],
        attention_grad[:, QD : QD + KVD],
        attention_grad[:, QD + KVD : QD + 2 * KVD],
        gain_grad[:gain_rows, 2],
        gain_grad[:gain_rows, 3],
        attention_grad[:, QD + 2 * KVD : QD + 2 * KVD + QD].T,
        gain_grad[:, 1],
        feed_grad[:, :FF],
        feed_grad[:, FF : 2 * FF],
        feed_grad[:, 2 * FF :].T,
    )


def solution(mesh):
    dp, ctx = mesh.shape["dp"], mesh.shape["ctx"]
    sizes = (2, dp // 2, ctx // 2)
    return jax.shard_map(
        functools.partial(shards, sizes),
        mesh=mesh,
        in_specs=(
            P("dp", "ctx", None),
            P("dp", "ctx", None),
            P("dp", None),
            P("dp", None),
            P("dp", None),
            P(("dp", "ctx")),
            P(("dp", "ctx"), None),
            P(("dp", "ctx"), None),
            P(("dp", "ctx"), None),
            P(("dp", "ctx")),
            P(("dp", "ctx")),
            P(None, ("dp", "ctx")),
            P(("dp", "ctx")),
            P(("dp", "ctx"), None),
            P(("dp", "ctx"), None),
            P(None, ("dp", "ctx")),
        ),
        out_specs=(
            P("dp", "ctx", None),
            P("dp", "ctx", None),
            P(("dp", "ctx")),
            P(("dp", "ctx"), None),
            P(("dp", "ctx"), None),
            P(("dp", "ctx"), None),
            P(("dp", "ctx")),
            P(("dp", "ctx")),
            P(None, ("dp", "ctx")),
            P(("dp", "ctx")),
            P(("dp", "ctx"), None),
            P(("dp", "ctx"), None),
            P(None, ("dp", "ctx")),
        ),
        check_vma=False,
    )
```

time: 1890 us -> 939 us (0.50)
  waiting for transfers between devices: 883 us -> 242 us
  matrix products: 676 us -> 126 us
  Pallas kernels: 0 us -> 322 us
  blocking collectives: 84.9 us -> 0 us
  other arithmetic: 142 us -> 78.5 us
  starting transfers between devices: 0.89 us -> 52.2 us
  local copies, waits for them, and re-layouts: 73.8 us -> 92.8 us
    dot_general x14 -> x6, matrix products: 495 us -> 43.6 us  [matmul_t(): lax.dot_general(left_side, right_side, (((1,), (1,)), ((), ())), preferre...]
    all_gather x11 -> x1, waiting for transfers between devices: 437 us -> 0.02 us  [shards(): feed_full = lax.all_gather(feed_shard, AXES, axis=0, tiled=True)]
    reduce_scatter x6 -> x2, waiting for transfers between devices: 442 us -> 99.9 us  [the longest x1 99.9 us: shards(): lax.psum_scatter(attention_part, AXES, scatter_dimension=0, tiled=True)]
    pallas_call x0 -> x4, Pallas kernels: none -> 322 us  [the longest x1 133 us: gather_weights(): pl.pallas_call(functools.partial(gather_kernel, sizes, orders), out_shape...]
    ppermute x0 -> x6, waiting for transfers between devices: none -> 142 us  [the longest x2 87.5 us: send_back(): got = lax.ppermute(pieces[1 - half].astype(jnp.bfloat16), 'ctx', swap)]
    unnamed x2 -> x0, blocking collectives: 84.9 us -> none
    add x10 -> x4, other arithmetic: 64 us -> 2.57 us  [the longest x1 1.82 us: group_scatter(): total = total + lax.ppermute(sent, 'ctx', hop).astype(jnp.float32)]
    dot_general x28 -> x7, matrix products: 106 us -> 49.9 us  [matmul(): return jnp.dot(left_side, right_side, preferred_element_type=jnp.float32)]
  transfers between devices with their start and end apart: 17 -> 9, of which waited for: 13 -> 5; matrix products, arithmetic and copies ran while one was open for 40% -> 21% of each run, Pallas kernels for 0% -> 35%
where the time goes in v1:
time: 939 us; the launch traced here: 929 us
  Pallas kernels  322 us (34%)
  waiting for transfers between devices  242 us (26%)
  matrix products  126 us (13%)
  local copies, waits for them, and re-layouts  92.8 us (10%)
  other arithmetic  78.5 us (8%)
  starting transfers between devices  52.2 us (6%)
  between operations  15.3 us (2%)
    pallas_call x1, Pallas kernels, gather_weights(): pl.pallas_call(functools.partial(gather_kernel, sizes, orders), out_shape...  133 us
    reduce_scatter x1, waiting for transfers between devices, shards(): lax.psum_scatter(attention_part, AXES, scatter_dimension=0, tiled=True)  99.9 us
    ppermute x2, waiting for transfers between devices, send_back(): got = lax.ppermute(pieces[1 - half].astype(jnp.bfloat16), 'ctx', swap)  87.5 us
    pallas_call x1, Pallas kernels, group_gather(): pl.pallas_call(functools.partial(group_gather_kernel, sizes), out_shape=[...  81.3 us
    pallas_call x1, Pallas kernels, attend_backward(): pl.pallas_call(functools.partial(attend_backward_kernel, rows), out_shape...  61.4 us
    ppermute x2, waiting for transfers between devices, group_scatter(): total = total + lax.ppermute(sent, 'ctx', hop).astype(jnp.float32)  54.6 us
    dot_general x7, matrix products, matmul(): return jnp.dot(left_side, right_side, preferred_element_type=jnp.float32)  49.9 us
    pallas_call x1, Pallas kernels, attend_forward(): pl.pallas_call(functools.partial(attend_forward_kernel, rows), out_shape=...  46.9 us
  transfers between devices with their start and end apart: 9, of which 5 were waited for; matrix products, arithmetic and copies ran while one was open for 21% of the time, Pallas kernels for 35%

profile of v1, /device:TPU:0, one launch (start us, length us, event | category | flops | bytes accessed | tf_op | source)
XLA Modules:
  0.0 928.8 jit_solution(15002468126092286795)
XLA Ops:
  19.2 132.8 %gather_weights.1 = (bf16[2,2,4,2,32,2048]{5,4,3,2,1,0:T(8,128)(2,1)}, bf16[2,2,4,2,32,2176]{5,4,3,2,1,0:T(8,128)(2,1)}, bf16[2,320,1024]{2,1,0:T(8,128)(2,1)}, bf16[2,320,1024]{2,1,0:T(8,128)(2,1)}) custom-call(bf16[32,2048]{1,0:T(8,128)(2,1)} %refs_0_.1, bf16[32,2176]{1,0:T(8,128)(2,1)} %fusion.65.refs_1_, bf16[2,320,1024]{2,1,0:T(8,128)(2,1)} %refs_2_.1, ...), custom_call_target="tpu_custom_call" | custom-call | tf_op jit(solution)/shard_map/gather_weights/pallas_call | solution.py:208
  176.6 6.5 copy.86
  203.0 81.3 %group_gather.1 = (bf16[2,4,320,1024]{3,2,1,0:T(8,128)(2,1)}, bf16[2,4,320,1024]{3,2,1,0:T(8,128)(2,1)}) custom-call(bf16[2,320,1024]{2,1,0:T(8,128)(2,1)} %copy.104.key_ref, bf16[2,320,1024]{2,1,0:T(8,128)(2,1)} %bitcast.164), custom_call_target="tpu_custom_call" | custom-call | tf_op jit(solution)/shard_map/group_gather/pallas_call | solution.py:285
  286.3 46.9 %attend_forward.1 = (bf16[640,2048]{1,0:T(8,128)(2,1)S(1)}, f32[1280,128]{1,0:T(8,128)S(1)}) custom-call(s32[34]{0:T(128)S(1)} %concatenate.53.meta, bf16[640,2048]{1,0:T(8,128)(2,1)S(1)} %copy-done.4, bf16[2560,1024]{1,0:T(8,128)(2,1)} %bitcast.179, bf16[2560,1024]{1,0:T(8,128)(2,1)} %bitcast.181), custom_call_target="tpu_custom_call" | custom-call | flops 6291456000 | bytes 20000000 | tf_op jit(solution)/shard_map/attend_forward/pallas_call | solution.py:418
  333.2 5.6 multiply_reduce_fusion.7
  341.1 9.2 fusion.3
  350.3 9.2 fusion.9
  359.5 14.4 %multiply_convert_fusion.1 = (bf16[640,3072]{1,0:T(8,128)(2,1)S(1)}, bf16[640,3072]{1,0:T(8,128)(2,1)}, bf16[640,3072]{1,0:T(8,128)(2,1)S(1)}) fusion(f32[640,3072]{1,0:T(8,128)} %fusion.3, f32[640,3072]{1,0:T(8,128)} %fusion.9, bf16[640,1024]{1,0:T(8,128)(2,1)S(1)} %multiply_convert_fusion.5, bf16[1024,11264]{1,0:T(8,128)(2,1)} %all-gather.2.cloned.1.call-done), kind=kOutput, calls=%fused_computation.8 | convolution fusion | flops 4056023040 | bytes 35127296 | tf_op jit(solution)/shard_map/dot_general | solution.py:36
  390.2 16.7 %pad_maximum_fusion = bf16[1024,9216]{1,0:T(8,128)(2,1)} fusion(bf16[1024,3072]{1,0:T(8,128)(2,1)S(1)} %convolution_convert_fusion, bf16[1024,3072]{1,0:T(8,128)(2,1)S(1)} %convolution_convert_fusion.1, bf16[1024,3072]{1,0:T(8,128)(2,1)S(1)} %convolution_convert_fusion.2), kind=kLoop, calls=%fused_computation.5 | loop fusion | flops 56623104 | bytes 37748736 | tf_op jit(solution)/shard_map/concatenate | solution.py:679
  410.6 7.7 fusion.7
  418.4 6.9 multiply_reduce_fusion.4
  446.6 61.4 %attend_backward.1 = (f32[640,2048]{1,0:T(8,128)}, bf16[2560,1024]{1,0:T(8,128)(2,1)}, bf16[2560,1024]{1,0:T(8,128)(2,1)}) custom-call(s32[34]{0:T(128)S(1)} %concatenate.53.meta, bf16[640,2048]{1,0:T(8,128)(2,1)S(1)} %copy-done.5, bf16[640,2048]{1,0:T(8,128)(2,1)S(1)} %copy-done.3, bf16[2560,1024]{1,0:T(8,128)(2,1)} %bitcast.180, ...), custom_call_target="tpu_custom_call" | custom-call | flops 15728640000 | bytes 40000000 | tf_op jit(solution)/shard_map/attend_backward/pallas_call | solution.py:524
  508.0 6.0 copy.107
  519.3 19.2 %collective-permute-start.1 = (bf16[2,2,320,1024]{3,2,0,1:T(8,128)(2,1)}, bf16[2,2,320,1024]{3,2,0,1:T(8,128)(2,1)}, u32[]{:S(2)}, u32[]{:S(2)}) collective-permute-start(bf16[2,2,320,1024]{3,2,0,1:T(8,128)(2,1)} %bitcast.138), channel_id=1, source_target_pairs={{0,1},{1,0},{2,3},{3,2},{4,5},{5,4},{6,7},{7,6},{8,9},{9,8},{10,11... | collective-permute-start | bytes 7864328 | tf_op jit(solution)/shard_map/ppermute | solution.py:309
  556.8 29.2 %collective-permute-start.2 = (bf16[2,320,1024]{2,1,0:T(8,128)(2,1)}, bf16[2,320,1024]{2,1,0:T(8,128)(2,1)}, u32[]{:S(2)}, u32[]{:S(2)}) collective-permute-start(bf16[2,320,1024]{2,1,0:T(8,128)(2,1)} %dynamic-slice_bitcast_fusion.2), channel_id=1, source_target_pairs={{0,2},{1,3},{2,0},{3,1},{4,6},{5,7},{6,4},{7,5},{8,10},{9,11},{10,... | collective-permute-start | bytes 3932168 | tf_op jit(solution)/shard_map/ppermute | solution.py:318
  591.8 7.5 fusion.82
  605.0 27.3 %collective-permute-done.2 = bf16[2,320,1024]{2,1,0:T(8,128)(2,1)} collective-permute-done((bf16[2,320,1024]{2,1,0:T(8,128)(2,1)}, bf16[2,320,1024]{2,1,0:T(8,128)(2,1)}, u32[]{:S(2)}, u32[]{:S(2)}) %collective-permute-start.2) | collective-permute-done | bytes 1310752 | tf_op jit(solution)/shard_map/ppermute | solution.py:318
  645.7 27.3 %collective-permute-done.4 = bf16[2,320,1024]{2,1,0:T(8,128)(2,1)} collective-permute-done((bf16[2,320,1024]{2,1,0:T(8,128)(2,1)}, bf16[2,320,1024]{2,1,0:T(8,128)(2,1)}, u32[]{:S(2)}, u32[]{:S(2)}) %collective-permute-start.4) | collective-permute-done | bytes 1310752 | tf_op jit(solution)/shard_map/ppermute | solution.py:318
  682.3 7.5 fusion.40
  695.4 8.3 fusion.1
  705.5 8.4 add_convert_fusion
  719.5 62.2 %collective-permute-done = bf16[320,1024]{1,0:T(8,128)(2,1)} collective-permute-done((bf16[320,1024]{1,0:T(8,128)(2,1)}, bf16[320,1024]{1,0:T(8,128)(2,1)}, u32[]{:S(2)}, u32[]{:S(2)}) %collective-permute-start) | collective-permute-done | bytes 655392 | tf_op jit(solution)/shard_map/ppermute | solution.py:758
  784.5 25.2 %collective-permute-done.5 = bf16[320,1024]{1,0:T(8,128)(2,1)} collective-permute-done((bf16[320,1024]{1,0:T(8,128)(2,1)}, bf16[320,1024]{1,0:T(8,128)(2,1)}, u32[]{:S(2)}, u32[]{:S(2)}) %collective-permute-start.5) | collective-permute-done | bytes 655392 | tf_op jit(solution)/shard_map/ppermute | solution.py:758
  815.7 99.9 %reduce-scatter.3.cloned.1.call-done = bf16[32,6272]{1,0:T(8,128)(2,1)} async-done(((bf16[1024,6272]{1,0:T(8,128)(2,1)}), bf16[32,6272]{1,0:T(8,128)(2,1)}) %reduce-scatter.3.cloned.1.call-update) | async-done | bytes 401424 | tf_op jit(solution)/shard_map/reduce_scatter | solution.py:751
  (289 shorter events, 186.7 us)
Async XLA Ops:
  7.2 326.0 %all-gather.2.cloned.1.call-start = ((), (), s32[]{:S(2)}) async-start(), calls=%async_computation.2 | async-start | bytes 23789568 | tf_op jit(solution)/shard_map/all_gather | solution.py:623
  9.4 803.4 %reduce-scatter.5.cloned.1.call-start = ((), (), s32[]{:S(2)}) async-start(), calls=%async_computation.4 | async-start | bytes 19464192 | tf_op jit(solution)/shard_map/reduce_scatter | solution.py:687
  153.8 44.2 %copy-start.52 = (f32[640]{0:T(1024)}, f32[640]{0:T(1024)S(1)}, u32[]{:S(2)}) copy-start(f32[640]{0:T(1024)S(1)} %rsqrt.39) | copy-start | bytes 7684
  156.0 33.8 %copy-start.54 = (f32[128]{0:T(128)}, f32[128]{0:T(128)S(1)}, u32[]{:S(2)}) copy-start(f32[128]{0:T(128)S(1)} %mul.339) | copy-start | bytes 1540
  161.6 28.2 %copy-start.22 = (f32[640,128]{0,1:T(8,128)}, f32[640,128]{0,1:T(8,128)S(1)}, u32[]{:S(2)}) copy-start(f32[640,128]{0,1:T(8,128)S(1)} %get-tuple-element.76) | copy-start | bytes 983044
  161.6 28.2 %copy-start.24 = (f32[640,128]{0,1:T(8,128)}, f32[640,128]{0,1:T(8,128)S(1)}, u32[]{:S(2)}) copy-start(f32[640,128]{0,1:T(8,128)S(1)} %get-tuple-element.77) | copy-start | bytes 983044
  163.8 34.1 %copy-start.48 = (f32[1024]{0:T(1024)}, f32[1024]{0:T(1024)S(1)}, u32[]{:S(2)}) copy-start(f32[1024]{0:T(1024)S(1)} %get-tuple-element.50) | copy-start | bytes 12292
  203.0 81.4 %copy-start.60 = (s32[10]{0:T(128)S(1)}, s32[10]{0:T(128)}, u32[]{:S(2)}) copy-start(s32[10]{0:T(128)} %gather_fusion.1) | copy-start | bytes 124
  203.0 81.4 %copy-start.61 = (pred[10]{0:T(512)(128)(4,1)S(1)}, pred[10]{0:T(512)(128)(4,1)}, u32[]{:S(2)}) copy-start(pred[10]{0:T(512)(128)(4,1)} %reshape.402) | copy-start | bytes 34
  203.0 81.4 %copy-start.62 = (s32[10]{0:T(128)S(1)}, s32[10]{0:T(128)}, u32[]{:S(2)}) copy-start(s32[10]{0:T(128)} %div.79) | copy-start | bytes 124
  203.0 81.4 %copy-start.59 = (s32[10]{0:T(128)S(1)}, s32[10]{0:T(128)}, u32[]{:S(2)}) copy-start(s32[10]{0:T(128)} %gather_fusion.2) | copy-start | bytes 124
  203.0 81.4 %copy-start.63 = (pred[10]{0:T(512)(128)(4,1)S(1)}, pred[10]{0:T(512)(128)(4,1)}, u32[]{:S(2)}) copy-start(pred[10]{0:T(512)(128)(4,1)} %ge.7) | copy-start | bytes 34
  203.0 81.4 %copy-start.58 = (s32[2]{0:T(128)S(1)}, s32[2]{0:T(128)}, u32[]{:S(2)}) copy-start(s32[2]{0:T(128)} %get-tuple-element.55) | copy-start | bytes 28
  407.0 508.6 %reduce-scatter.3.cloned.1.call-start = ((), (), s32[]{:S(2)}) async-start(), calls=%async_computation.3 | async-start | bytes 13246464 | tf_op jit(solution)/shard_map/reduce_scatter | solution.py:751
  519.3 33.7 %collective-permute-start.1 = (bf16[2,2,320,1024]{3,2,0,1:T(8,128)(2,1)}, bf16[2,2,320,1024]{3,2,0,1:T(8,128)(2,1)}, u32[]{:S(2)}, u32[]{:S(2)}) collective-permute-start(bf16[2,2,320,1024]{3,2,0,1:T(8,128)(2,1)} %bitcast.138), channel_id=1, source_target_pairs={{0,1},{1,0},{2,3},{3,2},{4,5},{5,4},{6,7},{7,6},{8,9},{9,8},{10,11... | collective-permute-start | bytes 7864328 | tf_op jit(solution)/shard_map/ppermute | solution.py:309
  540.2 59.1 %collective-permute-start.3 = (bf16[2,2,320,1024]{3,2,1,0:T(8,128)(2,1)}, bf16[2,2,320,1024]{3,2,1,0:T(8,128)(2,1)}, u32[]{:S(2)}, u32[]{:S(2)}) collective-permute-start(bf16[2,2,320,1024]{3,2,1,0:T(8,128)(2,1)} %dynamic-slice_bitcast_fusion), channel_id=1, source_target_pairs={{0,1},{1,0},{2,3},{3,2},{4,5},{5,4},{6,7},{7,6},{8,9},{9,8},{10,11... | collective-permute-start | bytes 7864328 | tf_op jit(solution)/shard_map/ppermute | solution.py:309
  547.9 38.1 %copy-start.32 = (bf16[640,16,128]{0,2,1:T(8,128)(2,1)}, bf16[640,16,128]{0,2,1:T(8,128)(2,1)S(1)}, u32[]{:S(2)}) copy-start(bf16[640,16,128]{0,2,1:T(8,128)(2,1)S(1)} %multiply_convert_fusion.3) | copy-start | bytes 7864324
  555.6 30.4 %copy-start.42 = (bf16[2,320,1024]{2,1,0:T(8,128)(2,1)S(1)}, bf16[2,320,1024]{2,1,0:T(8,128)(2,1)}, u32[]{:S(2)}) copy-start(bf16[2,320,1024]{2,1,0:T(8,128)(2,1)} %copy-done.40) | copy-start | bytes 3932164
  556.8 75.5 %collective-permute-start.2 = (bf16[2,320,1024]{2,1,0:T(8,128)(2,1)}, bf16[2,320,1024]{2,1,0:T(8,128)(2,1)}, u32[]{:S(2)}, u32[]{:S(2)}) collective-permute-start(bf16[2,320,1024]{2,1,0:T(8,128)(2,1)} %dynamic-slice_bitcast_fusion.2), channel_id=1, source_target_pairs={{0,2},{1,3},{2,0},{3,1},{4,6},{5,7},{6,4},{7,5},{8,10},{9,11},{10,... | collective-permute-start | bytes 3932168 | tf_op jit(solution)/shard_map/ppermute | solution.py:318
  603.1 31.0 %copy-start.21 = (bf16[2,2,320,1024]{3,2,1,0:T(8,128)(2,1)}, bf16[2,2,320,1024]{3,2,1,0:T(8,128)(2,1)S(1)}, u32[]{:S(2)}) copy-start(bf16[2,2,320,1024]{3,2,1,0:T(8,128)(2,1)S(1)} %fusion.17) | copy-start | bytes 7864324
  604.4 68.7 %collective-permute-start.4 = (bf16[2,320,1024]{2,1,0:T(8,128)(2,1)}, bf16[2,320,1024]{2,1,0:T(8,128)(2,1)}, u32[]{:S(2)}, u32[]{:S(2)}) collective-permute-start(bf16[2,320,1024]{2,1,0:T(8,128)(2,1)} %dynamic-slice_bitcast_fusion.1), channel_id=1, source_target_pairs={{0,2},{1,3},{2,0},{3,1},{4,6},{5,7},{6,4},{7,5},{8,10},{9,11},{10,... | collective-permute-start | bytes 3932168 | tf_op jit(solution)/shard_map/ppermute | solution.py:318
  714.8 66.9 %collective-permute-start = (bf16[320,1024]{1,0:T(8,128)(2,1)}, bf16[320,1024]{1,0:T(8,128)(2,1)}, u32[]{:S(2)}, u32[]{:S(2)}) collective-permute-start(bf16[320,1024]{1,0:T(8,128)(2,1)} %get-tuple-element.71), channel_id=1, source_target_pairs={{0,4},{1,5},{2,6},{3,7},{4,0},{5,1},{6,2},{7,3},{8,12},{9,13},{10,... | collective-permute-start | bytes 1966088 | tf_op jit(solution)/shard_map/ppermute | solution.py:758
  718.9 90.8 %collective-permute-start.5 = (bf16[320,1024]{1,0:T(8,128)(2,1)}, bf16[320,1024]{1,0:T(8,128)(2,1)}, u32[]{:S(2)}, u32[]{:S(2)}) collective-permute-start(bf16[320,1024]{1,0:T(8,128)(2,1)} %fusion.59), channel_id=1, source_target_pairs={{0,4},{1,5},{2,6},{3,7},{4,0},{5,1},{6,2},{7,3},{8,12},{9,13},{10,... | collective-permute-start | bytes 1966088 | tf_op jit(solution)/shard_map/ppermute | solution.py:758
  812.8 109.2 %copy-start.1 = (s32[2,13]{1,0:T(2,128)S(1)}, s32[2,13]{1,0:T(2,128)}, u32[]{:S(2)}) copy-start(s32[2,13]{1,0:T(2,128)} %param.20) | copy-start | bytes 316
  (56 other events, 295.6 us)
Sparse Core Ops, SparseCore 0:
  10.9 233.6 all-gather.1
  407.1 259.3 reduce-scatter.4
  703.9 211.6 reduce-scatter.2

commit v2 on v0

v2 whole, which is shorter than its diff:
```python
import functools
import math

import jax
import jax.numpy as jnp
from jax import lax
from jax.experimental import pallas as pl
from jax.experimental.pallas import tpu as pltpu
from jax.sharding import PartitionSpec as P

D = 1024
HEADS = 16
KV_HEADS = 8
HEAD_DIM = 128
FF = 3072
TRUNK = 1024
SEG = 128
TREE = 2560
QD = HEADS * HEAD_DIM
KVD = KV_HEADS * HEAD_DIM
SUBS = 5
CHUNK = 256
GAIN_COLS = 128
LOCAL_RUNS = 3
MIB = 1024 * 1024

eps_norm = 1e-06
rope_base = 1000000.0
exp2_scale = math.log2(math.e) / math.sqrt(HEAD_DIM)
score_scale = HEAD_DIM ** (-0.5)

MESH = pl.DeviceIdType.MESH
ANY = pl.BlockSpec(memory_space=pl.ANY)
F32 = jnp.float32
BF16 = jnp.bfloat16


def matmul(left_side, right_side):
    return jnp.dot(left_side, right_side, preferred_element_type=F32)


def nt(left_side, right_side):
    return lax.dot_general(
        left_side, right_side, (((1,), (1,)), ((), ())), preferred_element_type=F32
    )


def contract_rows(left_side, right_side):
    return lax.dot_general(
        left_side, right_side, (((0,), (0,)), ((), ())), preferred_element_type=F32
    )


def norm_factor(values):
    return lax.rsqrt(jnp.mean(values * values, axis=-1, keepdims=True) + eps_norm)


def norm_backward(grad_out, weight, normed, factor):
    weighted = grad_out * weight
    grad_in = factor * (weighted - normed * jnp.mean(weighted * normed, axis=-1, keepdims=True))
    return (grad_in, grad_out * normed)


def rope_tables(positions):
    steps_half = jnp.arange(HEAD_DIM // 2, dtype=F32)
    inverse = rope_base ** (-(steps_half * 2.0 / HEAD_DIM))
    angles = positions.astype(F32)[:, None] * inverse[None, :]
    cosine, sine = jnp.cos(angles), jnp.sin(angles)
    return jnp.concatenate([cosine, cosine], axis=-1), jnp.concatenate([-sine, sine], axis=-1)


class Links:
    def __init__(self, sizes, send_sem, recv_sem):
        self.sizes = sizes
        self.send_sem = send_sem
        self.recv_sem = recv_sem
        self.index = {}

    def place(self):
        _, nx, _ = self.sizes
        dp, ctx = lax.axis_index("dp"), lax.axis_index("ctx")
        return dp // nx, lax.rem(dp, nx), ctx // 2, lax.rem(ctx, 2)

    def device(self, y, x, z, core):
        return (y * self.sizes[1] + x, z * 2 + core)

    def peers(self, axis, back=False):
        y, x, z, core = self.place()
        at = {"y": y, "x": x, "z": z}
        n = self.sizes["yxz".index(axis)]
        found = []
        for s in range(1, n):
            moved = dict(at)
            moved[axis] = lax.rem(at[axis] + (n - s if back else s), n)
            found.append((moved["y"], moved["x"], moved["z"], core))
        return found

    def sibling(self):
        y, x, z, core = self.place()
        return self.device(y, x, z, 1 - core)

    def across(self):
        y, x, z, core = self.place()
        nz = self.sizes[2]
        return self.device(y, x, lax.rem(z + nz // 2, nz), core)

    def group(self, back=False):
        y, x, z, core = self.place()
        chips = self.sizes[2] // 2
        base = (z // chips) * chips
        here = z - base
        chosen = [lax.rem(here + (chips - s if back else s), chips) for s in range(1, chips)]
        return [(chip, self.device(y, x, base + chip, core)) for chip in chosen]

    def meet(self):
        barrier = pltpu.get_barrier_semaphore()
        partners = [self.device(*p) for a in "zxy" for p in self.peers(a)] + [self.sibling()]
        for partner in partners:
            pl.semaphore_signal(barrier, inc=1, device_id=partner, device_id_type=MESH)
        pl.semaphore_wait(barrier, len(partners))

    def copy(self, key, src, dst, target):
        k = self.index.setdefault(key, len(self.index))
        return pltpu.make_async_remote_copy(
            src_ref=src,
            dst_ref=dst,
            send_sem=self.send_sem.at[k],
            recv_sem=self.recv_sem.at[k],
            device_id=target,
            device_id_type=MESH,
        )


class Gather:
    def __init__(self, links, tag, shard, whole, order, cols, local_sem):
        self.links = links
        self.tag = tag
        self.shard = shard
        self.whole = whole
        self.order = order
        self.cols = cols
        self.local_sem = local_sem

    def own(self):
        y, x, z, core = self.links.place()
        return self.whole.at[y, x, z, core, :, self.cols]

    def slab(self, stage, at):
        y, x, z, core = at
        if stage == 0:
            return self.whole.at[y, x, z, core, :, self.cols]
        if stage == 1:
            return self.whole.at[y, x, :, core, :, self.cols]
        if self.order[0] == "x":
            return self.whole.at[y, :, :, core, :, self.cols]
        return self.whole.at[:, x, :, core, :, self.cols]

    def axis(self, stage):
        return ("z",) + tuple(self.order)[0:2] if stage is None else ("z", self.order[0], self.order[1])[stage]

    def send(self, stage):
        me = self.links.place()
        src = self.shard.at[:, self.cols] if stage == 0 else self.slab(stage, me)
        dst = self.slab(stage, me)
        return [
            self.links.copy((self.tag, stage, i), src, dst, self.links.device(*p))
            for i, p in enumerate(self.links.peers(self.axis(stage)))
        ]

    def forward(self, stage):
        sibling = self.links.sibling()
        if stage < 0:
            return [self.links.copy((self.tag, "own"), self.shard.at[:, self.cols], self.own(), sibling)]
        return [
            self.links.copy((self.tag, "pass", stage, i), self.slab(stage, p), self.slab(stage, p), sibling)
            for i, p in enumerate(self.links.peers(self.axis(stage), back=True))
        ]

    def local(self):
        return pltpu.make_async_copy(self.shard.at[:, self.cols], self.own(), self.local_sem)

    def start(self):
        self.local().start()
        for copy in self.send(0) + self.forward(-1):
            copy.start()

    def step(self, stage):
        if stage == 1:
            self.local().wait()
        for copy in self.send(stage - 1):
            copy.wait()
        if stage < 3:
            for copy in self.send(stage):
                copy.start()
        for copy in self.forward(stage - 1):
            copy.start()

    def close(self):
        for stage in range(-1, 3):
            for copy in self.forward(stage):
                copy.wait()

    @staticmethod
    def copies(sizes):
        return 2 * sum(n - 1 for n in sizes) + 1


class Scatter:
    def __init__(self, links, tag, part, order, cols, halves, firsts, seconds, thirds, temp, temp_sem, out):
        self.links = links
        self.tag = tag
        self.part = part
        self.order = order
        self.cols = cols
        self.sums = halves
        self.got = (firsts, seconds, thirds)
        self.temp = temp
        self.temp_sem = temp_sem
        self.out = out

    def first(self):
        _, _, _, core = self.links.place()
        return self.links.copy(
            (self.tag, "core"), self.part.at[:, :, :, 1 - core, :, self.cols], self.sums, self.links.sibling()
        )

    def load(self):
        _, _, _, core = self.links.place()
        return pltpu.make_async_copy(
            self.part.at[:, :, :, core, :, self.cols], self.temp, self.temp_sem
        )

    def axis(self, stage):
        return (self.order[0], self.order[1], "z")[stage]

    def at(self, stage, place, rest=None):
        y, x, z, _ = place
        if stage == 0:
            return (y,) if self.order[0] == "y" else (slice(None), x)
        if stage == 1:
            return (y, x)
        return (y, x, z)

    def send(self, stage):
        me = self.links.place()
        found = []
        for i, p in enumerate(self.links.peers(self.axis(stage))):
            index = self.at(stage, p)
            found.append(
                self.links.copy(
                    (self.tag, stage, i), self.sums.at[index], self.got[stage].at[i], self.links.device(*p)
                )
            )
        return found

    def start(self):
        self.first().start()

    def begin(self):
        self.first().wait()
        self.load().wait()
        ny, nx, nz = self.links.sizes

        def add(i, carry):
            a, b, c = i // (nx * nz), lax.rem(i // nz, nx), lax.rem(i, nz)
            self.sums[a, b, c] = (
                self.sums[a, b, c].astype(F32) + self.temp[a, b, c].astype(F32)
            ).astype(BF16)
            return carry

        lax.fori_loop(0, ny * nx * nz, add, 0)
        for copy in self.send(0):
            copy.start()

    def middle(self, stage):
        for copy in self.send(stage):
            copy.wait()
        y, x, z, _ = self.links.place()
        _, _, nz = self.links.sizes
        got = self.got[stage]
        peers = got.shape[0]
        if stage == 0:
            other = got.shape[1]

            def add(i, carry):
                b, c = i // nz, lax.rem(i, nz)
                index = (y, b, c) if self.order[0] == "y" else (b, x, c)
                total = self.sums[index].astype(F32)
                for p in range(peers):
                    total = total + got[p, b, c].astype(F32)
                self.sums[index] = total.astype(BF16)
                return carry

            lax.fori_loop(0, other * nz, add, 0)
        else:

            def add(c, carry):
                total = self.sums[y, x, c].astype(F32)
                for p in range(peers):
                    total = total + got[p, c].astype(F32)
                self.sums[y, x, c] = total.astype(BF16)
                return carry

            lax.fori_loop(0, nz, add, 0)
        for copy in self.send(stage + 1):
            copy.start()

    def finish(self):
        for copy in self.send(2):
            copy.wait()
        y, x, z, _ = self.links.place()
        total = self.sums[y, x, z].astype(F32)
        for p in range(self.got[2].shape[0]):
            total = total + self.got[2][p].astype(F32)
        self.out[:, self.cols] = total

    @staticmethod
    def copies(sizes):
        return sum(n - 1 for n in sizes) + 1

    @staticmethod
    def scratch(sizes, order, rows, width):
        ny, nx, nz = sizes
        na, nb = (ny, nx) if order[0] == "y" else (nx, ny)
        return [
            pltpu.VMEM((ny, nx, nz, rows, width), BF16),
            pltpu.VMEM((na - 1, nb, nz, rows, width), BF16),
            pltpu.VMEM((nb - 1, nz, rows, width), BF16),
            pltpu.VMEM((nz - 1, rows, width), BF16),
        ]


ORDERS = ("xy", "yx")


def halves_of(width):
    return (slice(0, width // 2), slice(width // 2, width)) if width >= 512 else (slice(0, width),)


def gather_kernel(sizes, query_ref, kv_ref, moved_ref, query_whole, kv_whole, placed_ref, send_sem, recv_sem, local_sem):
    links = Links(sizes, send_sem, recv_sem)
    links.meet()
    _, _, z, _ = links.place()
    half = z // (sizes[2] // 2)
    parts = []
    for a, (shard, whole) in enumerate(((query_ref, query_whole), (kv_ref, kv_whole))):
        width = shard.shape[-1]
        for b in range(2):
            edge = width // 2 // HEAD_DIM * HEAD_DIM
            cols = slice(0, edge) if b == 0 else slice(edge, width)
            parts.append(
                Gather(links, (a, b), shard, whole, ORDERS[b], cols, local_sem.at[2 * a + b])
            )
    keep = pltpu.make_async_copy(moved_ref.at[half], placed_ref.at[half], local_sem.at[4])
    give = links.copy("moved", moved_ref.at[1 - half], placed_ref.at[half], links.across())
    for part in parts[:2]:
        part.start()
    keep.start()
    for part in parts[2:]:
        part.start()
    for part in parts[:2]:
        part.step(1)
    give.start()
    for part in parts[2:]:
        part.step(1)
    for part in parts[:2]:
        part.step(2)
    for part in parts[2:]:
        part.step(2)
    for part in parts:
        part.step(3)
    for part in parts:
        part.close()
    keep.wait()
    give.wait()


def gather_start(sizes, query, key_value, moved):
    ny, nx, nz = sizes
    rounds = 4 * Gather.copies(sizes) + 1
    query_whole, kv_whole, placed = pl.pallas_call(
        functools.partial(gather_kernel, sizes),
        out_shape=[
            jax.ShapeDtypeStruct((ny, nx, nz, 2) + query.shape, BF16),
            jax.ShapeDtypeStruct((ny, nx, nz, 2) + key_value.shape, BF16),
            jax.ShapeDtypeStruct(moved.shape, BF16),
        ],
        in_specs=[ANY] * 3,
        out_specs=[ANY] * 3,
        scratch_shapes=[
            pltpu.SemaphoreType.DMA((rounds,)),
            pltpu.SemaphoreType.DMA((rounds,)),
            pltpu.SemaphoreType.DMA((5,)),
        ],
        compiler_params=pltpu.CompilerParams(collective_id=1, has_side_effects=True),
        name="gather_start",
    )(query, key_value, moved)
    return query_whole.reshape(D, -1), kv_whole.reshape(D, -1), placed


def roll_half(values):
    return pltpu.roll(values, HEAD_DIM // 2, 1)


def project_kernel(rows, x_ref, gain_ref, wq_ref, wk_ref, wv_ref, qg_ref, kg_ref, cos_ref, sin_ref, normed_ref, q_ref, kv_ref, pre_ref):
    sub = rows // SUBS

    @pl.when(pl.program_id(0) == 0)
    def _():
        values = x_ref[...].astype(F32)
        normed_ref[...] = (values * norm_factor(values) * gain_ref[...]).astype(BF16)

    normed = normed_ref[...]
    cosine, sine = cos_ref[...], sin_ref[...]

    def turned(pre, gain):
        values = pre * norm_factor(pre) * gain
        return (values * cosine + roll_half(values) * sine).astype(BF16)

    query = matmul(normed, wq_ref[...])
    for h in range(2):
        pre = query[:, h * HEAD_DIM : (h + 1) * HEAD_DIM]
        pre_ref[0, :, h * HEAD_DIM : (h + 1) * HEAD_DIM] = pre
        low = turned(pre, qg_ref[...])
        for s in range(2 * SUBS):
            q_ref[0, (2 * s + h) * sub : (2 * s + h + 1) * sub] = low[s * sub : (s + 1) * sub]
    pre = matmul(normed, wk_ref[...])
    pre_ref[0, :, 2 * HEAD_DIM :] = pre
    kv_ref[0, 0] = turned(pre, kg_ref[...]).reshape(2, rows, HEAD_DIM)
    kv_ref[1, 0] = matmul(normed, wv_ref[...]).astype(BF16).reshape(2, rows, HEAD_DIM)


def project(x, gain, query_full, kv_full, query_gain, key_gain, cosine, sine):
    count = x.shape[0]
    rows = count // 2
    full = pl.BlockSpec((count, D), lambda h: (0, 0))
    row = lambda n: pl.BlockSpec((1, n), lambda h: (0, 0))
    table = pl.BlockSpec((count, HEAD_DIM), lambda h: (0, 0))
    return pl.pallas_call(
        functools.partial(project_kernel, rows),
        grid=(KV_HEADS,),
        out_shape=[
            jax.ShapeDtypeStruct((count, D), BF16),
            jax.ShapeDtypeStruct((KV_HEADS, 2 * count, HEAD_DIM), BF16),
            jax.ShapeDtypeStruct((2, KV_HEADS, 2, rows, HEAD_DIM), BF16),
            jax.ShapeDtypeStruct((KV_HEADS, count, 3 * HEAD_DIM), F32),
        ],
        in_specs=[
            full,
            row(D),
            pl.BlockSpec((D, 2 * HEAD_DIM), lambda h: (0, h)),
            pl.BlockSpec((D, HEAD_DIM), lambda h: (0, h)),
            pl.BlockSpec((D, HEAD_DIM), lambda h: (0, KV_HEADS + h)),
            row(HEAD_DIM),
            row(HEAD_DIM),
            table,
            table,
        ],
        out_specs=[
            full,
            pl.BlockSpec((1, 2 * count, HEAD_DIM), lambda h: (h, 0, 0)),
            pl.BlockSpec((2, 1, 2, rows, HEAD_DIM), lambda h: (0, h, 0, 0, 0)),
            pl.BlockSpec((1, count, 3 * HEAD_DIM), lambda h: (h, 0, 0)),
        ],
        compiler_params=pltpu.CompilerParams(vmem_limit_bytes=40 * MIB),
        name="project",
    )(x, gain, query_full, kv_full, kv_full, query_gain, key_gain, cosine, sine)


def project_back_kernel(
    rows, dq_ref, dkv_ref, pre_ref, normed_ref, x_ref, hid_ref, gain_ref, wq_ref, wk_ref, wv_ref, qg_ref, kg_ref, cos_ref, sin_ref,
    dwq_ref, dwk_ref, dwv_ref, dx_ref, in_ref, qk_ref, normed_t, grads,
):
    sub = rows // SUBS
    head = pl.program_id(0)

    @pl.when(head == 0)
    def _():
        normed_t[...] = normed_ref[...].astype(F32).T.astype(BF16)
        grads[...] = jnp.zeros_like(grads)
        qk_ref[...] = jnp.zeros_like(qk_ref)

    cosine, sine = cos_ref[...], sin_ref[...]

    def back(turned_grad, pre, gain):
        grad = turned_grad * cosine - roll_half(turned_grad) * sine
        factor = norm_factor(pre)
        grad_pre, part = norm_backward(grad, gain, pre * factor, factor)
        return grad_pre.astype(BF16), jnp.sum(part, axis=0, keepdims=True)

    pieces = []
    for h in range(2):
        grad = jnp.concatenate(
            [dq_ref[0, (2 * s + h) * sub : (2 * s + h + 1) * sub] for s in range(2 * SUBS)], axis=0
        )
        low, part = back(grad, pre_ref[0, :, h * HEAD_DIM : (h + 1) * HEAD_DIM], qg_ref[...])
        qk_ref[0:1] += part
        pieces.append(low)
    low, part = back(dkv_ref[0, 0].reshape(2 * rows, HEAD_DIM), pre_ref[0, :, 2 * HEAD_DIM :], kg_ref[...])
    qk_ref[1:2] += part
    pieces.append(low)
    pieces.append(dkv_ref[1, 0].reshape(2 * rows, HEAD_DIM).astype(BF16))
    low = jnp.concatenate(pieces, axis=1)
    weights = jnp.concatenate([wq_ref[...], wk_ref[...], wv_ref[...]], axis=1)
    grads[...] += nt(low, weights)
    part = matmul(normed_t[...], low).astype(BF16)
    dwq_ref[...] = part[:, : 2 * HEAD_DIM]
    dwk_ref[...] = part[:, 2 * HEAD_DIM : 3 * HEAD_DIM]
    dwv_ref[...] = part[:, 3 * HEAD_DIM :]

    @pl.when(head == KV_HEADS - 1)
    def _():
        values = x_ref[...].astype(F32)
        factor = norm_factor(values)
        grad_in, part = norm_backward(grads[...], gain_ref[...], values * factor, factor)
        dx_ref[...] = (hid_ref[...] + grad_in).astype(BF16)
        in_ref[...] = jnp.sum(part, axis=0, keepdims=True)


def project_back(dq, dkv, pre, normed, x, grad_hidden, gain, query_full, kv_full, query_gain, key_gain, cosine, sine):
    count = x.shape[0]
    rows = count // 2
    full = pl.BlockSpec((count, D), lambda h: (0, 0))
    row = lambda n: pl.BlockSpec((1, n), lambda h: (0, 0))
    table = pl.BlockSpec((count, HEAD_DIM), lambda h: (0, 0))
    wide = pl.BlockSpec((D, 2 * HEAD_DIM), lambda h: (0, h))
    thin = pl.BlockSpec((D, HEAD_DIM), lambda h: (0, h))
    return pl.pallas_call(
        functools.partial(project_back_kernel, rows),
        grid=(KV_HEADS,),
        out_shape=[
            jax.ShapeDtypeStruct((D, QD), BF16),
            jax.ShapeDtypeStruct((D, KVD), BF16),
            jax.ShapeDtypeStruct((D, KVD), BF16),
            jax.ShapeDtypeStruct((count, D), BF16),
            jax.ShapeDtypeStruct((1, D), F32),
            jax.ShapeDtypeStruct((8, HEAD_DIM), F32),
        ],
        in_specs=[
            pl.BlockSpec((1, 2 * count, HEAD_DIM), lambda h: (h, 0, 0)),
            pl.BlockSpec((2, 1, 2, rows, HEAD_DIM), lambda h: (0, h, 0, 0, 0)),
            pl.BlockSpec((1, count, 3 * HEAD_DIM), lambda h: (h, 0, 0)),
            full,
            full,
            full,
            row(D),
            wide,
            thin,
            pl.BlockSpec((D, HEAD_DIM), lambda h: (0, KV_HEADS + h)),
            row(HEAD_DIM),
            row(HEAD_DIM),
            table,
            table,
        ],
        out_specs=[wide, thin, thin, full, row(D), pl.BlockSpec((8, HEAD_DIM), lambda h: (0, 0))],
        scratch_shapes=[pltpu.VMEM((D, count), BF16), pltpu.VMEM((count, D), F32)],
        compiler_params=pltpu.CompilerParams(vmem_limit_bytes=48 * MIB),
        name="project_back",
    )(dq, dkv, pre, normed, x, grad_hidden, gain, query_full, kv_full, kv_full, query_gain, key_gain, cosine, sine)


class KeyValues:
    def __init__(self, links, rows, own, held, local_sem):
        self.links = links
        self.rows = rows
        self.own = own
        self.held = held
        self.local_sem = local_sem

    def slab(self, group, piece, member):
        members = self.links.sizes[2]
        start = pl.multiple_of(self.rows * (piece * members + member), self.rows)
        return self.held.at[:, 2 * group : 2 * group + 2, pl.ds(start, self.rows)]

    def mine(self):
        _, _, z, core = self.links.place()
        return lax.rem(z, self.links.sizes[2] // 2) * 2 + core

    def across(self, group):
        found = []
        for piece in range(2):
            src = self.own.at[:, 2 * group : 2 * group + 2, piece]
            dst = self.slab(group, piece, self.mine())
            for i, (_, target) in enumerate(self.links.group()):
                found.append(self.links.copy(("kv", group, piece, i), src, dst, target))
        return found

    def near(self, group):
        found = []
        for piece in range(2):
            src = self.own.at[:, 2 * group : 2 * group + 2, piece]
            dst = self.slab(group, piece, self.mine())
            found.append(self.links.copy(("kv own", group, piece), src, dst, self.links.sibling()))
            found.append(pltpu.make_async_copy(src, dst, self.local_sem.at[2 * group + piece]))
        return found

    def forward(self, group):
        _, _, _, core = self.links.place()
        found = []
        for piece in range(2):
            for i, (chip, _) in enumerate(self.links.group(back=True)):
                slab = self.slab(group, piece, chip * 2 + core)
                found.append(
                    self.links.copy(("kv pass", group, piece, i), slab, slab, self.links.sibling())
                )
        return found

    @staticmethod
    def copies(sizes):
        return 4 * 2 * (2 * (sizes[2] // 2 - 1) + 1)


def run_all(copies, act):
    for copy in copies:
        if act == "start":
            copy.start()
        else:
            copy.wait()


def row_places(shape, dim, sub):
    t = lax.broadcasted_iota(jnp.int32, shape, dim)
    return (t // (2 * sub)) * sub + t % sub


def gather_parents(meta, lead, slot, pairs):
    runs = (TREE - TRUNK) // SEG
    for k in range(LOCAL_RUNS):
        parent = meta[jnp.minimum(lead + k, runs - 1)]
        for read, out in pairs:
            total = None
            for b in range(runs):
                share = (1 - jnp.minimum(jnp.abs(parent - b), 1)).astype(F32).astype(BF16)
                term = read(b) * share
                total = term if total is None else total + term
            out[slot + k] = total


def forward_kernel(sizes, rows, meta, q_ref, kv_ref, *refs):
    shard = refs[:4]
    mixed_ref, l_ref, kv_all = refs[4:7]
    whole = refs[7:11]
    kvs, acc, part, places, kp, vp, send_sem, recv_sem, local_sem = refs[11:]
    members = sizes[2]
    sub = rows // SUBS
    head = pl.program_id(0)
    links = Links(sizes, send_sem, recv_sem)
    kv = KeyValues(links, rows, kv_ref, kvs, local_sem)
    weights_ = []
    for a in range(4):
        for b, cols in enumerate(halves_of(shard[a].shape[-1])):
            weights_.append(
                (a, Gather(links, (a, b), shard[a], whole[a], ORDERS[b], cols, local_sem.at[16 + 2 * a + b]))
            )

    def each(array):
        return [g for a, g in weights_ if a == array]

    def kept(group):
        return pltpu.make_async_copy(
            kvs.at[:, 2 * group : 2 * group + 2],
            kv_all.at[:, 2 * group : 2 * group + 2],
            local_sem.at[8 + group],
        )

    @pl.when(head == 0)
    def _():
        links.meet()
        for group in range(4):
            run_all(kv.across(group), "start")
            run_all(kv.near(group), "start")
            for g in each(group):
                g.start()
        l_ref[...] = jnp.zeros_like(l_ref)
        places[...] = row_places(places.shape, 0, sub)

    for group in range(4):

        @pl.when(head == 2 * group)
        def _():
            run_all(kv.across(group), "wait")
            run_all(kv.forward(group), "start")
            run_all(kv.near(group), "wait")
            run_all(kv.forward(group), "wait")
            kept(group).start()

    _, _, z, core = links.place()
    mine = lax.rem(z, members // 2) * 2 + core
    lane = lax.broadcasted_iota(jnp.int32, (2 * rows, HEAD_DIM), 1)
    for piece in range(2):
        base = rows * (piece * members + mine)
        region = slice(piece * 2 * rows, (piece + 1) * 2 * rows)
        acc[...] = jnp.zeros_like(acc)
        part[...] = jnp.zeros_like(part)

        def trunk(step, masked):
            start = pl.multiple_of(step * CHUNK, CHUNK)
            weights = jnp.exp2(nt(q_ref[0, region], kvs[0, head, pl.ds(start, CHUNK)]) * exp2_scale)
            low, high = weights[:, :HEAD_DIM], weights[:, HEAD_DIM:]
            if masked:
                room = places[...] + (base - start)
                low = jnp.where(lane <= room, low, 0.0)
                high = jnp.where(lane + HEAD_DIM <= room, high, 0.0)
                weights = jnp.concatenate([low, high], axis=1)
            part[...] += low + high
            acc[...] += matmul(weights.astype(BF16), kvs[1, head, pl.ds(start, CHUNK)])
            return masked

        if piece == 0:
            clear = jnp.minimum(base // CHUNK, TRUNK // CHUNK)
            last = jnp.minimum((base + rows + CHUNK - 1) // CHUNK, TRUNK // CHUNK)
            lax.fori_loop(0, clear, lambda i, c: (trunk(i, False), c)[1], 0)
            lax.fori_loop(clear, last, lambda i, c: (trunk(i, True), c)[1], 0)
        else:
            lax.fori_loop(0, TRUNK // CHUNK, lambda i, c: (trunk(i, False), c)[1], 0)

        lead = jnp.maximum(base - TRUNK, 0) // SEG

        def parents_():
            gather_parents(
                meta,
                lead,
                0,
                [
                    (lambda b: kvs[0, head, TRUNK + b * SEG : TRUNK + (b + 1) * SEG], kp),
                    (lambda b: kvs[1, head, TRUNK + b * SEG : TRUNK + (b + 1) * SEG], vp),
                ],
            )

        if piece == 0:
            pl.when(base + rows > TRUNK)(parents_)
        else:
            parents_()
        for s in range(SUBS):
            block = slice(2 * sub * s, 2 * sub * (s + 1))

            def runs():
                row = base + s * sub - TRUNK
                run = row // SEG
                own = pl.multiple_of(TRUNK + run * SEG, SEG)
                flag = jnp.minimum(meta[run] + 1, 1).astype(F32)
                query = q_ref[0, piece * 2 * rows + 2 * sub * s : piece * 2 * rows + 2 * sub * (s + 1)]
                room = places[block] + (lax.rem(row, SEG) - s * sub)
                weights = jnp.exp2(nt(query, kvs[0, head, pl.ds(own, SEG)]) * exp2_scale)
                weights = jnp.where(lane[block] <= room, weights, 0.0)
                above = jnp.exp2(nt(query, kp[run - lead]) * exp2_scale) * flag
                part[block] += weights + above
                acc[block] += matmul(weights.astype(BF16), kvs[1, head, pl.ds(own, SEG)]) + matmul(
                    above.astype(BF16), vp[run - lead]
                )

            if piece == 0:
                pl.when(base + s * sub >= TRUNK)(runs)
            else:
                runs()

        total = jnp.sum(part[...], axis=-1, keepdims=True)
        mixed = (acc[...] / total).astype(BF16)
        for s in range(SUBS):
            for h in range(2):
                row = piece * rows + sub * s
                mixed_ref[row : row + sub, h * HEAD_DIM : (h + 1) * HEAD_DIM] = mixed[
                    (2 * s + h) * sub : (2 * s + h + 1) * sub
                ]
        l_ref[region] = jnp.where(lane == head, total, l_ref[region])

    plan = {
        0: [(0, 1)],
        1: [(1, 1)],
        2: [(0, 2)],
        3: [(2, 1)],
        4: [(1, 2), (0, 3)],
        5: [(3, 1)],
        6: [(2, 2), (1, 3)],
        7: [(3, 2), (2, 3), (3, 3)],
    }
    for at, steps in plan.items():

        @pl.when(head == at)
        def _():
            for array, stage in steps:
                for g in each(array):
                    g.step(stage)
            if at == KV_HEADS - 1:
                for _, g in weights_:
                    g.close()
                for group in range(4):
                    kept(group).wait()


def forward(sizes, meta, queries, kv, shards_):
    ny, nx, nz = sizes
    rows = kv.shape[3]
    rounds = KeyValues.copies(sizes) + 8 * Gather.copies(sizes)
    results = pl.pallas_call(
        functools.partial(forward_kernel, sizes, rows),
        out_shape=[
            jax.ShapeDtypeStruct((2 * rows, QD), BF16),
            jax.ShapeDtypeStruct((4 * rows, HEAD_DIM), F32),
            jax.ShapeDtypeStruct((2, KV_HEADS, TREE, HEAD_DIM), BF16),
        ]
        + [jax.ShapeDtypeStruct((ny, nx, nz, 2) + s.shape, BF16) for s in shards_],
        grid_spec=pltpu.PrefetchScalarGridSpec(
            num_scalar_prefetch=1,
            grid=(KV_HEADS,),
            in_specs=[pl.BlockSpec((1, 4 * rows, HEAD_DIM), lambda h, meta: (h, 0, 0)), ANY] + [ANY] * 4,
            out_specs=[
                pl.BlockSpec((2 * rows, 2 * HEAD_DIM), lambda h, meta: (0, h)),
                pl.BlockSpec((4 * rows, HEAD_DIM), lambda h, meta: (0, 0)),
                ANY,
            ]
            + [ANY] * 4,
            scratch_shapes=[
                pltpu.VMEM((2, KV_HEADS, TREE, HEAD_DIM), BF16),
                pltpu.VMEM((2 * rows, HEAD_DIM), F32),
                pltpu.VMEM((2 * rows, HEAD_DIM), F32),
                pltpu.VMEM((2 * rows, HEAD_DIM), jnp.int32),
                pltpu.VMEM((LOCAL_RUNS, SEG, HEAD_DIM), BF16),
                pltpu.VMEM((LOCAL_RUNS, SEG, HEAD_DIM), BF16),
                pltpu.SemaphoreType.DMA((rounds,)),
                pltpu.SemaphoreType.DMA((rounds,)),
                pltpu.SemaphoreType.DMA((24,)),
            ],
        ),
        compiler_params=pltpu.CompilerParams(
            collective_id=2, has_side_effects=True, vmem_limit_bytes=48 * MIB
        ),
        name="forward",
    )(meta, queries, kv, *shards_)
    return results[:3], [w.reshape(D, -1) for w in results[3:]]


def backward_kernel(sizes, rows, shard_rows, widths, meta, q_ref, g_ref, k_ref, v_ref, lse_ref, del_ref, *refs):
    parts = refs[:4]
    dq_ref, dkv_ref = refs[4:6]
    outs = refs[6:10]
    dq, dk, dv, pk, pv, kp, vp, stage, near, sums, far, last, temp = refs[10:23]
    buffers = refs[23:-3]
    send_sem, recv_sem, local_sem = refs[-3:]
    members = sizes[2]
    chips = members // 2
    sub = rows // SUBS
    head = pl.program_id(0)
    links = Links(sizes, send_sem, recv_sem)
    scatters = []
    for a in range(4):
        for b, cols in enumerate(halves_of(widths[a])):
            k = 4 * len(scatters)
            width = cols.stop - cols.start
            scatters.append(
                (
                    a,
                    Scatter(
                        links,
                        (a, b),
                        parts[a],
                        ORDERS[b],
                        cols,
                        *buffers[k : k + 4],
                        temp.at[b, :, :, :, :, :width],
                        local_sem.at[b],
                        outs[a],
                    ),
                )
            )

    def each(array):
        return [s for a, s in scatters if a == array]

    @pl.when(head == 0)
    def _():
        links.meet()
        for s in each(0):
            s.load().start()
        for _, s in scatters:
            s.start()

    _, _, z, core = links.place()
    here = lax.rem(z, chips)
    mine = here * 2 + core
    dk[...] = jnp.zeros_like(dk)
    dv[...] = jnp.zeros_like(dv)
    pk[...] = jnp.zeros_like(pk)
    pv[...] = jnp.zeros_like(pv)
    for piece in range(2):
        base = rows * (piece * members + mine)
        at = piece * 2 * rows
        region = slice(at, at + 2 * rows)
        dq[...] = jnp.zeros_like(dq)

        def pair(key, value, block, mask):
            spot = slice(at + block.start, at + block.stop)
            weights = jnp.exp2(nt(key, q_ref[0, spot]) * exp2_scale - lse_ref[0, :, spot])
            if mask is not None:
                weights = mask(weights)
            grads = (weights * (nt(value, g_ref[0, spot]) - del_ref[0, :, spot])).astype(BF16)
            weights = weights.astype(BF16)
            dq[block] += contract_rows(grads, key)
            return matmul(grads, q_ref[0, spot]), matmul(weights, g_ref[0, spot])

        everything = slice(0, 2 * rows)

        def trunk(step, masked):
            start = pl.multiple_of(step * CHUNK, CHUNK)

            def mask(weights):
                shape = weights.shape
                room = row_places((1, shape[1]), 1, sub) + (base - start)
                return jnp.where(lax.broadcasted_iota(jnp.int32, shape, 0) <= room, weights, 0.0)

            key_grad, value_grad = pair(
                k_ref[0, 0, pl.ds(start, CHUNK)],
                v_ref[0, 0, pl.ds(start, CHUNK)],
                everything,
                mask if masked else None,
            )
            dk[pl.ds(start, CHUNK)] += key_grad
            dv[pl.ds(start, CHUNK)] += value_grad

        if piece == 0:
            clear = jnp.minimum(base // CHUNK, TRUNK // CHUNK)
            end = jnp.minimum((base + rows + CHUNK - 1) // CHUNK, TRUNK // CHUNK)
            lax.fori_loop(0, clear, lambda i, c: (trunk(i, False), c)[1], 0)
            lax.fori_loop(clear, end, lambda i, c: (trunk(i, True), c)[1], 0)
        else:
            lax.fori_loop(0, TRUNK // CHUNK, lambda i, c: (trunk(i, False), c)[1], 0)

        lead = jnp.maximum(base - TRUNK, 0) // SEG

        def parents_():
            gather_parents(
                meta,
                lead,
                0,
                [
                    (lambda b: k_ref[0, 0, TRUNK + b * SEG : TRUNK + (b + 1) * SEG], kp),
                    (lambda b: v_ref[0, 0, TRUNK + b * SEG : TRUNK + (b + 1) * SEG], vp),
                ],
            )

        if piece == 0:
            pl.when(base + rows > TRUNK)(parents_)
        else:
            parents_()
        for s in range(SUBS):
            block = slice(2 * sub * s, 2 * sub * (s + 1))

            def runs():
                row = base + s * sub - TRUNK
                run = row // SEG
                own = pl.multiple_of(TRUNK + run * SEG, SEG)
                flag = jnp.minimum(meta[run] + 1, 1).astype(F32)

                def mask(weights):
                    shape = weights.shape
                    room = lax.broadcasted_iota(jnp.int32, shape, 1) % sub + lax.rem(row, SEG)
                    return jnp.where(lax.broadcasted_iota(jnp.int32, shape, 0) <= room, weights, 0.0)

                key_grad, value_grad = pair(
                    k_ref[0, 0, pl.ds(own, SEG)], v_ref[0, 0, pl.ds(own, SEG)], block, mask
                )
                dk[pl.ds(own, SEG)] += key_grad
                dv[pl.ds(own, SEG)] += value_grad
                key_grad, value_grad = pair(
                    kp[run - lead], vp[run - lead], block, lambda weights: weights * flag
                )
                slot = LOCAL_RUNS * piece + run - lead
                pk[slot] += key_grad
                pv[slot] += value_grad

            if piece == 0:
                pl.when(base + s * sub >= TRUNK)(runs)
            else:
                runs()

        dq_ref[0, region] = dq[...] * score_scale

        def spread():
            parents = [meta[jnp.minimum(lead + k, TREE // SEG - TRUNK // SEG - 1)] for k in range(LOCAL_RUNS)]

            def place(b, carry):
                start = pl.multiple_of(TRUNK + b * SEG, SEG)
                key_grad, value_grad = dk[pl.ds(start, SEG)], dv[pl.ds(start, SEG)]
                for k in range(LOCAL_RUNS):
                    share = (1 - jnp.minimum(jnp.abs(parents[k] - b), 1)).astype(F32)
                    key_grad += pk[LOCAL_RUNS * piece + k] * share
                    value_grad += pv[LOCAL_RUNS * piece + k] * share
                dk[pl.ds(start, SEG)] = key_grad
                dv[pl.ds(start, SEG)] = value_grad
                return carry

            lax.fori_loop(0, (TREE - TRUNK) // SEG, place, 0)

        if piece == 0:
            pl.when(base + rows > TRUNK)(spread)
        else:
            spread()

    def core_copy(h):
        return links.copy(("kv core", h), stage.at[h % 2, :, 1 - core], near.at[h % 2], links.sibling())

    def far_copies(h):
        return [
            links.copy(("kv z", h, i), sums.at[h, chip], far.at[h, i], target)
            for i, (chip, target) in enumerate(links.group())
        ]

    def pass_on(h):
        core_copy(h).wait()

        def add(i, carry):
            chip, which, piece = i // 4, lax.rem(i // 2, 2), lax.rem(i, 2)
            sums[h, chip, which, piece] = (
                stage[h % 2, chip, core, which, piece].astype(F32) + near[h % 2, chip, which, piece].astype(F32)
            ).astype(BF16)
            return carry

        lax.fori_loop(0, chips * 4, add, 0)
        run_all(far_copies(h), "start")

    for h in range(1, KV_HEADS):
        pl.when(head == h)(functools.partial(pass_on, h - 1))

    for which, grad, scale in ((0, dk, score_scale), (1, dv, 1.0)):
        for piece in range(2):
            for member in range(members):
                start = rows * (piece * members + member)
                stage[lax.rem(head, 2), member // 2, member % 2, which, piece] = (
                    grad[start : start + rows] * scale
                ).astype(BF16)
    for h in range(KV_HEADS):

        @pl.when(head == h)
        def _():
            core_copy(h).start()

    plan = {
        0: [(0, 0)],
        1: [(1, 0)],
        2: [(0, 1)],
        3: [(2, 0), (0, 2)],
        4: [(1, 1)],
        5: [(3, 0), (1, 2)],
        6: [(2, 1)],
        7: [(3, 1), (2, 2), (3, 2)],
    }
    for moment, steps in plan.items():

        @pl.when(head == moment)
        def _():
            if moment == KV_HEADS - 1:
                pass_on(moment)
            for array, step in steps:
                for s in each(array):
                    if step == 0:
                        s.begin()
                    else:
                        s.middle(step - 1)
                if step == 0 and array < 3:
                    for s in each(array + 1):
                        s.load().start()

            def result(h):
                return pltpu.make_async_copy(last.at[h % 2], dkv_ref.at[:, h], local_sem.at[2 + h % 2])

            if moment == KV_HEADS - 1:
                for h in range(KV_HEADS):
                    run_all(far_copies(h), "wait")
                    if h > 1:
                        result(h - 2).wait()
                    for which in range(2):
                        for piece in range(2):
                            total = sums[h, here, which, piece].astype(F32)
                            for i in range(chips - 1):
                                total = total + far[h, i, which, piece].astype(F32)
                            last[h % 2, which, piece] = total
                    result(h).start()
                for _, s in scatters:
                    s.finish()
                for h in (KV_HEADS - 2, KV_HEADS - 1):
                    result(h).wait()


def backward(sizes, meta, queries, grads, kv_all, log_total, delta, parts):
    ny, nx, nz = sizes
    chips = nz // 2
    rows = queries.shape[1] // 4
    widths = tuple(p.shape[-1] for p in parts)
    shard_rows = D // (ny * nx * nz * 2)
    pieces = [p.reshape(ny, nx, nz, 2, shard_rows, p.shape[-1]) for p in parts]
    stack = pl.BlockSpec((1, 4 * rows, HEAD_DIM), lambda h, meta: (h, 0, 0))
    line = pl.BlockSpec((1, 1, 4 * rows), lambda h, meta: (h, 0, 0))
    buffers = []
    for w in widths:
        for b, cols in enumerate(halves_of(w)):
            buffers += Scatter.scratch(sizes, ORDERS[b], shard_rows, cols.stop - cols.start)
    rounds = 8 * Scatter.copies(sizes) + KV_HEADS * chips
    results = pl.pallas_call(
        functools.partial(backward_kernel, sizes, rows, shard_rows, widths),
        out_shape=[
            jax.ShapeDtypeStruct((KV_HEADS, 4 * rows, HEAD_DIM), F32),
            jax.ShapeDtypeStruct((2, KV_HEADS, 2, rows, HEAD_DIM), F32),
        ]
        + [jax.ShapeDtypeStruct((shard_rows, w), F32) for w in widths],
        grid_spec=pltpu.PrefetchScalarGridSpec(
            num_scalar_prefetch=1,
            grid=(KV_HEADS,),
            in_specs=[
                stack,
                stack,
                pl.BlockSpec((1, 1, TREE, HEAD_DIM), lambda h, meta: (0, h, 0, 0)),
                pl.BlockSpec((1, 1, TREE, HEAD_DIM), lambda h, meta: (1, h, 0, 0)),
                line,
                line,
            ]
            + [ANY] * 4,
            out_specs=[stack, ANY] + [pl.BlockSpec((shard_rows, w), lambda h, meta: (0, 0)) for w in widths],
            scratch_shapes=[
                pltpu.VMEM((2 * rows, HEAD_DIM), F32),
                pltpu.VMEM((TREE, HEAD_DIM), F32),
                pltpu.VMEM((TREE, HEAD_DIM), F32),
                pltpu.VMEM((2 * LOCAL_RUNS, SEG, HEAD_DIM), F32),
                pltpu.VMEM((2 * LOCAL_RUNS, SEG, HEAD_DIM), F32),
                pltpu.VMEM((LOCAL_RUNS, SEG, HEAD_DIM), BF16),
                pltpu.VMEM((LOCAL_RUNS, SEG, HEAD_DIM), BF16),
                pltpu.VMEM((2, chips, 2, 2, 2, rows, HEAD_DIM), BF16),
                pltpu.VMEM((2, chips, 2, 2, rows, HEAD_DIM), BF16),
                pltpu.VMEM((KV_HEADS, chips, 2, 2, rows, HEAD_DIM), BF16),
                pltpu.VMEM((KV_HEADS, chips - 1, 2, 2, rows, HEAD_DIM), BF16),
                pltpu.VMEM((2, 2, 2, rows, HEAD_DIM), F32),
                pltpu.VMEM((2, ny, nx, nz, shard_rows, max(widths) // 2), BF16),
            ]
            + buffers
            + [
                pltpu.SemaphoreType.DMA((rounds,)),
                pltpu.SemaphoreType.DMA((rounds,)),
                pltpu.SemaphoreType.DMA((4,)),
            ],
        ),
        compiler_params=pltpu.CompilerParams(
            collective_id=3, has_side_effects=True, vmem_limit_bytes=61 * MIB
        ),
        name="backward",
    )(
        meta,
        queries,
        grads,
        kv_all,
        kv_all,
        log_total.reshape(KV_HEADS, 1, 4 * rows),
        delta.reshape(KV_HEADS, 1, 4 * rows),
        *pieces,
    )
    return results[0], results[1], results[2:]


def scatter_kernel(sizes, widths, *refs):
    count = len(widths)
    parts = refs[:count]
    moved_ref = refs[count]
    outs = refs[count + 1 : 2 * count + 1]
    placed_ref = refs[2 * count + 1]
    rest = refs[2 * count + 2 :]
    send_sem, recv_sem, local_sem = rest[-3:]
    links = Links(sizes, send_sem, recv_sem)
    scatters = []
    used = 0
    for a in range(count):
        for b, cols in enumerate(halves_of(widths[a])):
            k = 5 * used
            scatters.append(
                Scatter(
                    links,
                    (a, b),
                    parts[a],
                    ORDERS[b],
                    cols,
                    *rest[k : k + 4],
                    rest[k + 4],
                    local_sem.at[used],
                    outs[a],
                )
            )
            used += 1
    for s in scatters:
        s.load().start()
    links.meet()
    for s in scatters:
        s.start()
    _, _, z, _ = links.place()
    half = z // (sizes[2] // 2)
    keep = pltpu.make_async_copy(moved_ref.at[half], placed_ref.at[half], local_sem.at[used])
    give = links.copy("moved", moved_ref.at[1 - half], placed_ref.at[half], links.across())
    keep.start()
    give.start()
    depth = 2
    for i, s in enumerate(scatters):
        if i >= depth:
            scatters[i - depth].middle(0)
        s.begin()
    for s in scatters[-depth:]:
        s.middle(0)
    for s in scatters:
        s.middle(1)
    for s in scatters:
        s.finish()
    keep.wait()
    give.wait()


def scatter_end(sizes, parts, moved):
    ny, nx, nz = sizes
    shard_rows = D // (ny * nx * nz * 2)
    widths = tuple(p.shape[-1] for p in parts)
    pieces = [p.reshape(ny, nx, nz, 2, shard_rows, p.shape[-1]) for p in parts]
    buffers, count = [], 0
    for w in widths:
        for b, cols in enumerate(halves_of(w)):
            buffers += Scatter.scratch(sizes, ORDERS[b], shard_rows, cols.stop - cols.start)
            buffers.append(pltpu.VMEM((ny, nx, nz, shard_rows, cols.stop - cols.start), BF16))
            count += 1
    rounds = count * Scatter.copies(sizes) + 1
    results = pl.pallas_call(
        functools.partial(scatter_kernel, sizes, widths),
        out_shape=[jax.ShapeDtypeStruct((shard_rows, w), F32) for w in widths]
        + [jax.ShapeDtypeStruct(moved.shape, BF16)],
        in_specs=[ANY] * (len(widths) + 1),
        out_specs=[pl.BlockSpec(memory_space=pltpu.VMEM)] * len(widths) + [ANY],
        scratch_shapes=buffers
        + [
            pltpu.SemaphoreType.DMA((rounds,)),
            pltpu.SemaphoreType.DMA((rounds,)),
            pltpu.SemaphoreType.DMA((count + 1,)),
        ],
        compiler_params=pltpu.CompilerParams(
            collective_id=4, has_side_effects=True, vmem_limit_bytes=48 * MIB
        ),
        name="scatter_end",
    )(*pieces, moved)
    return results[:-1], results[-1]


def shards(
    sizes,
    tokens,
    cotangent,
    segment_ids,
    positions,
    parents,
    input_norm,
    query_proj,
    key_proj,
    value_proj,
    query_norm,
    key_norm,
    out_proj,
    post_norm,
    gate_proj,
    up_proj,
    down_proj,
):
    nz = sizes[2]
    rows = tokens.shape[1]
    shard_rows = query_proj.shape[0]
    gain_rows = query_norm.shape[0]
    ctx = lax.axis_index("ctx")
    half = ctx // nz
    member = ctx % nz
    count = 2 * rows
    sub = rows // SUBS
    swap = [(i, (i + nz) % (2 * nz)) for i in range(2 * nz)]

    def column(gain):
        return jnp.pad(gain, (0, shard_rows - gain.shape[0]))[:, None]

    gains = jnp.concatenate(
        [column(input_norm), column(post_norm), column(query_norm), column(key_norm)], axis=1
    )
    gains = jnp.pad(gains, ((0, 0), (0, GAIN_COLS - 4)))
    key_value = jnp.concatenate([key_proj, value_proj, gains], axis=1)
    query_full, kv_full, placed = gather_start(sizes, query_proj, key_value, tokens)
    x = placed.reshape(count, D)

    gain_block = kv_full[:, 2 * KVD :].astype(F32)
    in_weight = gain_block[:, 0][None, :]
    post_weight = gain_block[:, 1]
    by_device = gain_block.reshape(-1, shard_rows, GAIN_COLS)
    query_weight = by_device[:, :gain_rows, 2].reshape(1, HEAD_DIM)
    key_weight = by_device[:, :gain_rows, 3].reshape(1, HEAD_DIM)

    run_seg = segment_ids[half][TRUNK::SEG]
    run_parent = parents[half][run_seg]
    parent_run = jnp.argmax(run_seg[None, :] == run_parent[:, None], axis=1).astype(jnp.int32)
    meta = jnp.where(run_parent > 0, parent_run, -1)
    pos_tree = positions[half].reshape(2, nz, rows)
    pos_local = lax.dynamic_index_in_dim(pos_tree, member, 1, keepdims=False).reshape(count)
    cosine, sine = rope_tables(pos_local)

    normed, queries, kv, pre = project(
        x, in_weight, query_full, kv_full, query_weight, key_weight, cosine, sine
    )
    (mixed, totals, kv_all), (out_t, gate_full, up_full, down_t) = forward(
        sizes, meta, queries, kv, [out_proj.T, gate_proj, up_proj, down_proj.T]
    )
    log_total = jnp.log2(totals[:, :KV_HEADS]).T

    mixed, cotangent = lax.optimization_barrier((mixed, cotangent))
    cot_keep = cotangent[half]
    cot_got = lax.ppermute(cotangent[1 - half], "ctx", swap)
    grad_out = jnp.where(
        half == 0, jnp.concatenate([cot_keep, cot_got]), jnp.concatenate([cot_got, cot_keep])
    )

    hidden = x.astype(F32) + nt(mixed, out_t)
    post_factor = norm_factor(hidden)
    post_hat = hidden * post_factor
    second = (post_hat * post_weight).astype(BF16)
    gate_pre = matmul(second, gate_full)
    up_pre = matmul(second, up_full)
    activated = jax.nn.silu(gate_pre)
    inner = (activated * up_pre).astype(BF16)
    result = (hidden + nt(inner, down_t)).astype(BF16).reshape(2, rows, D)
    result_keep = result[half]
    result_got = lax.ppermute(result[1 - half], "ctx", swap)
    output = jnp.where(
        half == 0, jnp.stack([result_keep, result_got]), jnp.stack([result_got, result_keep])
    )

    grad_inner = matmul(grad_out, down_t)
    sigmoid_gate = jax.nn.sigmoid(gate_pre)
    grad_gate = (
        grad_inner * up_pre * sigmoid_gate * (1.0 + gate_pre * (1.0 - sigmoid_gate))
    ).astype(BF16)
    grad_up = (grad_inner * activated).astype(BF16)
    grad_second = nt(grad_gate, gate_full) + nt(grad_up, up_full)
    grad_post_in, post_part = norm_backward(grad_second, post_weight, post_hat, post_factor)
    grad_hidden = grad_out.astype(F32) + grad_post_in
    grad_branch = grad_hidden.astype(BF16)
    grad_mixed = matmul(grad_branch, out_t).astype(BF16)
    parts = [
        contract_rows(grad_branch, mixed).astype(BF16),
        contract_rows(second, grad_gate).astype(BF16),
        contract_rows(second, grad_up).astype(BF16),
        contract_rows(grad_out, inner).astype(BF16),
    ]
    delta = jnp.sum(
        (grad_mixed.astype(F32) * mixed.astype(F32)).reshape(count, HEADS, HEAD_DIM), axis=-1
    )
    delta = delta.reshape(2, SUBS, sub, KV_HEADS, 2).transpose(3, 0, 1, 4, 2)
    grad_stack = grad_mixed.reshape(2 * SUBS, sub, KV_HEADS, 2, HEAD_DIM).transpose(2, 0, 3, 1, 4)
    grad_stack = grad_stack.reshape(KV_HEADS, 2 * count, HEAD_DIM)
    dq, dkv, (out_grad, gate_grad, up_grad, down_grad) = backward(
        sizes, meta, queries, grad_stack, kv_all, log_total, delta, parts
    )

    dwq, dwk, dwv, dx, in_part, qk_part = project_back(
        dq, dkv, pre, normed, x, grad_hidden, in_weight, query_full, kv_full, query_weight, key_weight, cosine, sine
    )

    def gain_column(values):
        if values.shape[0] == D:
            return values[:, None]
        spread = jnp.pad(values.reshape(-1, gain_rows), ((0, 0), (0, shard_rows - gain_rows)))
        return spread.reshape(D, 1)

    gain_parts = jnp.concatenate(
        [
            gain_column(in_part[0]),
            gain_column(jnp.sum(post_part, axis=0)),
            gain_column(qk_part[0]),
            gain_column(qk_part[1]),
        ],
        axis=1,
    )
    gain_parts = jnp.pad(gain_parts, ((0, 0), (0, GAIN_COLS - 4))).astype(BF16)
    (query_grad, key_grad, value_grad, gain_grad), input_grad = scatter_end(
        sizes, [dwq, dwk, dwv, gain_parts], dx.reshape(2, rows, D)
    )
    return (
        output,
        input_grad.astype(F32),
        gain_grad[:, 0],
        query_grad,
        key_grad,
        value_grad,
        gain_grad[:gain_rows, 2],
        gain_grad[:gain_rows, 3],
        out_grad.T,
        gain_grad[:, 1],
        gate_grad,
        up_grad,
        down_grad.T,
    )


def solution(mesh):
    dp, ctx = mesh.shape["dp"], mesh.shape["ctx"]
    sizes = (2, dp // 2, ctx // 2)
    return jax.shard_map(
        functools.partial(shards, sizes),
        mesh=mesh,
        in_specs=(
            P("dp", "ctx", None),
            P("dp", "ctx", None),
            P("dp", None),
            P("dp", None),
            P("dp", None),
            P(("dp", "ctx")),
            P(("dp", "ctx"), None),
            P(("dp", "ctx"), None),
            P(("dp", "ctx"), None),
            P(("dp", "ctx")),
            P(("dp", "ctx")),
            P(None, ("dp", "ctx")),
            P(("dp", "ctx")),
            P(("dp", "ctx"), None),
            P(("dp", "ctx"), None),
            P(None, ("dp", "ctx")),
        ),
        out_specs=(
            P("dp", "ctx", None),
            P("dp", "ctx", None),
            P(("dp", "ctx")),
            P(("dp", "ctx"), None),
            P(("dp", "ctx"), None),
            P(("dp", "ctx"), None),
            P(("dp", "ctx")),
            P(("dp", "ctx")),
            P(None, ("dp", "ctx")),
            P(("dp", "ctx")),
            P(("dp", "ctx"), None),
            P(("dp", "ctx"), None),
            P(None, ("dp", "ctx")),
        ),
        check_vma=False,
    )
```

time: 1890 us -> 698 us (0.37)
  waiting for transfers between devices: 883 us -> 9.18 us
  matrix products: 676 us -> 84.6 us
  Pallas kernels: 0 us -> 529 us
  other arithmetic: 142 us -> 21.1 us
  blocking collectives: 84.9 us -> 0 us
  local copies, waits for them, and re-layouts: 73.8 us -> 44 us
    dot_general x42 -> x8, matrix products: 601 us -> 55.4 us  [the longest x4 32.6 us: matmul(): return jnp.dot(left_side, right_side, preferred_element_type=F32)]
    pallas_call x0 -> x6, Pallas kernels: none -> 529 us  [the longest x1 169 us: forward(): pl.pallas_call(functools.partial(forward_kernel, sizes, rows), out_shape=...]
    reduce_scatter x6 -> x0, waiting for transfers between devices: 442 us -> none  [the longest x1 352 us: shards(): lax.psum_scatter((lambda first_row, row_count: feed_whole)(jnp.int32(0),...]
    all_gather x11 -> x0, waiting for transfers between devices: 437 us -> none  [the longest x2 72.4 us: shards(): lax.all_gather(key_low.reshape(TR, tree_rows, KV_HEADS, HEAD_DIM), 'ctx',...]
    unnamed x2 -> x0, blocking collectives: 84.9 us -> none
    add x11 -> x1, other arithmetic: 64.6 us -> 2.34 us  [shards(): grad_hidden = grad_out.astype(F32) + grad_post_in]
    dot_general x8 -> x4, matrix products: 74.8 us -> 29.2 us  [contract_rows(): lax.dot_general(left_side, right_side, (((0,), (0,)), ((), ())), preferre...]
    reduce_sum x10 -> x1, other arithmetic: 48 us -> 3.93 us  [shards(): jnp.sum((grad_mixed.astype(F32) * mixed.astype(F32)).reshape(count, HEADS...]
  transfers between devices with their start and end apart: 17 -> 2, of which waited for: 13 -> 1; matrix products, arithmetic and copies ran while one was open for 40% -> 7% of each run, Pallas kernels for 0% -> 39%
where the time goes in v2:
time: 698 us; the launch traced here: 689 us
  Pallas kernels  529 us (76%)
  matrix products  84.6 us (12%)
  local copies, waits for them, and re-layouts  44 us (6%)
  other arithmetic  21.1 us (3%)
  waiting for transfers between devices  9.18 us (1%)
    pallas_call x1, Pallas kernels, forward(): pl.pallas_call(functools.partial(forward_kernel, sizes, rows), out_shape=...  169 us
    pallas_call x1, Pallas kernels, backward(): pl.pallas_call(functools.partial(backward_kernel, sizes, rows, shard_rows...  157 us
    pallas_call x1, Pallas kernels, scatter_end(): pl.pallas_call(functools.partial(scatter_kernel, sizes, widths), out_shap...  72.1 us
    pallas_call x1, Pallas kernels, gather_start(): pl.pallas_call(functools.partial(gather_kernel, sizes), out_shape=[jax.Sh...  68.8 us
    pallas_call x1, Pallas kernels, project_back(): pl.pallas_call(functools.partial(project_back_kernel, rows), grid=(KV_HEA...  39.1 us
    dot_general x4, matrix products, matmul(): return jnp.dot(left_side, right_side, preferred_element_type=F32)  32.6 us
    dot_general x4, matrix products, contract_rows(): lax.dot_general(left_side, right_side, (((0,), (0,)), ((), ())), preferre...  29.2 us
    unnamed x89, local copies, waits for them, and re-layouts  24.6 us
  transfers between devices with their start and end apart: 2, of which 1 were waited for; matrix products, arithmetic and copies ran while one was open for 7% of the time, Pallas kernels for 39%

profile of v2, /device:TPU:0, one launch (start us, length us, event | category | flops | bytes accessed | tf_op | source)
XLA Modules:
  0.0 689.3 jit_solution(3354571284488772392)
XLA Ops:
  7.6 68.8 %gather_start.1 = (bf16[2,2,4,2,32,2048]{5,4,3,2,1,0:T(8,128)(2,1)}, bf16[2,2,4,2,32,2176]{5,4,3,2,1,0:T(8,128)(2,1)}, bf16[2,320,1024]{2,1,0:T(8,128)(2,1)}) custom-call(bf16[32,2048]{1,0:T(8,128)(2,1)} %query_ref.1, bf16[32,2176]{1,0:T(8,128)(2,1)} %fusion.4.kv_ref, bf16[2,320,1024]{2,1,0:T(8,128)(2,1)} %moved_ref.1), custom_call_target="tpu_custom_call" | custom-call | tf_op jit(solution)/shard_map/gather_start/pallas_call | solution.py:381
  80.9 22.7 %project.1 = (bf16[640,1024]{1,0:T(8,128)(2,1)S(1)}, bf16[8,1280,128]{2,1,0:T(8,128)(2,1)S(1)}, bf16[2,8,2,320,128]{4,3,2,1,0:T(8,128)(2,1)S(1)}, f32[8,640,384]{2,1,0:T(8,128)}) custom-call(bf16[640,1024]{1,0:T(8,128)(2,1)S(1)} %bitcast.73, f32[1,1024]{1,0:T(1,128)S(1)} %bitcast.81, bf16[1024,2048]{1,0:T(8,128)(2,1)S(1)} %bitcast.72, ...), custom_call_target="tpu_custom_call" | custom-call | tf_op jit(solution)/shard_map/project/pallas_call | solution.py:439
  107.6 168.8 %forward.1 = (bf16[640,2048]{1,0:T(8,128)(2,1)S(1)}, f32[1280,128]{1,0:T(8,128)S(1)}, bf16[2,8,2560,128]{3,2,1,0:T(8,128)(2,1)}, bf16[2,2,4,2,32,2048]{5,4,3,2,1...) custom-call(s32[12]{0:T(128)S(1)} %compare_select_fusion.1.meta, ...), custom_call_target="tpu_custom_call" | custom-call | tf_op jit(solution)/shard_map/forward/pallas_call | solution.py:795
  282.9 6.0 multiply_reduce_fusion.2
  289.3 6.4 fusion.11
  295.7 6.5 fusion.10
  302.2 9.2 %collective-permute-done.1 = bf16[320,1024]{1,0:T(8,128)(2,1)} collective-permute-done((bf16[320,1024]{1,0:T(8,128)(2,1)}, bf16[320,1024]{1,0:T(8,128)(2,1)}, u32[]{:S(2)}, u32[]{:S(2)}) %collective-permute-start.1) | collective-permute-done | bytes 655392 | tf_op jit(solution)/shard_map/ppermute | solution.py:1309
  311.4 15.4 %multiply_convert_fusion = (bf16[640,3072]{1,0:T(8,128)(2,1)S(1)}, bf16[640,3072]{1,0:T(8,128)(2,1)}, bf16[640,3072]{1,0:T(8,128)(2,1)}) fusion(f32[640,3072]{1,0:T(8,128)} %fusion.10, f32[640,3072]{1,0:T(8,128)} %fusion.11, bf16[1024,3072]{1,0:T(8,128)(2,1)} %bitcast.103, bf16[320,1024]{1,0:T(8,128)(2,1)} %collective-permute-done.1, ...), kind=kOutput, calls=%fused_computation.1 | convolution fusion | flops 4061921280 | bytes 35127296 | tf_op jit(solution)/shard_map/dot_general | solution.py:39
  326.9 7.7 %fusion.12 = f32[640,1024]{1,0:T(8,128)S(1)} fusion(bf16[640,3072]{1,0:T(8,128)(2,1)} %get-tuple-element.94, bf16[1024,3072]{1,0:T(8,128)(2,1)} %bitcast.113), kind=kOutput, calls=%fused_computation.70 | convolution fusion | flops 4026531840 | bytes 12845056 | tf_op jit(solution)/shard_map/dot_general | solution.py:43
  334.6 7.6 %convolution_convert_fusion.2 = bf16[1024,3072]{1,0:T(8,128)(2,1)} fusion(bf16[640,1024]{1,0:T(8,128)(2,1)S(1)} %multiply_convert_fusion.3, bf16[640,3072]{1,0:T(8,128)(2,1)S(1)} %copy-done.31), kind=kOutput, calls=%fused_computation.8 | convolution fusion | flops 4029677568 | bytes 11534336 | tf_op jit(solution)/shard_map/dot_general | solution.py:49
  342.2 7.1 %convolution_convert_fusion.1 = bf16[1024,3072]{1,0:T(8,128)(2,1)} fusion(bf16[640,1024]{1,0:T(8,128)(2,1)S(1)} %multiply_convert_fusion.3, bf16[640,3072]{1,0:T(8,128)(2,1)S(1)} %get-tuple-element.93), kind=kOutput, calls=%fused_computation.7 | convolution fusion | flops 4029677568 | bytes 11534336 | tf_op jit(solution)/shard_map/dot_general | solution.py:49
  349.3 4.8 multiply_reduce_fusion
  358.0 4.2 convolution_convert_fusion.4
  362.2 5.4 reshape.144
  367.7 3.7 multiply_bitcast_fusion
  371.8 5.1 convolution_convert_fusion.3
  376.9 4.3 add_convert_fusion
  385.8 3.5 copy.68
  389.2 3.9 reduce_sum.38
  394.2 9.4 %convolution_convert_fusion = bf16[1024,3072]{1,0:T(8,128)(2,1)} fusion(bf16[640,3072]{1,0:T(8,128)(2,1)} %get-tuple-element.95, bf16[320,1024]{1,0:T(8,128)(2,1)} %collective-permute-done.1, bf16[320,1024]{1,0:T(8,128)(2,1)S(1)} %copy-done.23, pred[]{:T(512)S(6)} %eq.12), kind=kOutput, calls=%fused_computation.6 | convolution fusion | flops 4035575808 | bytes 11534337 | tf_op jit(solution)/shard_map/dot_general | solution.py:49
  403.6 157.2 %backward.1 = (f32[8,1280,128]{2,1,0:T(8,128)}, f32[2,8,2,320,128]{4,3,2,1,0:T(8,128)}, f32[32,2048]{1,0:T(8,128)}, f32[32,3072]{1,0:T(8,128)}, f32[32,3072]{1,0:T(8,128)}, /*index=5*/f32[32,3072]{1,0:T(8,128)}) custom-call(s32[12]{0:T(128)} %copy-done.17, bf16[8,1280,128]{2,1,0:T(8,128)(2,1)} %copy-done.3, bf16[8,1280,128]{2,1,0:T(8,128)(2,1)} %bitcast.89, ...), custom_call_target="tpu_custom_call" | custom-call | tf_op jit(solution)/shard_map/backward/pallas_call | solution.py:1098
  562.1 39.1 %project_back.1 = (bf16[1024,2048]{1,0:T(8,128)(2,1)}, bf16[1024,1024]{1,0:T(8,128)(2,1)}, bf16[1024,1024]{1,0:T(8,128)(2,1)}, bf16[640,1024]{1,0:T(8,128)(2,1)S...) custom-call(f32[8,1280,128]{2,1,0:T(8,128)} %get-tuple-element.62.dq_ref, ...), custom_call_target="tpu_custom_call" | custom-call | tf_op jit(solution)/shard_map/project_back/pallas_call | solution.py:528
  606.0 72.1 %scatter_end.1 = (f32[32,2048]{1,0:T(8,128)S(1)}, f32[32,1024]{1,0:T(8,128)S(1)}, f32[32,1024]{1,0:T(8,128)S(1)}, f32[32,128]{1,0:T(8,128)S(1)}, bf16[2,320,1024]{2,1,0:T(8,128)(2,1)S(1)}) custom-call(bf16[2,2,4,2,32,2048]{5,4,3,2,1,0:T(8,128)(2,1)} %bitcast.95, bf16[2,2,4,2,32,1024]{5,4,3,2,1,0:T(8,128)(2,1)S(1)} %bitcast.76, ...), custom_call_target="tpu_custom_call" | custom-call | tf_op jit(solution)/shard_map/scatter_end/pallas_call | solution.py:1223
  681.3 2.6 maximum_select_fusion
  (148 shorter events, 46.0 us)
Async XLA Ops:
  4.7 102.9 %copy-start.17 = (s32[12]{0:T(128)}, s32[12]{0:T(128)S(1)}, u32[]{:S(2)}) copy-start(s32[12]{0:T(128)S(1)} %compare_select_fusion.1.meta) | copy-start | bytes 148
  80.9 26.7 %copy-start.13 = (bf16[32,3072]{1,0:T(8,128)(2,1)S(1)}, bf16[32,3072]{1,0:T(8,128)(2,1)}, u32[]{:S(2)}) copy-start(bf16[32,3072]{1,0:T(8,128)(2,1)} %refs_1_.1) | copy-start | bytes 589828
  80.9 26.7 %copy-start.14 = (bf16[32,3072]{1,0:T(8,128)(2,1)S(1)}, bf16[32,3072]{1,0:T(8,128)(2,1)}, u32[]{:S(2)}) copy-start(bf16[32,3072]{1,0:T(8,128)(2,1)} %refs_2_.1) | copy-start | bytes 589828
  80.9 26.7 %copy-start.15 = (bf16[3072,32]{0,1:T(8,128)(2,1)S(1)}, bf16[3072,32]{0,1:T(8,128)(2,1)}, u32[]{:S(2)}) copy-start(bf16[3072,32]{0,1:T(8,128)(2,1)} %param.31) | copy-start | bytes 589828
  80.9 26.7 %copy-start.16 = (bf16[2048,32]{0,1:T(8,128)(2,1)S(1)}, bf16[2048,32]{0,1:T(8,128)(2,1)}, u32[]{:S(2)}) copy-start(bf16[2048,32]{0,1:T(8,128)(2,1)} %param.27) | copy-start | bytes 393220
  280.4 31.0 %collective-permute-start.1 = (bf16[320,1024]{1,0:T(8,128)(2,1)}, bf16[320,1024]{1,0:T(8,128)(2,1)}, u32[]{:S(2)}, u32[]{:S(2)}) collective-permute-start(bf16[320,1024]{1,0:T(8,128)(2,1)} %get-tuple-element.97), channel_id=1, source_target_pairs={{0,4},{1,5},{2,6},{3,7},{4,0},{5,1},{6,2},{7,3},{8,12},{9,13},{10,... | collective-permute-start | bytes 1966088 | tf_op jit(solution)/shard_map/ppermute | solution.py:1309
  282.9 6.4 slice-start.2
  282.9 6.4 slice-start.3
  289.0 65.2 %copy-start.20 = (f32[640,1024]{1,0:T(8,128)}, f32[640,1024]{1,0:T(8,128)S(1)}, u32[]{:S(2)}) copy-start(f32[640,1024]{1,0:T(8,128)S(1)} %get-tuple-element.104) | copy-start | bytes 7864324
  289.0 6.7 slice-start.6
  289.3 6.4 slice-start.7
  295.7 15.7 %copy-start.23 = (bf16[320,1024]{1,0:T(8,128)(2,1)S(1)}, bf16[320,1024]{1,0:T(8,128)(2,1)}, u32[]{:S(2)}) copy-start(bf16[320,1024]{1,0:T(8,128)(2,1)} %get-tuple-element.96) | copy-start | bytes 1966084
  326.9 7.7 %copy-start.31 = (bf16[640,3072]{1,0:T(8,128)(2,1)S(1)}, bf16[640,3072]{1,0:T(8,128)(2,1)}, u32[]{:S(2)}) copy-start(bf16[640,3072]{1,0:T(8,128)(2,1)} %get-tuple-element.94) | copy-start | bytes 11796484
  334.6 14.7 %slice-start.4 = ((s8[6291456]{0:T(1024)(128)(4,1)}), s8[4194304]{0:T(1024)(128)(4,1)S(1)}, s32[]{:S(2)}) async-start(s8[6291456]{0:T(1024)(128)(4,1)} %bitcast.110), calls=%async_computation.4 | async-start | bytes 8388608
  342.2 7.1 %slice-start.5 = ((s8[6291456]{0:T(1024)(128)(4,1)}), s8[2097152]{0:T(1024)(128)(4,1)S(1)}, s32[]{:S(2)}) async-start(s8[6291456]{0:T(1024)(128)(4,1)} %bitcast.110), calls=%async_computation.5 | async-start | bytes 4194304
  367.7 9.2 %slice-start = ((s8[6291456]{0:T(1024)(128)(4,1)}), s8[4194304]{0:T(1024)(128)(4,1)S(1)}, s32[]{:S(2)}) async-start(s8[6291456]{0:T(1024)(128)(4,1)} %bitcast.104), calls=%async_computation | async-start | bytes 8388608
  371.8 5.2 slice-start.1
  371.8 5.2 copy-start.30
  382.4 298.9 %collective-permute-start = (bf16[320,1024]{1,0:T(8,128)(2,1)}, bf16[320,1024]{1,0:T(8,128)(2,1)}, u32[]{:S(2)}, u32[]{:S(2)}) collective-permute-start(bf16[320,1024]{1,0:T(8,128)(2,1)} %get-tuple-element.99), channel_id=1, source_target_pairs={{0,4},{1,5},{2,6},{3,7},{4,0},{5,1},{6,2},{7,3},{8,12},{9,13},{10,... | collective-permute-start | bytes 1966088 | tf_op jit(solution)/shard_map/ppermute | solution.py:1324
  679.9 6.1 copy-start.28
  679.9 6.8 copy-start.27
  679.9 7.5 %copy-start.26 = (f32[32,3072]{1,0:T(8,128)S(1)}, f32[32,3072]{1,0:T(8,128)}, u32[]{:S(2)}) copy-start(f32[32,3072]{1,0:T(8,128)} %get-tuple-element.134) | copy-start | bytes 1179652
  681.3 6.8 copy-start.25
  681.3 7.6 %copy-start.1 = (s32[2,13]{1,0:T(2,128)S(1)}, s32[2,13]{1,0:T(2,128)}, u32[]{:S(2)}) copy-start(s32[2,13]{1,0:T(2,128)} %param.20) | copy-start | bytes 316
  (18 other events, 40.7 us)

commit v3 on v2

--- a/solution.py
+++ b/solution.py
@@ -21,6 +21,9 @@
 SUBS = 5
 CHUNK = 256
 GAIN_COLS = 128
+FF_CHUNK = 512
+FF_CHUNKS = FF // FF_CHUNK
+FF_EARLY = 4
 LOCAL_RUNS = 3
 MIB = 1024 * 1024
 
@@ -129,6 +132,30 @@
             device_id=target,
             device_id_type=MESH,
         )
+
+
+class Exchange:
+    def __init__(self, links, source, placed, local_sem):
+        self.links = links
+        self.source = source
+        self.placed = placed
+        self.local_sem = local_sem
+
+    def copies_(self):
+        _, _, z, _ = self.links.place()
+        half = z // (self.links.sizes[2] // 2)
+        return [
+            self.links.copy("swap", self.source.at[1 - half], self.placed.at[half], self.links.across()),
+            pltpu.make_async_copy(self.source.at[half], self.placed.at[half], self.local_sem),
+        ]
+
+    def start(self):
+        for copy in self.copies_():
+            copy.start()
+
+    def wait(self):
+        for copy in self.copies_():
+            copy.wait()
 
 
 class Gather:
@@ -258,7 +285,8 @@
 
     def begin(self):
         self.first().wait()
-        self.load().wait()
+        if self.temp_sem is not None:
+            self.load().wait()
         ny, nx, nz = self.links.sizes
 
         def add(i, carry):
@@ -331,6 +359,46 @@
 
 
 ORDERS = ("xy", "yx")
+
+FORWARD_START = [(0, 0), ("kv", 0), (1, 0), (0, 1), ("use", 0), (2, 0), (0, 2)]
+FORWARD_BEFORE = {
+    0: [("got", 0), ("kv", 1)],
+    2: [("use", 1), (0, 4), ("kv", 2), (3, 1), ("got", 1)],
+    4: [("use", 2), (0, 6), ("kv", 3), (2, 3), ("got", 2)],
+    6: [("use", 3), (1, 6), ("swap", 0), ("got", 3)],
+}
+FORWARD_AFTER = {
+    0: [(1, 1), (3, 0), (2, 1), (0, 3)],
+    1: [(1, 2), (2, 2)],
+    2: [(1, 3), (3, 2)],
+    3: [(0, 5), (1, 4)],
+    4: [(2, 4), (1, 5)],
+    5: [(3, 3), (2, 5)],
+    6: [(3, 4), (2, 6), (3, 5)],
+    7: [(3, 6)],
+}
+FEED_MIDDLE = {
+    1: [("begin", 0)],
+    2: [("begin", 1), (1, 0)],
+    3: [("begin", 2), (1, 1)],
+    4: [("begin", 3), (1, 2)],
+    5: [(1, 3)],
+}
+FEED_AFTER = {
+    0: [("core", 0)],
+    1: [("core", 1), (0, 0)],
+    2: [("core", 2), (0, 1)],
+    3: [("core", 3), (0, 2)],
+    4: [(0, 3)],
+}
+FEED_LAST = []
+BACKWARD_AFTER = {
+    0: [(0, 0)],
+    1: [(1, 0), (0, 1)],
+    2: [(2, 0), (1, 1), (0, 2)],
+    3: [(2, 1), (1, 2)],
+    4: [(2, 2)],
+}
 
 
 def halves_of(width):
@@ -636,25 +704,24 @@
             out[slot + k] = total
 
 
-def forward_kernel(sizes, rows, meta, q_ref, kv_ref, *refs):
-    shard = refs[:4]
-    mixed_ref, l_ref, kv_all = refs[4:7]
-    whole = refs[7:11]
-    kvs, acc, part, places, kp, vp, send_sem, recv_sem, local_sem = refs[11:]
+def forward_kernel(sizes, rows, meta, q_ref, kv_ref, cot_ref, out_shard, *refs):
+    shard = (out_shard,) + refs[:FF_CHUNKS]
+    mixed_ref, l_ref, kv_all, out_whole, feed_whole, cot_placed = refs[FF_CHUNKS : FF_CHUNKS + 6]
+    whole = (out_whole,) + tuple(feed_whole.at[c] for c in range(FF_CHUNKS))
+    kvs, acc, part, places, kp, vp, send_sem, recv_sem, local_sem = refs[FF_CHUNKS + 6 :]
     members = sizes[2]
     sub = rows // SUBS
     head = pl.program_id(0)
     links = Links(sizes, send_sem, recv_sem)
     kv = KeyValues(links, rows, kv_ref, kvs, local_sem)
-    weights_ = []
-    for a in range(4):
-        for b, cols in enumerate(halves_of(shard[a].shape[-1])):
-            weights_.append(
-                (a, Gather(links, (a, b), shard[a], whole[a], ORDERS[b], cols, local_sem.at[16 + 2 * a + b]))
-            )
-
-    def each(array):
-        return [g for a, g in weights_ if a == array]
+    swap = Exchange(links, cot_ref, cot_placed, local_sem.at[12 + 2 * (FF_CHUNKS + 1)])
+    weights_ = [
+        [
+            Gather(links, (a, b), shard[a], whole[a], ORDERS[b], cols, local_sem.at[12 + 2 * a + b])
+            for b, cols in enumerate(halves_of(shard[a].shape[-1]))
+        ]
+        for a in range(FF_CHUNKS + 1)
+    ]
 
     def kept(group):
         return pltpu.make_async_copy(
@@ -663,26 +730,36 @@
             local_sem.at[8 + group],
         )
 
+    def act(steps):
+        for what, a in steps:
+            if what == "swap":
+                swap.start()
+            elif what == "kv":
+                run_all(kv.across(a), "start")
+                run_all(kv.near(a), "start")
+            elif what == "use":
+                run_all(kv.across(a), "wait")
+                run_all(kv.forward(a), "start")
+            elif what == "got":
+                run_all(kv.near(a), "wait")
+                run_all(kv.forward(a), "wait")
+                kept(a).start()
+            else:
+                for g in weights_[a]:
+                    if what == 0:
+                        g.start()
+                    else:
+                        g.step(what)
+
     @pl.when(head == 0)
     def _():
         links.meet()
-        for group in range(4):
-            run_all(kv.across(group), "start")
-            run_all(kv.near(group), "start")
-            for g in each(group):
-                g.start()
+        act(FORWARD_START)
         l_ref[...] = jnp.zeros_like(l_ref)
         places[...] = row_places(places.shape, 0, sub)
 
-    for group in range(4):
-
-        @pl.when(head == 2 * group)
-        def _():
-            run_all(kv.across(group), "wait")
-            run_all(kv.forward(group), "start")
-            run_all(kv.near(group), "wait")
-            run_all(kv.forward(group), "wait")
-            kept(group).start()
+    for moment, steps in FORWARD_BEFORE.items():
+        pl.when(head == moment)(functools.partial(act, steps))
 
     _, _, z, core = links.place()
     mine = lax.rem(z, members // 2) * 2 + core
@@ -764,52 +841,46 @@
                 ]
         l_ref[region] = jnp.where(lane == head, total, l_ref[region])
 
-    plan = {
-        0: [(0, 1)],
-        1: [(1, 1)],
-        2: [(0, 2)],
-        3: [(2, 1)],
-        4: [(1, 2), (0, 3)],
-        5: [(3, 1)],
-        6: [(2, 2), (1, 3)],
-        7: [(3, 2), (2, 3), (3, 3)],
-    }
-    for at, steps in plan.items():
-
-        @pl.when(head == at)
-        def _():
-            for array, stage in steps:
-                for g in each(array):
-                    g.step(stage)
-            if at == KV_HEADS - 1:
-                for _, g in weights_:
-                    g.close()
-                for group in range(4):
-                    kept(group).wait()
-
-
-def forward(sizes, meta, queries, kv, shards_):
+    for moment, steps in FORWARD_AFTER.items():
+        pl.when(head == moment)(functools.partial(act, steps))
+
+    @pl.when(head == KV_HEADS - 1)
+    def _():
+        for pair in weights_:
+            for g in pair:
+                g.close()
+        for group in range(4):
+            kept(group).wait()
+        swap.wait()
+
+
+def forward(sizes, meta, queries, kv, cotangent, out_shard, feed_shards):
     ny, nx, nz = sizes
     rows = kv.shape[3]
-    rounds = KeyValues.copies(sizes) + 8 * Gather.copies(sizes)
+    count = 1 + FF_CHUNKS
+    rounds = KeyValues.copies(sizes) + 2 * count * Gather.copies(sizes) + 1
     results = pl.pallas_call(
         functools.partial(forward_kernel, sizes, rows),
         out_shape=[
             jax.ShapeDtypeStruct((2 * rows, QD), BF16),
             jax.ShapeDtypeStruct((4 * rows, HEAD_DIM), F32),
             jax.ShapeDtypeStruct((2, KV_HEADS, TREE, HEAD_DIM), BF16),
-        ]
-        + [jax.ShapeDtypeStruct((ny, nx, nz, 2) + s.shape, BF16) for s in shards_],
+            jax.ShapeDtypeStruct((ny, nx, nz, 2) + out_shard.shape, BF16),
+            jax.ShapeDtypeStruct((FF_CHUNKS, ny, nx, nz, 2) + feed_shards[0].shape, BF16),
+            jax.ShapeDtypeStruct(cotangent.shape, BF16),
+        ],
         grid_spec=pltpu.PrefetchScalarGridSpec(
             num_scalar_prefetch=1,
             grid=(KV_HEADS,),
-            in_specs=[pl.BlockSpec((1, 4 * rows, HEAD_DIM), lambda h, meta: (h, 0, 0)), ANY] + [ANY] * 4,
+            in_specs=[pl.BlockSpec((1, 4 * rows, HEAD_DIM), lambda h, meta: (h, 0, 0)), ANY, ANY] + [ANY] * count,
             out_specs=[
                 pl.BlockSpec((2 * rows, 2 * HEAD_DIM), lambda h, meta: (0, h)),
                 pl.BlockSpec((4 * rows, HEAD_DIM), lambda h, meta: (0, 0)),
                 ANY,
-            ]
-            + [ANY] * 4,
+                ANY,
+                ANY,
+                ANY,
+            ],
             scratch_shapes=[
                 pltpu.VMEM((2, KV_HEADS, TREE, HEAD_DIM), BF16),
                 pltpu.VMEM((2 * rows, HEAD_DIM), F32),
@@ -819,23 +890,263 @@
                 pltpu.VMEM((LOCAL_RUNS, SEG, HEAD_DIM), BF16),
                 pltpu.SemaphoreType.DMA((rounds,)),
                 pltpu.SemaphoreType.DMA((rounds,)),
-                pltpu.SemaphoreType.DMA((24,)),
+                pltpu.SemaphoreType.DMA((13 + 2 * count,)),
             ],
         ),
         compiler_params=pltpu.CompilerParams(
             collective_id=2, has_side_effects=True, vmem_limit_bytes=48 * MIB
         ),
         name="forward",
-    )(meta, queries, kv, *shards_)
-    return results[:3], [w.reshape(D, -1) for w in results[3:]]
-
-
-def backward_kernel(sizes, rows, shard_rows, widths, meta, q_ref, g_ref, k_ref, v_ref, lse_ref, del_ref, *refs):
-    parts = refs[:4]
-    dq_ref, dkv_ref = refs[4:6]
-    outs = refs[6:10]
-    dq, dk, dv, pk, pv, kp, vp, stage, near, sums, far, last, temp = refs[10:23]
-    buffers = refs[23:-3]
+    )(meta, queries, kv, cotangent, out_shard, *feed_shards)
+    mixed, totals, kv_all, out_whole, feed_whole, cot = results
+    return mixed, totals, kv_all, out_whole.reshape(D, QD), feed_whole.reshape(FF_CHUNKS, D, -1), cot
+
+
+def feed_kernel(
+    sizes, rows, x_ref, mixed_ref, cot_ref, out_ref, gain_ref, w_ref,
+    result_ref, hid_ref, stack_ref, delta_ref, post_ref, dout_ref, late_ref, early_ref, *refs,
+):
+    hidden, second, second_t, cot_t, total, grads, inner, gate_up, low, stack, part = refs[:11]
+    buffers = refs[11:-3]
+    send_sem, recv_sem, local_sem = refs[-3:]
+    ny, nx, nz = sizes
+    count = 2 * rows
+    sub = rows // SUBS
+    shard_rows = part.shape[5]
+    width = 3 * FF_CHUNK
+    tile = 256
+    chunk = pl.program_id(0)
+    links = Links(sizes, send_sem, recv_sem)
+    _, _, _, core = links.place()
+    scatters = []
+    for c in range(FF_EARLY):
+        for b, cols in enumerate(halves_of(width)):
+            k = 4 * len(scatters)
+            scatters.append(
+                Scatter(
+                    links,
+                    (c, b),
+                    part.at[c % 2],
+                    ORDERS[b],
+                    cols,
+                    *buffers[k : k + 4],
+                    part.at[c % 2, :, :, :, core, :, cols],
+                    None,
+                    early_ref.at[c],
+                )
+            )
+
+    def act(steps):
+        for what, c in steps:
+            for s in scatters[2 * c : 2 * c + 2]:
+                if what == "core":
+                    s.start()
+                elif what == "begin":
+                    s.begin()
+                elif what == "finish":
+                    s.finish()
+                else:
+                    s.middle(what)
+
+    def rows_of(block):
+        return (block // (2 * nz * nx), lax.rem(block // (2 * nz), nx), lax.rem(block // 2, nz), lax.rem(block, 2))
+
+    def put(slot, first, cols, value):
+        for k in range(value.shape[0] // shard_rows):
+            y, x, z, c = rows_of(first // shard_rows + k)
+            part[slot, y, x, z, c, :, cols] = value[k * shard_rows : (k + 1) * shard_rows].astype(BF16)
+
+    def late(c):
+        return pltpu.make_async_copy(part.at[c % 2], late_ref.at[c - FF_EARLY], local_sem.at[c % 2])
+
+    @pl.when(chunk == 0)
+    def _():
+        links.meet()
+
+        def project_out(t, carry):
+            at = pl.multiple_of(t * tile, tile)
+            hidden[:, pl.ds(at, tile)] = x_ref[:, pl.ds(at, tile)].astype(F32) + nt(
+                mixed_ref[...], out_ref[pl.ds(at, tile), :]
+            )
+            return carry
+
+        lax.fori_loop(0, D // tile, project_out, 0)
+        values = hidden[...]
+        values = values * norm_factor(values) * gain_ref[...]
+        second[...] = values.astype(BF16)
+        second_t[...] = values.T.astype(BF16)
+        cot_t[...] = cot_ref[...].astype(F32).T.astype(BF16)
+        total[...] = jnp.zeros_like(total)
+        grads[...] = jnp.zeros_like(grads)
+
+    slot = lax.rem(chunk, 2)
+
+    def columns(t, carry):
+        at = pl.multiple_of(t * tile, tile)
+        gate = matmul(second[...], w_ref[0, :, pl.ds(at, tile)])
+        up = matmul(second[...], w_ref[0, :, pl.ds(FF_CHUNK + at, tile)])
+        grad = matmul(cot_ref[...], w_ref[0, :, pl.ds(2 * FF_CHUNK + at, tile)])
+        sigmoid = 1.0 / (1.0 + jnp.exp(-gate))
+        active = gate * sigmoid
+        inner[:, pl.ds(at, tile)] = (active * up).astype(BF16)
+        gate_up[:, pl.ds(at, tile)] = (grad * up * sigmoid * (1.0 + gate * (1.0 - sigmoid))).astype(BF16)
+        gate_up[:, pl.ds(FF_CHUNK + at, tile)] = (grad * active).astype(BF16)
+        return carry
+
+    lax.fori_loop(0, FF_CHUNK // tile, columns, 0)
+    for moment, steps in FEED_MIDDLE.items():
+        pl.when(chunk == moment)(functools.partial(act, steps))
+    for c in range(FF_EARLY, FF_CHUNKS - 2):
+        pl.when(chunk == c + 2)(lambda: late(c).wait())
+
+    def model(t, carry):
+        at = pl.multiple_of(t * tile, tile)
+        total[:, pl.ds(at, tile)] += nt(inner[...], w_ref[0, pl.ds(at, tile), 2 * FF_CHUNK :])
+        grads[:, pl.ds(at, tile)] += nt(gate_up[...], w_ref[0, pl.ds(at, tile), : 2 * FF_CHUNK])
+        put(slot, at, slice(0, 2 * FF_CHUNK), matmul(second_t[pl.ds(at, tile)], gate_up[...]))
+        put(slot, at, slice(2 * FF_CHUNK, width), matmul(cot_t[pl.ds(at, tile)], inner[...]))
+        return carry
+
+    lax.fori_loop(0, D // tile, model, 0)
+    for c in range(FF_EARLY, FF_CHUNKS):
+        pl.when(chunk == c)(lambda: late(c).start())
+    for moment, steps in FEED_AFTER.items():
+        pl.when(chunk == moment)(functools.partial(act, steps))
+
+    @pl.when(chunk == FF_CHUNKS - 1)
+    def _():
+        values = hidden[...]
+        low[...] = (values + total[...]).astype(BF16)
+        output = pltpu.make_async_copy(low, result_ref, local_sem.at[2])
+        output.start()
+        factor = norm_factor(values)
+        grad_in, share = norm_backward(grads[...], gain_ref[...], values * factor, factor)
+        post_ref[...] = jnp.sum(share, axis=0, keepdims=True)
+        hidden[...] = cot_ref[...].astype(F32) + grad_in
+        saved = pltpu.make_async_copy(hidden, hid_ref, local_sem.at[3])
+        saved.start()
+        second[...] = hidden[...].astype(BF16)
+        second_t[...] = hidden[...].T.astype(BF16)
+        lane = lax.broadcasted_iota(jnp.int32, (count, HEAD_DIM), 1)
+        dots = jnp.zeros((count, HEAD_DIM), F32)
+        for h in range(KV_HEADS):
+            cols = slice(2 * h * HEAD_DIM, 2 * (h + 1) * HEAD_DIM)
+            grad = matmul(second[...], out_ref[:, cols]).astype(BF16)
+            for g in range(2):
+                one = grad[:, g * HEAD_DIM : (g + 1) * HEAD_DIM]
+                for s in range(2 * SUBS):
+                    stack[h, (2 * s + g) * sub : (2 * s + g + 1) * sub] = one[s * sub : (s + 1) * sub]
+                head = 2 * h + g
+                product = one.astype(F32) * mixed_ref[:, head * HEAD_DIM : (head + 1) * HEAD_DIM].astype(F32)
+                dots = jnp.where(lane == head, jnp.sum(product, axis=-1, keepdims=True), dots)
+        delta_ref[...] = dots.T
+        stacked_ = pltpu.make_async_copy(stack, stack_ref, local_sem.at[4])
+        stacked_.start()
+        act(FEED_LAST)
+        for c in range(FF_CHUNKS - 2, FF_CHUNKS):
+            late(c).wait()
+
+        def model_out(t, carry):
+            at = pl.multiple_of(t * tile, tile)
+            for a in range(0, QD, 2 * FF_CHUNK):
+                cols = slice(a, a + 2 * FF_CHUNK)
+                value = matmul(second_t[pl.ds(at, tile)], mixed_ref[:, cols])
+                slot = a // (2 * FF_CHUNK)
+                put(slot, at, slice(0, 2 * FF_CHUNK), value)
+            return carry
+
+        lax.fori_loop(0, D // tile, model_out, 0)
+        gone = [
+            pltpu.make_async_copy(
+                part.at[k, :, :, :, :, :, : 2 * FF_CHUNK],
+                dout_ref.at[:, :, :, :, :, 2 * FF_CHUNK * k : 2 * FF_CHUNK * (k + 1)],
+                local_sem.at[k],
+            )
+            for k in range(2)
+        ]
+        run_all(gone, "start")
+        for c in range(FF_EARLY):
+            act([("finish", c)])
+        run_all(gone + [output, saved, stacked_], "wait")
+
+
+def feed(sizes, x, mixed, cot, out_t, gain, feed_whole):
+    ny, nx, nz = sizes
+    count = x.shape[0]
+    rows = count // 2
+    shard_rows = D // (ny * nx * nz * 2)
+    width = 3 * FF_CHUNK
+    buffers = []
+    for c in range(FF_EARLY):
+        for b, cols in enumerate(halves_of(width)):
+            buffers += Scatter.scratch(sizes, ORDERS[b], shard_rows, cols.stop - cols.start)
+    rounds = 2 * FF_EARLY * Scatter.copies(sizes)
+
+    def whole_block(shape):
+        return pl.BlockSpec(shape, lambda c: (0,) * len(shape), pipeline_mode=pl.Buffered(1))
+
+    blocks = (ny, nx, nz, 2, shard_rows)
+    return pl.pallas_call(
+        functools.partial(feed_kernel, sizes, rows),
+        grid=(FF_CHUNKS,),
+        out_shape=[
+            jax.ShapeDtypeStruct((count, D), BF16),
+            jax.ShapeDtypeStruct((count, D), F32),
+            jax.ShapeDtypeStruct((KV_HEADS, 2 * count, HEAD_DIM), BF16),
+            jax.ShapeDtypeStruct((HEAD_DIM, count), F32),
+            jax.ShapeDtypeStruct((1, D), F32),
+            jax.ShapeDtypeStruct(blocks + (QD,), BF16),
+            jax.ShapeDtypeStruct((FF_CHUNKS - FF_EARLY,) + blocks + (width,), BF16),
+            jax.ShapeDtypeStruct((FF_EARLY, shard_rows, width), F32),
+        ],
+        in_specs=[
+            whole_block((count, D)),
+            whole_block((count, QD)),
+            whole_block((count, D)),
+            whole_block((D, QD)),
+            whole_block((1, D)),
+            pl.BlockSpec((1, D, width), lambda c: (c, 0, 0)),
+        ],
+        out_specs=[
+            ANY,
+            ANY,
+            ANY,
+            pl.BlockSpec((HEAD_DIM, count), lambda c: (0, 0)),
+            pl.BlockSpec((1, D), lambda c: (0, 0)),
+            ANY,
+            ANY,
+            pl.BlockSpec((FF_EARLY, shard_rows, width), lambda c: (0, 0, 0)),
+        ],
+        scratch_shapes=[
+            pltpu.VMEM((count, D), F32),
+            pltpu.VMEM((count, D), BF16),
+            pltpu.VMEM((D, count), BF16),
+            pltpu.VMEM((D, count), BF16),
+            pltpu.VMEM((count, D), F32),
+            pltpu.VMEM((count, D), F32),
+            pltpu.VMEM((count, FF_CHUNK), BF16),
+            pltpu.VMEM((count, 2 * FF_CHUNK), BF16),
+            pltpu.VMEM((count, D), BF16),
+            pltpu.VMEM((KV_HEADS, 2 * count, HEAD_DIM), BF16),
+            pltpu.VMEM((2,) + blocks + (width,), BF16),
+        ]
+        + buffers
+        + [
+            pltpu.SemaphoreType.DMA((rounds,)),
+            pltpu.SemaphoreType.DMA((rounds,)),
+            pltpu.SemaphoreType.DMA((5,)),
+        ],
+        compiler_params=pltpu.CompilerParams(
+            collective_id=5, has_side_effects=True, vmem_limit_bytes=61 * MIB
+        ),
+        name="feed",
+    )(x, mixed, cot, out_t, gain, feed_whole)
+
+
+def backward_kernel(sizes, rows, widths, meta, q_ref, g_ref, k_ref, v_ref, lse_ref, del_ref, late_ref, dout_ref, done_ref, *refs):
+    dq_ref, dkv_ref, late_out, dout_out, done_placed = refs[:5]
+    dq, dk, dv, pk, pv, kp, vp, stage, near, sums, far, last = refs[5:17]
+    buffers = refs[17:-3]
     send_sem, recv_sem, local_sem = refs[-3:]
     members = sizes[2]
     chips = members // 2
@@ -843,37 +1154,36 @@
     head = pl.program_id(0)
     links = Links(sizes, send_sem, recv_sem)
     scatters = []
-    for a in range(4):
-        for b, cols in enumerate(halves_of(widths[a])):
-            k = 4 * len(scatters)
-            width = cols.stop - cols.start
+    late = FF_CHUNKS - FF_EARLY
+    for a, width in enumerate(widths):
+        for b, cols in enumerate(halves_of(width)):
+            k = 5 * len(scatters)
             scatters.append(
-                (
-                    a,
-                    Scatter(
-                        links,
-                        (a, b),
-                        parts[a],
-                        ORDERS[b],
-                        cols,
-                        *buffers[k : k + 4],
-                        temp.at[b, :, :, :, :, :width],
-                        local_sem.at[b],
-                        outs[a],
-                    ),
+                Scatter(
+                    links,
+                    (a, b),
+                    late_ref.at[a] if a < late else dout_ref,
+                    ORDERS[b],
+                    cols,
+                    *buffers[k : k + 5],
+                    local_sem.at[2 + len(scatters)],
+                    late_out.at[a] if a < late else dout_out,
                 )
             )
 
+    swap = Exchange(links, done_ref, done_placed, local_sem.at[2 + len(scatters)])
+
     def each(array):
-        return [s for a, s in scatters if a == array]
+        return scatters[2 * array : 2 * array + 2]
 
     @pl.when(head == 0)
     def _():
+        for s in scatters:
+            s.load().start()
         links.meet()
-        for s in each(0):
-            s.load().start()
-        for _, s in scatters:
+        for s in scatters:
             s.start()
+        swap.start()
 
     _, _, z, core = links.place()
     here = lax.rem(z, chips)
@@ -952,21 +1262,24 @@
                 flag = jnp.minimum(meta[run] + 1, 1).astype(F32)
 
                 def mask(weights):
-                    shape = weights.shape
+                    shape = (SEG, 2 * sub)
                     room = lax.broadcasted_iota(jnp.int32, shape, 1) % sub + lax.rem(row, SEG)
-                    return jnp.where(lax.broadcasted_iota(jnp.int32, shape, 0) <= room, weights, 0.0)
+                    seen = lax.broadcasted_iota(jnp.int32, shape, 0) <= room
+                    return jnp.concatenate(
+                        [jnp.where(seen, weights[:SEG], 0.0), weights[SEG:] * flag], axis=0
+                    )
 
                 key_grad, value_grad = pair(
-                    k_ref[0, 0, pl.ds(own, SEG)], v_ref[0, 0, pl.ds(own, SEG)], block, mask
+                    jnp.concatenate([k_ref[0, 0, pl.ds(own, SEG)], kp[run - lead]], axis=0),
+                    jnp.concatenate([v_ref[0, 0, pl.ds(own, SEG)], vp[run - lead]], axis=0),
+                    block,
+                    mask,
                 )
-                dk[pl.ds(own, SEG)] += key_grad
-                dv[pl.ds(own, SEG)] += value_grad
-                key_grad, value_grad = pair(
-                    kp[run - lead], vp[run - lead], block, lambda weights: weights * flag
-                )
+                dk[pl.ds(own, SEG)] += key_grad[:SEG]
+                dv[pl.ds(own, SEG)] += value_grad[:SEG]
                 slot = LOCAL_RUNS * piece + run - lead
-                pk[slot] += key_grad
-                pv[slot] += value_grad
+                pk[slot] += key_grad[SEG:]
+                pv[slot] += value_grad[SEG:]
 
             if piece == 0:
                 pl.when(base + s * sub >= TRUNK)(runs)
@@ -1034,74 +1347,67 @@
         def _():
             core_copy(h).start()
 
-    plan = {
-        0: [(0, 0)],
-        1: [(1, 0)],
-        2: [(0, 1)],
-        3: [(2, 0), (0, 2)],
-        4: [(1, 1)],
-        5: [(3, 0), (1, 2)],
-        6: [(2, 1)],
-        7: [(3, 1), (2, 2), (3, 2)],
-    }
-    for moment, steps in plan.items():
+    for moment, steps in BACKWARD_AFTER.items():
 
         @pl.when(head == moment)
         def _():
-            if moment == KV_HEADS - 1:
-                pass_on(moment)
-            for array, step in steps:
+            for step, array in steps:
                 for s in each(array):
                     if step == 0:
                         s.begin()
                     else:
                         s.middle(step - 1)
-                if step == 0 and array < 3:
-                    for s in each(array + 1):
-                        s.load().start()
-
-            def result(h):
-                return pltpu.make_async_copy(last.at[h % 2], dkv_ref.at[:, h], local_sem.at[2 + h % 2])
-
-            if moment == KV_HEADS - 1:
-                for h in range(KV_HEADS):
-                    run_all(far_copies(h), "wait")
-                    if h > 1:
-                        result(h - 2).wait()
-                    for which in range(2):
-                        for piece in range(2):
-                            total = sums[h, here, which, piece].astype(F32)
-                            for i in range(chips - 1):
-                                total = total + far[h, i, which, piece].astype(F32)
-                            last[h % 2, which, piece] = total
-                    result(h).start()
-                for _, s in scatters:
-                    s.finish()
-                for h in (KV_HEADS - 2, KV_HEADS - 1):
-                    result(h).wait()
-
-
-def backward(sizes, meta, queries, grads, kv_all, log_total, delta, parts):
+
+    def result(h):
+        return pltpu.make_async_copy(last.at[h % 2], dkv_ref.at[:, h], local_sem.at[h % 2])
+
+    @pl.when(head == KV_HEADS - 1)
+    def _():
+        pass_on(KV_HEADS - 1)
+        for s in scatters:
+            s.finish()
+        for h in range(KV_HEADS):
+            run_all(far_copies(h), "wait")
+            if h > 1:
+                result(h - 2).wait()
+            for which in range(2):
+                for piece in range(2):
+                    total = sums[h, here, which, piece].astype(F32)
+                    for i in range(chips - 1):
+                        total = total + far[h, i, which, piece].astype(F32)
+                    last[h % 2, which, piece] = total
+            result(h).start()
+        for h in (KV_HEADS - 2, KV_HEADS - 1):
+            result(h).wait()
+        swap.wait()
+
+
+def backward(sizes, meta, queries, grads, kv_all, log_total, delta, late, dout, done):
     ny, nx, nz = sizes
     chips = nz // 2
     rows = queries.shape[1] // 4
-    widths = tuple(p.shape[-1] for p in parts)
-    shard_rows = D // (ny * nx * nz * 2)
-    pieces = [p.reshape(ny, nx, nz, 2, shard_rows, p.shape[-1]) for p in parts]
+    widths = (late.shape[-1],) * late.shape[0] + (dout.shape[-1],)
+    shard_rows = dout.shape[4]
     stack = pl.BlockSpec((1, 4 * rows, HEAD_DIM), lambda h, meta: (h, 0, 0))
     line = pl.BlockSpec((1, 1, 4 * rows), lambda h, meta: (h, 0, 0))
-    buffers = []
+    buffers, count = [], 0
     for w in widths:
         for b, cols in enumerate(halves_of(w)):
             buffers += Scatter.scratch(sizes, ORDERS[b], shard_rows, cols.stop - cols.start)
-    rounds = 8 * Scatter.copies(sizes) + KV_HEADS * chips
-    results = pl.pallas_call(
-        functools.partial(backward_kernel, sizes, rows, shard_rows, widths),
+            buffers.append(pltpu.VMEM((ny, nx, nz, shard_rows, cols.stop - cols.start), BF16))
+            count += 1
+    rounds = count * Scatter.copies(sizes) + KV_HEADS * chips + 1
+    late_shape = (late.shape[0], shard_rows, late.shape[-1])
+    dout_shape = (shard_rows, dout.shape[-1])
+    return pl.pallas_call(
+        functools.partial(backward_kernel, sizes, rows, widths),
         out_shape=[
             jax.ShapeDtypeStruct((KV_HEADS, 4 * rows, HEAD_DIM), F32),
             jax.ShapeDtypeStruct((2, KV_HEADS, 2, rows, HEAD_DIM), F32),
-        ]
-        + [jax.ShapeDtypeStruct((shard_rows, w), F32) for w in widths],
+            jax.ShapeDtypeStruct(late_shape, F32),
+            jax.ShapeDtypeStruct(dout_shape, F32),
+            jax.ShapeDtypeStruct(done.shape, BF16),
+        ],
         grid_spec=pltpu.PrefetchScalarGridSpec(
             num_scalar_prefetch=1,
             grid=(KV_HEADS,),
@@ -1112,9 +1418,17 @@
                 pl.BlockSpec((1, 1, TREE, HEAD_DIM), lambda h, meta: (1, h, 0, 0)),
                 line,
                 line,
-            ]
-            + [ANY] * 4,
-            out_specs=[stack, ANY] + [pl.BlockSpec((shard_rows, w), lambda h, meta: (0, 0)) for w in widths],
+                ANY,
+                ANY,
+                ANY,
+            ],
+            out_specs=[
+                stack,
+                ANY,
+                pl.BlockSpec(late_shape, lambda h, meta: (0, 0, 0)),
+                pl.BlockSpec(dout_shape, lambda h, meta: (0, 0)),
+                ANY,
+            ],
             scratch_shapes=[
                 pltpu.VMEM((2 * rows, HEAD_DIM), F32),
                 pltpu.VMEM((TREE, HEAD_DIM), F32),
@@ -1128,17 +1442,16 @@
                 pltpu.VMEM((KV_HEADS, chips, 2, 2, rows, HEAD_DIM), BF16),
                 pltpu.VMEM((KV_HEADS, chips - 1, 2, 2, rows, HEAD_DIM), BF16),
                 pltpu.VMEM((2, 2, 2, rows, HEAD_DIM), F32),
-                pltpu.VMEM((2, ny, nx, nz, shard_rows, max(widths) // 2), BF16),
             ]
             + buffers
             + [
                 pltpu.SemaphoreType.DMA((rounds,)),
                 pltpu.SemaphoreType.DMA((rounds,)),
-                pltpu.SemaphoreType.DMA((4,)),
+                pltpu.SemaphoreType.DMA((3 + count,)),
             ],
         ),
         compiler_params=pltpu.CompilerParams(
-            collective_id=3, has_side_effects=True, vmem_limit_bytes=61 * MIB
+            collective_id=3, has_side_effects=True, vmem_limit_bytes=60 * MIB
         ),
         name="backward",
     )(
@@ -1149,9 +1462,10 @@
         kv_all,
         log_total.reshape(KV_HEADS, 1, 4 * rows),
         delta.reshape(KV_HEADS, 1, 4 * rows),
-        *pieces,
+        late,
+        dout,
+        done,
     )
-    return results[0], results[1], results[2:]
 
 
 def scatter_kernel(sizes, widths, *refs):
@@ -1268,7 +1582,6 @@
     member = ctx % nz
     count = 2 * rows
     sub = rows // SUBS
-    swap = [(i, (i + nz) % (2 * nz)) for i in range(2 * nz)]
 
     def column(gain):
         return jnp.pad(gain, (0, shard_rows - gain.shape[0]))[:, None]
@@ -1283,7 +1596,7 @@
 
     gain_block = kv_full[:, 2 * KVD :].astype(F32)
     in_weight = gain_block[:, 0][None, :]
-    post_weight = gain_block[:, 1]
+    post_weight = gain_block[:, 1][None, :]
     by_device = gain_block.reshape(-1, shard_rows, GAIN_COLS)
     query_weight = by_device[:, :gain_rows, 2].reshape(1, HEAD_DIM)
     key_weight = by_device[:, :gain_rows, 3].reshape(1, HEAD_DIM)
@@ -1299,59 +1612,30 @@
     normed, queries, kv, pre = project(
         x, in_weight, query_full, kv_full, query_weight, key_weight, cosine, sine
     )
-    (mixed, totals, kv_all), (out_t, gate_full, up_full, down_t) = forward(
-        sizes, meta, queries, kv, [out_proj.T, gate_proj, up_proj, down_proj.T]
+    down_t = down_proj.T
+    feed_shards = [
+        jnp.concatenate(
+            [w[:, c * FF_CHUNK : (c + 1) * FF_CHUNK] for w in (gate_proj, up_proj, down_t)], axis=1
+        )
+        for c in range(FF_CHUNKS)
+    ]
+    mixed, totals, kv_all, out_t, feed_whole, cot = forward(
+        sizes, meta, queries, kv, cotangent, out_proj.T, feed_shards
     )
     log_total = jnp.log2(totals[:, :KV_HEADS]).T
-
-    mixed, cotangent = lax.optimization_barrier((mixed, cotangent))
-    cot_keep = cotangent[half]
-    cot_got = lax.ppermute(cotangent[1 - half], "ctx", swap)
-    grad_out = jnp.where(
-        half == 0, jnp.concatenate([cot_keep, cot_got]), jnp.concatenate([cot_got, cot_keep])
+    cot = cot.reshape(count, D)
+    result, grad_hidden, grad_stack, delta, post_part, dout, late, early_grad = feed(
+        sizes, x, mixed, cot, out_t, post_weight, feed_whole
     )
-
-    hidden = x.astype(F32) + nt(mixed, out_t)
-    post_factor = norm_factor(hidden)
-    post_hat = hidden * post_factor
-    second = (post_hat * post_weight).astype(BF16)
-    gate_pre = matmul(second, gate_full)
-    up_pre = matmul(second, up_full)
-    activated = jax.nn.silu(gate_pre)
-    inner = (activated * up_pre).astype(BF16)
-    result = (hidden + nt(inner, down_t)).astype(BF16).reshape(2, rows, D)
-    result_keep = result[half]
-    result_got = lax.ppermute(result[1 - half], "ctx", swap)
-    output = jnp.where(
-        half == 0, jnp.stack([result_keep, result_got]), jnp.stack([result_got, result_keep])
+    delta = delta[:HEADS].reshape(KV_HEADS, 2, 2 * SUBS, sub).transpose(0, 2, 1, 3)
+    dq, dkv, late_grad, out_grad, output = backward(
+        sizes, meta, queries, grad_stack, kv_all, log_total, delta, late, dout, result.reshape(2, rows, D)
     )
-
-    grad_inner = matmul(grad_out, down_t)
-    sigmoid_gate = jax.nn.sigmoid(gate_pre)
-    grad_gate = (
-        grad_inner * up_pre * sigmoid_gate * (1.0 + gate_pre * (1.0 - sigmoid_gate))
-    ).astype(BF16)
-    grad_up = (grad_inner * activated).astype(BF16)
-    grad_second = nt(grad_gate, gate_full) + nt(grad_up, up_full)
-    grad_post_in, post_part = norm_backward(grad_second, post_weight, post_hat, post_factor)
-    grad_hidden = grad_out.astype(F32) + grad_post_in
-    grad_branch = grad_hidden.astype(BF16)
-    grad_mixed = matmul(grad_branch, out_t).astype(BF16)
-    parts = [
-        contract_rows(grad_branch, mixed).astype(BF16),
-        contract_rows(second, grad_gate).astype(BF16),
-        contract_rows(second, grad_up).astype(BF16),
-        contract_rows(grad_out, inner).astype(BF16),
-    ]
-    delta = jnp.sum(
-        (grad_mixed.astype(F32) * mixed.astype(F32)).reshape(count, HEADS, HEAD_DIM), axis=-1
-    )
-    delta = delta.reshape(2, SUBS, sub, KV_HEADS, 2).transpose(3, 0, 1, 4, 2)
-    grad_stack = grad_mixed.reshape(2 * SUBS, sub, KV_HEADS, 2, HEAD_DIM).transpose(2, 0, 3, 1, 4)
-    grad_stack = grad_stack.reshape(KV_HEADS, 2 * count, HEAD_DIM)
-    dq, dkv, (out_grad, gate_grad, up_grad, down_grad) = backward(
-        sizes, meta, queries, grad_stack, kv_all, log_total, delta, parts
-    )
+    feed_grad = jnp.concatenate([early_grad, late_grad], axis=0)
+
+    def feed_columns(k):
+        piece = feed_grad[:, :, k * FF_CHUNK : (k + 1) * FF_CHUNK]
+        return piece.transpose(1, 0, 2).reshape(shard_rows, FF)
 
     dwq, dwk, dwv, dx, in_part, qk_part = project_back(
         dq, dkv, pre, normed, x, grad_hidden, in_weight, query_full, kv_full, query_weight, key_weight, cosine, sine
@@ -1366,7 +1650,7 @@
     gain_parts = jnp.concatenate(
         [
             gain_column(in_part[0]),
-            gain_column(jnp.sum(post_part, axis=0)),
+            gain_column(post_part[0]),
             gain_column(qk_part[0]),
             gain_column(qk_part[1]),
         ],
@@ -1387,9 +1671,9 @@
         gain_grad[:gain_rows, 3],
         out_grad.T,
         gain_grad[:, 1],
-        gate_grad,
-        up_grad,
-        down_grad.T,
+        feed_columns(0),
+        feed_columns(1),
+        feed_columns(2).T,
     )
 
 

time: 698 us -> 625 us (0.90)
  matrix products: 84.6 us -> 0 us
  Pallas kernels: 529 us -> 575 us
  local copies, waits for them, and re-layouts: 44 us -> 30.7 us
  other arithmetic: 21.1 us -> 8.2 us
  waiting for transfers between devices: 9.18 us -> 0 us
    dot_general x12 -> x0, matrix products: 84.6 us -> none  [the longest x4 32.6 us: matmul(): return jnp.dot(left_side, right_side, preferred_element_type=F32)]
    pallas_call x1 -> x2, Pallas kernels: 157 us -> 224 us  [the longest x1 120 us: backward(): pl.pallas_call(functools.partial(backward_kernel, sizes, rows, widths), o...]
    pallas_call x1, Pallas kernels: 169 us -> 151 us  [forward(): pl.pallas_call(functools.partial(forward_kernel, sizes, rows), out_shape=...]
    ppermute x2 -> x0, waiting for transfers between devices: 9.18 us -> none  [the longest x1 9.18 us: shards(): cot_got = lax.ppermute(cotangent[1 - half], 'ctx', swap)]
    unnamed x89 -> x48, local copies, waits for them, and re-layouts: 24.6 us -> 17.4 us
  transfers between devices with their start and end apart: 2 -> 0, of which waited for: 1 -> 0; matrix products, arithmetic and copies ran while one was open for 7% -> 0% of each run, Pallas kernels for 39% -> 0%
where the time goes in v3:
time: 625 us; the launch traced here: 616 us
  Pallas kernels  575 us (92%)
  local copies, waits for them, and re-layouts  30.7 us (5%)
  other arithmetic  8.2 us (1%)
    pallas_call x1, Pallas kernels, forward(): pl.pallas_call(functools.partial(forward_kernel, sizes, rows), out_shape=...  151 us
    pallas_call x1, Pallas kernels, backward(): pl.pallas_call(functools.partial(backward_kernel, sizes, rows, widths), o...  120 us
    pallas_call x1, Pallas kernels, feed(): pl.pallas_call(functools.partial(feed_kernel, sizes, rows), grid=(FF_CHUN...  103 us
    pallas_call x1, Pallas kernels, scatter_end(): pl.pallas_call(functools.partial(scatter_kernel, sizes, widths), out_shap...  70.2 us
    pallas_call x1, Pallas kernels, gather_start(): pl.pallas_call(functools.partial(gather_kernel, sizes), out_shape=[jax.Sh...  68.9 us
    pallas_call x1, Pallas kernels, project_back(): pl.pallas_call(functools.partial(project_back_kernel, rows), grid=(KV_HEA...  39.1 us
    pallas_call x1, Pallas kernels, project(): pl.pallas_call(functools.partial(project_kernel, rows), grid=(KV_HEADS,),...  22.6 us
    unnamed x48, local copies, waits for them, and re-layouts  17.4 us

profile of v3, /device:TPU:0, one launch (start us, length us, event | category | flops | bytes accessed | tf_op | source)
XLA Modules:
  0.0 615.7 jit_solution(2121379204551406146)
XLA Ops:
  5.3 1.5 fusion.1.kv_ref
  7.7 0.9 fusion.7
  8.6 0.9 fusion.8
  9.5 1.2 fusion.2
  11.0 68.9 %gather_start.1 = (bf16[2,2,4,2,32,2048]{5,4,3,2,1,0:T(8,128)(2,1)}, bf16[2,2,4,2,32,2176]{5,4,3,2,1,0:T(8,128)(2,1)}, bf16[2,320,1024]{2,1,0:T(8,128)(2,1)}) custom-call(bf16[32,2048]{1,0:T(8,128)(2,1)} %query_ref.1, bf16[32,2176]{1,0:T(8,128)(2,1)} %fusion.1.kv_ref, bf16[2,320,1024]{2,1,0:T(8,128)(2,1)} %moved_ref.1), custom_call_target="tpu_custom_call" | custom-call | tf_op jit(solution)/shard_map/gather_start/pallas_call | solution.py:449
  80.0 1.1 slice_convert_fusion
  81.1 1.0 slice_reduce_fusion
  82.5 2.2 copy-done.2
  84.7 22.6 %project.1 = (bf16[640,1024]{1,0:T(8,128)(2,1)S(1)}, bf16[8,1280,128]{2,1,0:T(8,128)(2,1)S(1)}, bf16[2,8,2,320,128]{4,3,2,1,0:T(8,128)(2,1)S(1)}, f32[8,640,384]{2,1,0:T(8,128)}) custom-call(bf16[640,1024]{1,0:T(8,128)(2,1)S(1)} %bitcast.50, f32[1,1024]{1,0:T(1,128)S(1)} %bitcast.57, bf16[1024,2048]{1,0:T(8,128)(2,1)S(1)} %bitcast.48, ...), custom_call_target="tpu_custom_call" | custom-call | tf_op jit(solution)/shard_map/project/pallas_call | solution.py:507
  107.3 1.5 copy-done.5
  108.8 1.5 copy-done.6
  110.3 1.1 copy-done.8
  111.4 151.1 %forward.1 = (bf16[640,2048]{1,0:T(8,128)(2,1)}, f32[1280,128]{1,0:T(8,128)S(1)}, bf16[2,8,2560,128]{3,2,1,0:T(8,128)(2,1)}, bf16[2,2,4,2,32,2048]{5,4,3,2,1,0:T...) custom-call(s32[12]{0:T(128)S(1)} %compare_select_fusion.1.meta, ...), custom_call_target="tpu_custom_call" | custom-call | tf_op jit(solution)/shard_map/forward/pallas_call | solution.py:862
  262.5 1.0 copy-done.13
  263.5 103.2 %feed.1 = (bf16[640,1024]{1,0:T(8,128)(2,1)}, f32[640,1024]{1,0:T(8,128)}, bf16[8,1280,128]{2,1,0:T(8,128)(2,1)}, f32[128,640]{1,0:T(8,128)}, f32[1,1024]{1,0:T(...) custom-call(bf16[640,1024]{1,0:T(8,128)(2,1)} %bitcast.49, ...), custom_call_target="tpu_custom_call" | custom-call | tf_op jit(solution)/shard_map/feed/pallas_call | solution.py:1089
  369.9 120.3 %backward.1 = (f32[8,1280,128]{2,1,0:T(8,128)}, f32[2,8,2,320,128]{4,3,2,1,0:T(8,128)}, f32[2,32,1536]{2,1,0:T(8,128)}, f32[32,2048]{1,0:T(8,128)}, bf16[2,320,1024]{2,1,0:T(8,128)(2,1)}) custom-call(s32[12]{0:T(128)} %copy-done.15, bf16[8,1280,128]{2,1,0:T(8,128)(2,1)} %copy-done.5, bf16[8,1280,128]{2,1,0:T(8,128)(2,1)} %get-tuple-element.61.g_ref, ...), custom_call_target="tpu_custom_call" | custom-call | tf_op jit(solution)/shard_map/backward/pallas_call | solution.py:1402
  490.3 1.3 copy-done.9
  491.6 39.1 %project_back.1 = (bf16[1024,2048]{1,0:T(8,128)(2,1)}, bf16[1024,1024]{1,0:T(8,128)(2,1)}, bf16[1024,1024]{1,0:T(8,128)(2,1)}, bf16[640,1024]{1,0:T(8,128)(2,1)S...) custom-call(f32[8,1280,128]{2,1,0:T(8,128)} %get-tuple-element.69.dq_ref, ...), custom_call_target="tpu_custom_call" | custom-call | tf_op jit(solution)/shard_map/project_back/pallas_call | solution.py:596
  530.8 1.1 copy-done.11
  532.6 1.6 copy-done.7
  534.2 1.3 copy-done.12
  535.5 70.2 %scatter_end.1 = (f32[32,2048]{1,0:T(8,128)S(1)}, f32[32,1024]{1,0:T(8,128)S(1)}, f32[32,1024]{1,0:T(8,128)S(1)}, f32[32,128]{1,0:T(8,128)S(1)}, bf16[2,320,1024]{2,1,0:T(8,128)(2,1)S(1)}) custom-call(bf16[2,2,4,2,32,2048]{5,4,3,2,1,0:T(8,128)(2,1)} %bitcast.66, bf16[2,2,4,2,32,1024]{5,4,3,2,1,0:T(8,128)(2,1)S(1)} %bitcast.52, ...), custom_call_target="tpu_custom_call" | custom-call | tf_op jit(solution)/shard_map/scatter_end/pallas_call | solution.py:1537
  609.7 1.8 convert_element_type.30
  611.5 1.1 copy.81
  (87 shorter events, 16.9 us)
Async XLA Ops:
  0.6 0.7 copy-start
  5.3 106.1 %copy-start.15 = (s32[12]{0:T(128)}, s32[12]{0:T(128)S(1)}, u32[]{:S(2)}) copy-start(s32[12]{0:T(128)S(1)} %compare_select_fusion.1.meta) | copy-start | bytes 148
  80.0 2.5 copy-start.3
  82.5 2.2 copy-start.2
  84.7 26.7 %copy-start.10 = (bf16[2,320,1024]{2,1,0:T(8,128)(2,1)S(1)}, bf16[2,320,1024]{2,1,0:T(8,128)(2,1)}, u32[]{:S(2)}) copy-start(bf16[2,320,1024]{2,1,0:T(8,128)(2,1)} %cot_ref.1) | copy-start | bytes 3932164
  84.7 26.7 %copy-start.14 = (bf16[2048,32]{0,1:T(8,128)(2,1)S(1)}, bf16[2048,32]{0,1:T(8,128)(2,1)}, u32[]{:S(2)}) copy-start(bf16[2048,32]{0,1:T(8,128)(2,1)} %param.27) | copy-start | bytes 393220
  107.3 1.5 copy-start.5
  108.8 1.5 copy-start.6
  110.3 1.1 copy-start.8
  262.4 1.1 copy-start.13
  369.9 120.4 %copy-start.4 = (bf16[2,320,1024]{2,1,0:T(8,128)(2,1)S(1)}, bf16[2,320,1024]{2,1,0:T(8,128)(2,1)}, u32[]{:S(2)}) copy-start(bf16[2,320,1024]{2,1,0:T(8,128)(2,1)} %get-tuple-element.52) | copy-start | bytes 3932164
  490.3 1.3 copy-start.9
  530.8 1.1 copy-start.11
  532.6 1.6 copy-start.7
  534.2 1.3 copy-start.12
  535.5 71.6 %copy-start.17 = (f32[4,32,1536]{2,1,0:T(8,128)S(1)}, f32[4,32,1536]{2,1,0:T(8,128)}, u32[]{:S(2)}) copy-start(f32[4,32,1536]{2,1,0:T(8,128)} %get-tuple-element.87) | copy-start | bytes 2359300
  535.5 71.7 %copy-start.18 = (f32[2,32,1536]{2,1,0:T(8,128)S(1)}, f32[2,32,1536]{2,1,0:T(8,128)}, u32[]{:S(2)}) copy-start(f32[2,32,1536]{2,1,0:T(8,128)} %get-tuple-element.88) | copy-start | bytes 1179652
  609.7 1.8 copy-start.16
  609.7 5.6 copy-start.1
  611.5 3.1 copy-start.19

commit v4 on v3

--- a/solution.py
+++ b/solution.py
@@ -22,6 +22,7 @@
 CHUNK = 256
 GAIN_COLS = 128
 FF_CHUNK = 512
+PAIRS = KV_HEADS // 2
 FF_CHUNKS = FF // FF_CHUNK
 FF_EARLY = 4
 LOCAL_RUNS = 3
@@ -135,7 +136,8 @@
 
 
 class Exchange:
-    def __init__(self, links, source, placed, local_sem):
+    def __init__(self, links, source, placed, local_sem, tag="swap"):
+        self.tag = tag
         self.links = links
         self.source = source
         self.placed = placed
@@ -145,7 +147,7 @@
         _, _, z, _ = self.links.place()
         half = z // (self.links.sizes[2] // 2)
         return [
-            self.links.copy("swap", self.source.at[1 - half], self.placed.at[half], self.links.across()),
+            self.links.copy(self.tag, self.source.at[1 - half], self.placed.at[half], self.links.across()),
             pltpu.make_async_copy(self.source.at[half], self.placed.at[half], self.local_sem),
         ]
 
@@ -360,22 +362,19 @@
 
 ORDERS = ("xy", "yx")
 
-FORWARD_START = [(0, 0), ("kv", 0), (1, 0), (0, 1), ("use", 0), (2, 0), (0, 2)]
-FORWARD_BEFORE = {
-    0: [("got", 0), ("kv", 1)],
-    2: [("use", 1), (0, 4), ("kv", 2), (3, 1), ("got", 1)],
-    4: [("use", 2), (0, 6), ("kv", 3), (2, 3), ("got", 2)],
-    6: [("use", 3), (1, 6), ("swap", 0), ("got", 3)],
-}
+FORWARD_START = [("swap", "tokens"), (0, 2), (0, 0), (1, 0), (0, 1), (1, 1), (1, 2), (0, 11), (2, 1), (1, 11), (2, 11), (0, 10), (2, 0), (0, 3), (3, 11), (0, 5), (3, 1), (0, 6), (3, 0), (2, 2), ("swapped", "tokens"), (4, 11), (0, 8)]
 FORWARD_AFTER = {
-    0: [(1, 1), (3, 0), (2, 1), (0, 3)],
-    1: [(1, 2), (2, 2)],
-    2: [(1, 3), (3, 2)],
-    3: [(0, 5), (1, 4)],
-    4: [(2, 4), (1, 5)],
-    5: [(3, 3), (2, 5)],
-    6: [(3, 4), (2, 6), (3, 5)],
-    7: [(3, 6)],
+    0: [(1, 3), (3, 2), ("kv", 0), (2, 3), (1, 10)],
+    1: [(1, 5), (1, 8), (2, 10), (1, 6), ("kv", 1), ("use", 0), (3, 3), (0, 7)],
+    3: [(0, 4), (1, 7), (2, 6), ("got", 0)],
+    4: [("use", 1), (2, 8), ("kv", 2)],
+    5: [("got", 1), (1, 4)],
+    6: [("kv", 3), (3, 6), (2, 5), (0, 9), (2, 7), ("use", 2), (3, 10)],
+    7: [("got", 2)],
+    8: [(3, 8), (1, 9), (2, 4), ("swap", "cot")],
+    9: [("use", 3), (3, 7), ("got", 3)],
+    10: [(2, 9), (3, 5)],
+    11: [(3, 4), (3, 9), ("swapped", "cot")],
 }
 FEED_MIDDLE = {
     1: [("begin", 0)],
@@ -405,134 +404,8 @@
     return (slice(0, width // 2), slice(width // 2, width)) if width >= 512 else (slice(0, width),)
 
 
-def gather_kernel(sizes, query_ref, kv_ref, moved_ref, query_whole, kv_whole, placed_ref, send_sem, recv_sem, local_sem):
-    links = Links(sizes, send_sem, recv_sem)
-    links.meet()
-    _, _, z, _ = links.place()
-    half = z // (sizes[2] // 2)
-    parts = []
-    for a, (shard, whole) in enumerate(((query_ref, query_whole), (kv_ref, kv_whole))):
-        width = shard.shape[-1]
-        for b in range(2):
-            edge = width // 2 // HEAD_DIM * HEAD_DIM
-            cols = slice(0, edge) if b == 0 else slice(edge, width)
-            parts.append(
-                Gather(links, (a, b), shard, whole, ORDERS[b], cols, local_sem.at[2 * a + b])
-            )
-    keep = pltpu.make_async_copy(moved_ref.at[half], placed_ref.at[half], local_sem.at[4])
-    give = links.copy("moved", moved_ref.at[1 - half], placed_ref.at[half], links.across())
-    for part in parts[:2]:
-        part.start()
-    keep.start()
-    for part in parts[2:]:
-        part.start()
-    for part in parts[:2]:
-        part.step(1)
-    give.start()
-    for part in parts[2:]:
-        part.step(1)
-    for part in parts[:2]:
-        part.step(2)
-    for part in parts[2:]:
-        part.step(2)
-    for part in parts:
-        part.step(3)
-    for part in parts:
-        part.close()
-    keep.wait()
-    give.wait()
-
-
-def gather_start(sizes, query, key_value, moved):
-    ny, nx, nz = sizes
-    rounds = 4 * Gather.copies(sizes) + 1
-    query_whole, kv_whole, placed = pl.pallas_call(
-        functools.partial(gather_kernel, sizes),
-        out_shape=[
-            jax.ShapeDtypeStruct((ny, nx, nz, 2) + query.shape, BF16),
-            jax.ShapeDtypeStruct((ny, nx, nz, 2) + key_value.shape, BF16),
-            jax.ShapeDtypeStruct(moved.shape, BF16),
-        ],
-        in_specs=[ANY] * 3,
-        out_specs=[ANY] * 3,
-        scratch_shapes=[
-            pltpu.SemaphoreType.DMA((rounds,)),
-            pltpu.SemaphoreType.DMA((rounds,)),
-            pltpu.SemaphoreType.DMA((5,)),
-        ],
-        compiler_params=pltpu.CompilerParams(collective_id=1, has_side_effects=True),
-        name="gather_start",
-    )(query, key_value, moved)
-    return query_whole.reshape(D, -1), kv_whole.reshape(D, -1), placed
-
-
 def roll_half(values):
     return pltpu.roll(values, HEAD_DIM // 2, 1)
-
-
-def project_kernel(rows, x_ref, gain_ref, wq_ref, wk_ref, wv_ref, qg_ref, kg_ref, cos_ref, sin_ref, normed_ref, q_ref, kv_ref, pre_ref):
-    sub = rows // SUBS
-
-    @pl.when(pl.program_id(0) == 0)
-    def _():
-        values = x_ref[...].astype(F32)
-        normed_ref[...] = (values * norm_factor(values) * gain_ref[...]).astype(BF16)
-
-    normed = normed_ref[...]
-    cosine, sine = cos_ref[...], sin_ref[...]
-
-    def turned(pre, gain):
-        values = pre * norm_factor(pre) * gain
-        return (values * cosine + roll_half(values) * sine).astype(BF16)
-
-    query = matmul(normed, wq_ref[...])
-    for h in range(2):
-        pre = query[:, h * HEAD_DIM : (h + 1) * HEAD_DIM]
-        pre_ref[0, :, h * HEAD_DIM : (h + 1) * HEAD_DIM] = pre
-        low = turned(pre, qg_ref[...])
-        for s in range(2 * SUBS):
-            q_ref[0, (2 * s + h) * sub : (2 * s + h + 1) * sub] = low[s * sub : (s + 1) * sub]
-    pre = matmul(normed, wk_ref[...])
-    pre_ref[0, :, 2 * HEAD_DIM :] = pre
-    kv_ref[0, 0] = turned(pre, kg_ref[...]).reshape(2, rows, HEAD_DIM)
-    kv_ref[1, 0] = matmul(normed, wv_ref[...]).astype(BF16).reshape(2, rows, HEAD_DIM)
-
-
-def project(x, gain, query_full, kv_full, query_gain, key_gain, cosine, sine):
-    count = x.shape[0]
-    rows = count // 2
-    full = pl.BlockSpec((count, D), lambda h: (0, 0))
-    row = lambda n: pl.BlockSpec((1, n), lambda h: (0, 0))
-    table = pl.BlockSpec((count, HEAD_DIM), lambda h: (0, 0))
-    return pl.pallas_call(
-        functools.partial(project_kernel, rows),
-        grid=(KV_HEADS,),
-        out_shape=[
-            jax.ShapeDtypeStruct((count, D), BF16),
-            jax.ShapeDtypeStruct((KV_HEADS, 2 * count, HEAD_DIM), BF16),
-            jax.ShapeDtypeStruct((2, KV_HEADS, 2, rows, HEAD_DIM), BF16),
-            jax.ShapeDtypeStruct((KV_HEADS, count, 3 * HEAD_DIM), F32),
-        ],
-        in_specs=[
-            full,
-            row(D),
-            pl.BlockSpec((D, 2 * HEAD_DIM), lambda h: (0, h)),
-            pl.BlockSpec((D, HEAD_DIM), lambda h: (0, h)),
-            pl.BlockSpec((D, HEAD_DIM), lambda h: (0, KV_HEADS + h)),
-            row(HEAD_DIM),
-            row(HEAD_DIM),
-            table,
-            table,
-        ],
-        out_specs=[
-            full,
-            pl.BlockSpec((1, 2 * count, HEAD_DIM), lambda h: (h, 0, 0)),
-            pl.BlockSpec((2, 1, 2, rows, HEAD_DIM), lambda h: (0, h, 0, 0, 0)),
-            pl.BlockSpec((1, count, 3 * HEAD_DIM), lambda h: (h, 0, 0)),
-        ],
-        compiler_params=pltpu.CompilerParams(vmem_limit_bytes=40 * MIB),
-        name="project",
-    )(x, gain, query_full, kv_full, kv_full, query_gain, key_gain, cosine, sine)
 
 
 def project_back_kernel(
@@ -569,7 +442,7 @@
     pieces.append(low)
     pieces.append(dkv_ref[1, 0].reshape(2 * rows, HEAD_DIM).astype(BF16))
     low = jnp.concatenate(pieces, axis=1)
-    weights = jnp.concatenate([wq_ref[...], wk_ref[...], wv_ref[...]], axis=1)
+    weights = jnp.concatenate([wq_ref[0], wk_ref[0], wv_ref[0]], axis=1)
     grads[...] += nt(low, weights)
     part = matmul(normed_t[...], low).astype(BF16)
     dwq_ref[...] = part[:, : 2 * HEAD_DIM]
@@ -585,7 +458,7 @@
         in_ref[...] = jnp.sum(part, axis=0, keepdims=True)
 
 
-def project_back(dq, dkv, pre, normed, x, grad_hidden, gain, query_full, kv_full, query_gain, key_gain, cosine, sine):
+def project_back(dq, dkv, pre, normed, x, grad_hidden, gain, qkv_full, query_gain, key_gain, cosine, sine):
     count = x.shape[0]
     rows = count // 2
     full = pl.BlockSpec((count, D), lambda h: (0, 0))
@@ -612,9 +485,9 @@
             full,
             full,
             row(D),
-            wide,
-            thin,
-            pl.BlockSpec((D, HEAD_DIM), lambda h: (0, KV_HEADS + h)),
+            pl.BlockSpec((1, D, 2 * HEAD_DIM), lambda h: (h // 2, 0, h % 2)),
+            pl.BlockSpec((1, D, HEAD_DIM), lambda h: (h // 2, 0, 4 + h % 2)),
+            pl.BlockSpec((1, D, HEAD_DIM), lambda h: (h // 2, 0, 6 + h % 2)),
             row(HEAD_DIM),
             row(HEAD_DIM),
             table,
@@ -624,16 +497,14 @@
         scratch_shapes=[pltpu.VMEM((D, count), BF16), pltpu.VMEM((count, D), F32)],
         compiler_params=pltpu.CompilerParams(vmem_limit_bytes=48 * MIB),
         name="project_back",
-    )(dq, dkv, pre, normed, x, grad_hidden, gain, query_full, kv_full, kv_full, query_gain, key_gain, cosine, sine)
+    )(dq, dkv, pre, normed, x, grad_hidden, gain, qkv_full, qkv_full, qkv_full, query_gain, key_gain, cosine, sine)
 
 
 class KeyValues:
-    def __init__(self, links, rows, own, held, local_sem):
+    def __init__(self, links, rows, held):
         self.links = links
         self.rows = rows
-        self.own = own
         self.held = held
-        self.local_sem = local_sem
 
     def slab(self, group, piece, member):
         members = self.links.sizes[2]
@@ -647,19 +518,16 @@
     def across(self, group):
         found = []
         for piece in range(2):
-            src = self.own.at[:, 2 * group : 2 * group + 2, piece]
-            dst = self.slab(group, piece, self.mine())
+            slab = self.slab(group, piece, self.mine())
             for i, (_, target) in enumerate(self.links.group()):
-                found.append(self.links.copy(("kv", group, piece, i), src, dst, target))
+                found.append(self.links.copy(("kv", group, piece, i), slab, slab, target))
         return found
 
     def near(self, group):
         found = []
         for piece in range(2):
-            src = self.own.at[:, 2 * group : 2 * group + 2, piece]
-            dst = self.slab(group, piece, self.mine())
-            found.append(self.links.copy(("kv own", group, piece), src, dst, self.links.sibling()))
-            found.append(pltpu.make_async_copy(src, dst, self.local_sem.at[2 * group + piece]))
+            slab = self.slab(group, piece, self.mine())
+            found.append(self.links.copy(("kv own", group, piece), slab, slab, self.links.sibling()))
         return found
 
     def forward(self, group):
@@ -704,36 +572,64 @@
             out[slot + k] = total
 
 
-def forward_kernel(sizes, rows, meta, q_ref, kv_ref, cot_ref, out_shard, *refs):
-    shard = (out_shard,) + refs[:FF_CHUNKS]
-    mixed_ref, l_ref, kv_all, out_whole, feed_whole, cot_placed = refs[FF_CHUNKS : FF_CHUNKS + 6]
-    whole = (out_whole,) + tuple(feed_whole.at[c] for c in range(FF_CHUNKS))
-    kvs, acc, part, places, kp, vp, send_sem, recv_sem, local_sem = refs[FF_CHUNKS + 6 :]
+def forward_kernel(sizes, rows, meta, cos_ref, sin_ref, tok_ref, cot_ref, *refs):
+    arrays = PAIRS + 2 + FF_CHUNKS
+    shard = refs[:arrays]
+    (mixed_ref, l_ref, pre_ref, normed_ref, gains_ref, qk_ref,
+     placed, cot_placed, q_all, kv_all, qkv_whole, gain_whole, out_whole, feed_whole) = refs[arrays : arrays + 14]
+    whole = (
+        tuple(qkv_whole.at[c] for c in range(PAIRS))
+        + (out_whole,)
+        + tuple(feed_whole.at[c] for c in range(FF_CHUNKS))
+        + (gain_whole,)
+    )
+    (qs, kvs, xs, ws, gs, acc, part, places, kp, vp, send_sem, recv_sem, local_sem) = refs[arrays + 14 :]
     members = sizes[2]
     sub = rows // SUBS
-    head = pl.program_id(0)
+    count = 2 * rows
+    step = pl.program_id(0)
+    head = jnp.maximum(step - PAIRS, 0)
     links = Links(sizes, send_sem, recv_sem)
-    kv = KeyValues(links, rows, kv_ref, kvs, local_sem)
-    swap = Exchange(links, cot_ref, cot_placed, local_sem.at[12 + 2 * (FF_CHUNKS + 1)])
+    kv = KeyValues(links, rows, kvs)
+    swaps = {
+        "tokens": Exchange(links, tok_ref, placed, local_sem.at[0], "tokens"),
+        "cot": Exchange(links, cot_ref, cot_placed, local_sem.at[1], "cot"),
+    }
     weights_ = [
         [
             Gather(links, (a, b), shard[a], whole[a], ORDERS[b], cols, local_sem.at[12 + 2 * a + b])
             for b, cols in enumerate(halves_of(shard[a].shape[-1]))
         ]
-        for a in range(FF_CHUNKS + 1)
+        for a in range(arrays)
     ]
+    _, _, z, core = links.place()
+    mine = lax.rem(z, members // 2) * 2 + core
 
     def kept(group):
-        return pltpu.make_async_copy(
-            kvs.at[:, 2 * group : 2 * group + 2],
-            kv_all.at[:, 2 * group : 2 * group + 2],
-            local_sem.at[8 + group],
-        )
+        pair = slice(2 * group, 2 * group + 2)
+        return [
+            pltpu.make_async_copy(kvs.at[:, pair], kv_all.at[:, pair], local_sem.at[2 + group]),
+            pltpu.make_async_copy(qs.at[pair], q_all.at[pair], local_sem.at[6 + group]),
+        ]
+
+    def fetch(src, dst):
+        ny, nx, nz = sizes
+        shard_rows = src.shape[4]
+        copies = []
+        for i in range(ny * nx * nz * 2):
+            block = src.at[i // (nx * nz * 2), i // (nz * 2) % nx, i // 2 % nz, i % 2]
+            copies.append(
+                pltpu.make_async_copy(block, dst.at[i * shard_rows : (i + 1) * shard_rows], local_sem.at[10])
+            )
+        run_all(copies, "start")
+        pltpu.make_async_copy(dst, dst, local_sem.at[10]).wait()
 
     def act(steps):
         for what, a in steps:
             if what == "swap":
-                swap.start()
+                swaps[a].start()
+            elif what == "swapped":
+                swaps[a].wait()
             elif what == "kv":
                 run_all(kv.across(a), "start")
                 run_all(kv.near(a), "start")
@@ -743,163 +639,225 @@
             elif what == "got":
                 run_all(kv.near(a), "wait")
                 run_all(kv.forward(a), "wait")
-                kept(a).start()
+                run_all(kept(a), "start")
             else:
                 for g in weights_[a]:
                     if what == 0:
                         g.start()
+                    elif what == 4:
+                        g.close()
                     else:
                         g.step(what)
 
-    @pl.when(head == 0)
+    @pl.when(step == 0)
     def _():
         links.meet()
         act(FORWARD_START)
         l_ref[...] = jnp.zeros_like(l_ref)
         places[...] = row_places(places.shape, 0, sub)
-
-    for moment, steps in FORWARD_BEFORE.items():
-        pl.when(head == moment)(functools.partial(act, steps))
-
-    _, _, z, core = links.place()
-    mine = lax.rem(z, members // 2) * 2 + core
-    lane = lax.broadcasted_iota(jnp.int32, (2 * rows, HEAD_DIM), 1)
-    for piece in range(2):
-        base = rows * (piece * members + mine)
-        region = slice(piece * 2 * rows, (piece + 1) * 2 * rows)
-        acc[...] = jnp.zeros_like(acc)
-        part[...] = jnp.zeros_like(part)
-
-        def trunk(step, masked):
-            start = pl.multiple_of(step * CHUNK, CHUNK)
-            weights = jnp.exp2(nt(q_ref[0, region], kvs[0, head, pl.ds(start, CHUNK)]) * exp2_scale)
-            low, high = weights[:, :HEAD_DIM], weights[:, HEAD_DIM:]
-            if masked:
-                room = places[...] + (base - start)
-                low = jnp.where(lane <= room, low, 0.0)
-                high = jnp.where(lane + HEAD_DIM <= room, high, 0.0)
-                weights = jnp.concatenate([low, high], axis=1)
-            part[...] += low + high
-            acc[...] += matmul(weights.astype(BF16), kvs[1, head, pl.ds(start, CHUNK)])
-            return masked
-
-        if piece == 0:
-            clear = jnp.minimum(base // CHUNK, TRUNK // CHUNK)
-            last = jnp.minimum((base + rows + CHUNK - 1) // CHUNK, TRUNK // CHUNK)
-            lax.fori_loop(0, clear, lambda i, c: (trunk(i, False), c)[1], 0)
-            lax.fori_loop(clear, last, lambda i, c: (trunk(i, True), c)[1], 0)
-        else:
-            lax.fori_loop(0, TRUNK // CHUNK, lambda i, c: (trunk(i, False), c)[1], 0)
-
-        lead = jnp.maximum(base - TRUNK, 0) // SEG
-
-        def parents_():
-            gather_parents(
-                meta,
-                lead,
-                0,
-                [
-                    (lambda b: kvs[0, head, TRUNK + b * SEG : TRUNK + (b + 1) * SEG], kp),
-                    (lambda b: kvs[1, head, TRUNK + b * SEG : TRUNK + (b + 1) * SEG], vp),
-                ],
-            )
-
-        if piece == 0:
-            pl.when(base + rows > TRUNK)(parents_)
-        else:
-            parents_()
-        for s in range(SUBS):
-            block = slice(2 * sub * s, 2 * sub * (s + 1))
-
-            def runs():
-                row = base + s * sub - TRUNK
-                run = row // SEG
-                own = pl.multiple_of(TRUNK + run * SEG, SEG)
-                flag = jnp.minimum(meta[run] + 1, 1).astype(F32)
-                query = q_ref[0, piece * 2 * rows + 2 * sub * s : piece * 2 * rows + 2 * sub * (s + 1)]
-                room = places[block] + (lax.rem(row, SEG) - s * sub)
-                weights = jnp.exp2(nt(query, kvs[0, head, pl.ds(own, SEG)]) * exp2_scale)
-                weights = jnp.where(lane[block] <= room, weights, 0.0)
-                above = jnp.exp2(nt(query, kp[run - lead]) * exp2_scale) * flag
-                part[block] += weights + above
-                acc[block] += matmul(weights.astype(BF16), kvs[1, head, pl.ds(own, SEG)]) + matmul(
-                    above.astype(BF16), vp[run - lead]
+        fetch(gain_whole, gs)
+        loaded = pltpu.make_async_copy(placed, xs, local_sem.at[11])
+        loaded.start()
+        gains_ref[...] = gs[:, :GAIN_COLS].astype(F32).T[:8]
+        qk_ref[0:1] = jnp.sum(gs[:, GAIN_COLS : 2 * GAIN_COLS].astype(F32), axis=0, keepdims=True)
+        qk_ref[1:2] = jnp.sum(gs[:, 2 * GAIN_COLS :].astype(F32), axis=0, keepdims=True)
+        loaded.wait()
+        values = xs[...].reshape(count, D).astype(F32)
+        normed_ref[...] = (values * norm_factor(values) * gains_ref[0:1]).astype(BF16)
+
+    for c in range(PAIRS):
+
+        @pl.when(step == c)
+        def _():
+            act([(4, c)])
+            fetch(qkv_whole.at[c], ws)
+
+    @pl.when(step < PAIRS)
+    def _():
+        normed = normed_ref[...]
+        cosine, sine = cos_ref[...], sin_ref[...]
+
+        def turned(pre, gain):
+            values = pre * norm_factor(pre) * gain
+            return (values * cosine + roll_half(values) * sine).astype(BF16)
+
+        for hh in range(2):
+            at = 2 * step + hh
+            query = matmul(normed, ws[:, 2 * hh * HEAD_DIM : 2 * (hh + 1) * HEAD_DIM])
+            for h in range(2):
+                pre = query[:, h * HEAD_DIM : (h + 1) * HEAD_DIM]
+                pre_ref[hh, :, h * HEAD_DIM : (h + 1) * HEAD_DIM] = pre
+                low = turned(pre, qk_ref[0:1])
+                for s in range(2 * SUBS):
+                    qs[at, (2 * s + h) * sub : (2 * s + h + 1) * sub] = low[s * sub : (s + 1) * sub]
+            pre = matmul(normed, ws[:, (4 + hh) * HEAD_DIM : (5 + hh) * HEAD_DIM])
+            pre_ref[hh, :, 2 * HEAD_DIM :] = pre
+            low = turned(pre, qk_ref[1:2])
+            value = matmul(normed, ws[:, (6 + hh) * HEAD_DIM : (7 + hh) * HEAD_DIM]).astype(BF16)
+            for piece in range(2):
+                start = pl.multiple_of(rows * (piece * members + mine), rows)
+                kvs[0, at, pl.ds(start, rows)] = low[piece * rows : (piece + 1) * rows]
+                kvs[1, at, pl.ds(start, rows)] = value[piece * rows : (piece + 1) * rows]
+
+    def attend():
+        lane = lax.broadcasted_iota(jnp.int32, (2 * rows, HEAD_DIM), 1)
+        for piece in range(2):
+            base = rows * (piece * members + mine)
+            region = slice(piece * 2 * rows, (piece + 1) * 2 * rows)
+            acc[...] = jnp.zeros_like(acc)
+            part[...] = jnp.zeros_like(part)
+
+            def trunk(step, masked):
+                start = pl.multiple_of(step * CHUNK, CHUNK)
+                weights = jnp.exp2(nt(qs[head, region], kvs[0, head, pl.ds(start, CHUNK)]) * exp2_scale)
+                low, high = weights[:, :HEAD_DIM], weights[:, HEAD_DIM:]
+                if masked:
+                    room = places[...] + (base - start)
+                    low = jnp.where(lane <= room, low, 0.0)
+                    high = jnp.where(lane + HEAD_DIM <= room, high, 0.0)
+                    weights = jnp.concatenate([low, high], axis=1)
+                part[...] += low + high
+                acc[...] += matmul(weights.astype(BF16), kvs[1, head, pl.ds(start, CHUNK)])
+                return masked
+
+            if piece == 0:
+                clear = jnp.minimum(base // CHUNK, TRUNK // CHUNK)
+                last = jnp.minimum((base + rows + CHUNK - 1) // CHUNK, TRUNK // CHUNK)
+                lax.fori_loop(0, clear, lambda i, c: (trunk(i, False), c)[1], 0)
+                lax.fori_loop(clear, last, lambda i, c: (trunk(i, True), c)[1], 0)
+            else:
+                lax.fori_loop(0, TRUNK // CHUNK, lambda i, c: (trunk(i, False), c)[1], 0)
+
+            lead = jnp.maximum(base - TRUNK, 0) // SEG
+
+            def parents_():
+                gather_parents(
+                    meta,
+                    lead,
+                    0,
+                    [
+                        (lambda b: kvs[0, head, TRUNK + b * SEG : TRUNK + (b + 1) * SEG], kp),
+                        (lambda b: kvs[1, head, TRUNK + b * SEG : TRUNK + (b + 1) * SEG], vp),
+                    ],
                 )
 
             if piece == 0:
-                pl.when(base + s * sub >= TRUNK)(runs)
+                pl.when(base + rows > TRUNK)(parents_)
             else:
-                runs()
-
-        total = jnp.sum(part[...], axis=-1, keepdims=True)
-        mixed = (acc[...] / total).astype(BF16)
-        for s in range(SUBS):
-            for h in range(2):
-                row = piece * rows + sub * s
-                mixed_ref[row : row + sub, h * HEAD_DIM : (h + 1) * HEAD_DIM] = mixed[
-                    (2 * s + h) * sub : (2 * s + h + 1) * sub
-                ]
-        l_ref[region] = jnp.where(lane == head, total, l_ref[region])
-
+                parents_()
+            for s in range(SUBS):
+                block = slice(2 * sub * s, 2 * sub * (s + 1))
+
+                def runs():
+                    row = base + s * sub - TRUNK
+                    run = row // SEG
+                    own = pl.multiple_of(TRUNK + run * SEG, SEG)
+                    flag = jnp.minimum(meta[run] + 1, 1).astype(F32)
+                    query = qs[head, piece * 2 * rows + 2 * sub * s : piece * 2 * rows + 2 * sub * (s + 1)]
+                    room = places[block] + (lax.rem(row, SEG) - s * sub)
+                    weights = jnp.exp2(nt(query, kvs[0, head, pl.ds(own, SEG)]) * exp2_scale)
+                    weights = jnp.where(lane[block] <= room, weights, 0.0)
+                    above = jnp.exp2(nt(query, kp[run - lead]) * exp2_scale) * flag
+                    part[block] += weights + above
+                    acc[block] += matmul(weights.astype(BF16), kvs[1, head, pl.ds(own, SEG)]) + matmul(
+                        above.astype(BF16), vp[run - lead]
+                    )
+
+                if piece == 0:
+                    pl.when(base + s * sub >= TRUNK)(runs)
+                else:
+                    runs()
+
+            total = jnp.sum(part[...], axis=-1, keepdims=True)
+            mixed = (acc[...] / total).astype(BF16)
+            for s in range(SUBS):
+                for h in range(2):
+                    row = piece * rows + sub * s
+                    mixed_ref[row : row + sub, h * HEAD_DIM : (h + 1) * HEAD_DIM] = mixed[
+                        (2 * s + h) * sub : (2 * s + h + 1) * sub
+                    ]
+            l_ref[region] = jnp.where(lane == head, total, l_ref[region])
+
+
+    pl.when(step >= PAIRS)(attend)
     for moment, steps in FORWARD_AFTER.items():
-        pl.when(head == moment)(functools.partial(act, steps))
-
-    @pl.when(head == KV_HEADS - 1)
+        pl.when(step == moment)(functools.partial(act, steps))
+
+    @pl.when(step == PAIRS + KV_HEADS - 1)
     def _():
-        for pair in weights_:
-            for g in pair:
+        for array in weights_[PAIRS : PAIRS + 1 + FF_CHUNKS]:
+            for g in array:
                 g.close()
         for group in range(4):
-            kept(group).wait()
-        swap.wait()
-
-
-def forward(sizes, meta, queries, kv, cotangent, out_shard, feed_shards):
+            run_all(kept(group), "wait")
+
+
+def forward(sizes, meta, cosine, sine, tokens, cotangent, shards_):
     ny, nx, nz = sizes
-    rows = kv.shape[3]
-    count = 1 + FF_CHUNKS
-    rounds = KeyValues.copies(sizes) + 2 * count * Gather.copies(sizes) + 1
+    rows = tokens.shape[1]
+    count = 2 * rows
+    arrays = PAIRS + 2 + FF_CHUNKS
+    shard_rows = shards_[0].shape[0]
+    blocks = (ny, nx, nz, 2, shard_rows)
+    widths = [w.shape[-1] for w in shards_]
+    rounds = KeyValues.copies(sizes) + 2 * arrays * Gather.copies(sizes) + 2
+
+    def at_head(s):
+        return jnp.maximum(s - PAIRS, 0)
+
     results = pl.pallas_call(
         functools.partial(forward_kernel, sizes, rows),
         out_shape=[
-            jax.ShapeDtypeStruct((2 * rows, QD), BF16),
-            jax.ShapeDtypeStruct((4 * rows, HEAD_DIM), F32),
+            jax.ShapeDtypeStruct((count, QD), BF16),
+            jax.ShapeDtypeStruct((2 * count, HEAD_DIM), F32),
+            jax.ShapeDtypeStruct((KV_HEADS, count, 3 * HEAD_DIM), F32),
+            jax.ShapeDtypeStruct((count, D), BF16),
+            jax.ShapeDtypeStruct((8, D), F32),
+            jax.ShapeDtypeStruct((8, HEAD_DIM), F32),
+            jax.ShapeDtypeStruct(tokens.shape, BF16),
+            jax.ShapeDtypeStruct(tokens.shape, BF16),
+            jax.ShapeDtypeStruct((KV_HEADS, 2 * count, HEAD_DIM), BF16),
             jax.ShapeDtypeStruct((2, KV_HEADS, TREE, HEAD_DIM), BF16),
-            jax.ShapeDtypeStruct((ny, nx, nz, 2) + out_shard.shape, BF16),
-            jax.ShapeDtypeStruct((FF_CHUNKS, ny, nx, nz, 2) + feed_shards[0].shape, BF16),
-            jax.ShapeDtypeStruct(cotangent.shape, BF16),
+            jax.ShapeDtypeStruct((PAIRS,) + blocks + (widths[0],), BF16),
+            jax.ShapeDtypeStruct(blocks + (widths[-1],), BF16),
+            jax.ShapeDtypeStruct(blocks + (widths[PAIRS],), BF16),
+            jax.ShapeDtypeStruct((FF_CHUNKS,) + blocks + (widths[PAIRS + 1],), BF16),
         ],
         grid_spec=pltpu.PrefetchScalarGridSpec(
             num_scalar_prefetch=1,
-            grid=(KV_HEADS,),
-            in_specs=[pl.BlockSpec((1, 4 * rows, HEAD_DIM), lambda h, meta: (h, 0, 0)), ANY, ANY] + [ANY] * count,
+            grid=(PAIRS + KV_HEADS,),
+            in_specs=[pl.BlockSpec((count, HEAD_DIM), lambda s, meta: (0, 0))] * 2 + [ANY] * (2 + arrays),
             out_specs=[
-                pl.BlockSpec((2 * rows, 2 * HEAD_DIM), lambda h, meta: (0, h)),
-                pl.BlockSpec((4 * rows, HEAD_DIM), lambda h, meta: (0, 0)),
-                ANY,
-                ANY,
-                ANY,
-                ANY,
-            ],
+                pl.BlockSpec((count, 2 * HEAD_DIM), lambda s, meta: (0, at_head(s))),
+                pl.BlockSpec((2 * count, HEAD_DIM), lambda s, meta: (0, 0)),
+                pl.BlockSpec((2, count, 3 * HEAD_DIM), lambda s, meta: (jnp.minimum(s, PAIRS - 1), 0, 0)),
+                pl.BlockSpec((count, D), lambda s, meta: (0, 0)),
+                pl.BlockSpec((8, D), lambda s, meta: (0, 0)),
+                pl.BlockSpec((8, HEAD_DIM), lambda s, meta: (0, 0)),
+            ]
+            + [ANY] * 8,
             scratch_shapes=[
+                pltpu.VMEM((KV_HEADS, 2 * count, HEAD_DIM), BF16),
                 pltpu.VMEM((2, KV_HEADS, TREE, HEAD_DIM), BF16),
-                pltpu.VMEM((2 * rows, HEAD_DIM), F32),
-                pltpu.VMEM((2 * rows, HEAD_DIM), F32),
-                pltpu.VMEM((2 * rows, HEAD_DIM), jnp.int32),
+                pltpu.VMEM(tokens.shape, BF16),
+                pltpu.VMEM((D, widths[0]), BF16),
+                pltpu.VMEM((D, widths[-1]), BF16),
+                pltpu.VMEM((count, HEAD_DIM), F32),
+                pltpu.VMEM((count, HEAD_DIM), F32),
+                pltpu.VMEM((count, HEAD_DIM), jnp.int32),
                 pltpu.VMEM((LOCAL_RUNS, SEG, HEAD_DIM), BF16),
                 pltpu.VMEM((LOCAL_RUNS, SEG, HEAD_DIM), BF16),
                 pltpu.SemaphoreType.DMA((rounds,)),
                 pltpu.SemaphoreType.DMA((rounds,)),
-                pltpu.SemaphoreType.DMA((13 + 2 * count,)),
+                pltpu.SemaphoreType.DMA((12 + 2 * arrays,)),
             ],
         ),
         compiler_params=pltpu.CompilerParams(
-            collective_id=2, has_side_effects=True, vmem_limit_bytes=48 * MIB
+            collective_id=2, has_side_effects=True, vmem_limit_bytes=56 * MIB
         ),
         name="forward",
-    )(meta, queries, kv, cotangent, out_shard, *feed_shards)
-    mixed, totals, kv_all, out_whole, feed_whole, cot = results
-    return mixed, totals, kv_all, out_whole.reshape(D, QD), feed_whole.reshape(FF_CHUNKS, D, -1), cot
+    )(meta, cosine, sine, tokens, cotangent, *shards_)
+    return results
 
 
 def feed_kernel(
@@ -1583,23 +1541,35 @@
     count = 2 * rows
     sub = rows // SUBS
 
-    def column(gain):
-        return jnp.pad(gain, (0, shard_rows - gain.shape[0]))[:, None]
-
-    gains = jnp.concatenate(
-        [column(input_norm), column(post_norm), column(query_norm), column(key_norm)], axis=1
+    device = lax.axis_index("dp") * 2 * nz + ctx
+
+    def spread(gain):
+        line = jnp.zeros((1, HEAD_DIM), BF16)
+        line = lax.dynamic_update_slice(line, gain[None, :], (0, device * gain_rows))
+        return jnp.pad(line, ((0, shard_rows - 1), (0, 0)))
+
+    gains = jnp.pad(
+        jnp.stack([input_norm, post_norm], axis=1), ((0, 0), (0, GAIN_COLS - 2))
     )
-    gains = jnp.pad(gains, ((0, 0), (0, GAIN_COLS - 4)))
-    key_value = jnp.concatenate([key_proj, value_proj, gains], axis=1)
-    query_full, kv_full, placed = gather_start(sizes, query_proj, key_value, tokens)
-    x = placed.reshape(count, D)
-
-    gain_block = kv_full[:, 2 * KVD :].astype(F32)
-    in_weight = gain_block[:, 0][None, :]
-    post_weight = gain_block[:, 1][None, :]
-    by_device = gain_block.reshape(-1, shard_rows, GAIN_COLS)
-    query_weight = by_device[:, :gain_rows, 2].reshape(1, HEAD_DIM)
-    key_weight = by_device[:, :gain_rows, 3].reshape(1, HEAD_DIM)
+    gains = jnp.concatenate([gains, spread(query_norm), spread(key_norm)], axis=1)
+    qkv_shards = [
+        jnp.concatenate(
+            [
+                query_proj[:, 4 * HEAD_DIM * c : 4 * HEAD_DIM * (c + 1)],
+                key_proj[:, 2 * HEAD_DIM * c : 2 * HEAD_DIM * (c + 1)],
+                value_proj[:, 2 * HEAD_DIM * c : 2 * HEAD_DIM * (c + 1)],
+            ],
+            axis=1,
+        )
+        for c in range(PAIRS)
+    ]
+    down_t = down_proj.T
+    feed_shards = [
+        jnp.concatenate(
+            [w[:, c * FF_CHUNK : (c + 1) * FF_CHUNK] for w in (gate_proj, up_proj, down_t)], axis=1
+        )
+        for c in range(FF_CHUNKS)
+    ]
 
     run_seg = segment_ids[half][TRUNK::SEG]
     run_parent = parents[half][run_seg]
@@ -1609,21 +1579,18 @@
     pos_local = lax.dynamic_index_in_dim(pos_tree, member, 1, keepdims=False).reshape(count)
     cosine, sine = rope_tables(pos_local)
 
-    normed, queries, kv, pre = project(
-        x, in_weight, query_full, kv_full, query_weight, key_weight, cosine, sine
+    (mixed, totals, pre, normed, gain_rows_, qk_gains, placed, cot, queries, kv_all,
+     qkv_full, _, out_t, feed_whole) = forward(
+        sizes, meta, cosine, sine, tokens, cotangent, qkv_shards + [out_proj.T] + feed_shards + [gains]
     )
-    down_t = down_proj.T
-    feed_shards = [
-        jnp.concatenate(
-            [w[:, c * FF_CHUNK : (c + 1) * FF_CHUNK] for w in (gate_proj, up_proj, down_t)], axis=1
-        )
-        for c in range(FF_CHUNKS)
-    ]
-    mixed, totals, kv_all, out_t, feed_whole, cot = forward(
-        sizes, meta, queries, kv, cotangent, out_proj.T, feed_shards
-    )
+    x = placed.reshape(count, D)
+    cot = cot.reshape(count, D)
+    in_weight, post_weight = gain_rows_[0:1], gain_rows_[1:2]
+    query_weight, key_weight = qk_gains[0:1], qk_gains[1:2]
+    qkv_full = qkv_full.reshape(PAIRS, D, -1)
+    out_t = out_t.reshape(D, QD)
+    feed_whole = feed_whole.reshape(FF_CHUNKS, D, -1)
     log_total = jnp.log2(totals[:, :KV_HEADS]).T
-    cot = cot.reshape(count, D)
     result, grad_hidden, grad_stack, delta, post_part, dout, late, early_grad = feed(
         sizes, x, mixed, cot, out_t, post_weight, feed_whole
     )
@@ -1638,7 +1605,7 @@
         return piece.transpose(1, 0, 2).reshape(shard_rows, FF)
 
     dwq, dwk, dwv, dx, in_part, qk_part = project_back(
-        dq, dkv, pre, normed, x, grad_hidden, in_weight, query_full, kv_full, query_weight, key_weight, cosine, sine
+        dq, dkv, pre, normed, x, grad_hidden, in_weight, qkv_full, query_weight, key_weight, cosine, sine
     )
 
     def gain_column(values):

time: 625 us -> 583 us (0.933)
  Pallas kernels: 575 us -> 542 us
  local copies, waits for them, and re-layouts: 30.7 us -> 24.4 us
    pallas_call x2 -> x0, Pallas kernels: 91.5 us -> none  [the longest x1 68.9 us: gather_start(): pl.pallas_call(functools.partial(gather_kernel, sizes), out_shape=[jax.Sh...]
    pallas_call x1, Pallas kernels: 151 us -> 213 us  [forward(): pl.pallas_call(functools.partial(forward_kernel, sizes, rows), out_shape=...]
    unnamed x48 -> x40, local copies, waits for them, and re-layouts: 17.4 us -> 8.76 us
where the time goes in v4:
time: 583 us; the launch traced here: 579 us
  Pallas kernels  542 us (93%)
  local copies, waits for them, and re-layouts  24.4 us (4%)
  other arithmetic  11.5 us (2%)
    pallas_call x1, Pallas kernels, forward(): pl.pallas_call(functools.partial(forward_kernel, sizes, rows), out_shape=...  213 us
    pallas_call x1, Pallas kernels, backward(): pl.pallas_call(functools.partial(backward_kernel, sizes, rows, widths), o...  120 us
    pallas_call x1, Pallas kernels, feed(): pl.pallas_call(functools.partial(feed_kernel, sizes, rows), grid=(FF_CHUN...  100 us
    pallas_call x1, Pallas kernels, scatter_end(): pl.pallas_call(functools.partial(scatter_kernel, sizes, widths), out_shap...  69.7 us
    pallas_call x1, Pallas kernels, project_back(): pl.pallas_call(functools.partial(project_back_kernel, rows), grid=(KV_HEA...  39 us

profile of v4, /device:TPU:0, one launch (start us, length us, event | category | flops | bytes accessed | tf_op | source)
XLA Modules:
  0.0 578.8 jit_solution(2168271143678305025)
XLA Ops:
  2.0 0.8 dynamic_update_slice.7
  2.8 0.8 dynamic_update_slice.6
  4.3 0.8 dynamic-slice_reduce_fusion
  7.3 0.8 fusion.14
  8.8 0.8 fusion.13
  11.0 0.9 fusion.10
  14.0 1.2 fusion
  15.2 0.9 pad_maximum_fusion.1.sin_ref
  16.1 0.9 pad_maximum_fusion.cos_ref
  17.0 212.9 %forward.1 = (bf16[640,2048]{1,0:T(8,128)(2,1)}, f32[1280,128]{1,0:T(8,128)}, f32[8,640,384]{2,1,0:T(8,128)}, bf16[640,1024]{1,0:T(8,128)(2,1)}, f32[8,1024]{1,0...) custom-call(s32[12]{0:T(128)} %compare_select_fusion.1.meta, ...), custom_call_target="tpu_custom_call" | custom-call | tf_op jit(solution)/shard_map/forward/pallas_call | solution.py:808
  230.7 1.4 fusion.16
  232.1 100.4 %feed.1 = (bf16[640,1024]{1,0:T(8,128)(2,1)}, f32[640,1024]{1,0:T(8,128)}, bf16[8,1280,128]{2,1,0:T(8,128)(2,1)}, f32[128,640]{1,0:T(8,128)}, f32[1,1024]{1,0:T(...) custom-call(bf16[640,1024]{1,0:T(8,128)(2,1)} %bitcast.41, ...), custom_call_target="tpu_custom_call" | custom-call | tf_op jit(solution)/shard_map/feed/pallas_call | solution.py:1047
  333.2 0.8 slice.173
  335.8 119.7 %backward.1 = (f32[8,1280,128]{2,1,0:T(8,128)}, f32[2,8,2,320,128]{4,3,2,1,0:T(8,128)}, f32[2,32,1536]{2,1,0:T(8,128)}, f32[32,2048]{1,0:T(8,128)}, bf16[2,320,1024]{2,1,0:T(8,128)(2,1)}) custom-call(s32[12]{0:T(128)} %compare_select_fusion.1.meta, bf16[8,1280,128]{2,1,0:T(8,128)(2,1)} %get-tuple-element.52.q_ref, ...), custom_call_target="tpu_custom_call" | custom-call | tf_op jit(solution)/shard_map/backward/pallas_call | solution.py:1360
  455.6 39.0 %project_back.1 = (bf16[1024,2048]{1,0:T(8,128)(2,1)}, bf16[1024,1024]{1,0:T(8,128)(2,1)}, bf16[1024,1024]{1,0:T(8,128)(2,1)}, bf16[640,1024]{1,0:T(8,128)(2,1)S...) custom-call(f32[8,1280,128]{2,1,0:T(8,128)} %get-tuple-element.67.dq_ref, ...), custom_call_target="tpu_custom_call" | custom-call | tf_op jit(solution)/shard_map/project_back/pallas_call | solution.py:469
  494.6 1.1 copy-done.7
  496.4 1.6 copy-done.5
  498.0 1.3 copy-done.8
  499.3 69.7 %scatter_end.1 = (f32[32,2048]{1,0:T(8,128)S(1)}, f32[32,1024]{1,0:T(8,128)S(1)}, f32[32,1024]{1,0:T(8,128)S(1)}, f32[32,128]{1,0:T(8,128)S(1)}, bf16[2,320,1024]{2,1,0:T(8,128)(2,1)S(1)}) custom-call(bf16[2,2,4,2,32,2048]{5,4,3,2,1,0:T(8,128)(2,1)} %bitcast.50, bf16[2,2,4,2,32,1024]{5,4,3,2,1,0:T(8,128)(2,1)S(1)} %bitcast.43, ...), custom_call_target="tpu_custom_call" | custom-call | tf_op jit(solution)/shard_map/scatter_end/pallas_call | solution.py:1495
  570.7 0.8 copy.60
  571.5 0.8 copy.59
  572.3 0.8 copy.58
  573.0 1.8 convert_element_type.26
  574.9 1.1 copy.72
  (82 shorter events, 16.7 us)
Async XLA Ops:
  0.6 0.7 copy-start
  0.7 11.2 %copy-start.15 = (bf16[3072,32]{0,1:T(8,128)(2,1)S(1)}, bf16[3072,32]{0,1:T(8,128)(2,1)}, u32[]{:S(2)}) copy-start(bf16[3072,32]{0,1:T(8,128)(2,1)} %param.31) | copy-start | bytes 589828
  0.7 11.2 %copy-start.14 = (bf16[32,3072]{1,0:T(8,128)(2,1)S(1)}, bf16[32,3072]{1,0:T(8,128)(2,1)}, u32[]{:S(2)}) copy-start(bf16[32,3072]{1,0:T(8,128)(2,1)} %param.30) | copy-start | bytes 589828
  232.1 102.8 %copy-start.11 = (f32[1280,128]{1,0:T(8,128)S(1)}, f32[1280,128]{1,0:T(8,128)}, u32[]{:S(2)}) copy-start(f32[1280,128]{1,0:T(8,128)} %get-tuple-element.61) | copy-start | bytes 1966084
  335.8 119.8 %copy-start.2 = (bf16[2,320,1024]{2,1,0:T(8,128)(2,1)S(1)}, bf16[2,320,1024]{2,1,0:T(8,128)(2,1)}, u32[]{:S(2)}) copy-start(bf16[2,320,1024]{2,1,0:T(8,128)(2,1)} %get-tuple-element.53) | copy-start | bytes 3932164
  335.8 119.8 %copy-start.3 = (f32[640,128]{1,0:T(8,128)S(1)}, f32[640,128]{1,0:T(8,128)}, u32[]{:S(2)}) copy-start(f32[640,128]{1,0:T(8,128)} %pad_maximum_fusion.cos_ref) | copy-start | bytes 983044
  335.8 119.8 %copy-start.4 = (f32[640,128]{1,0:T(8,128)S(1)}, f32[640,128]{1,0:T(8,128)}, u32[]{:S(2)}) copy-start(f32[640,128]{1,0:T(8,128)} %pad_maximum_fusion.1.sin_ref) | copy-start | bytes 983044
  335.8 119.8 %copy-start.6 = (bf16[640,1024]{1,0:T(8,128)(2,1)S(1)}, bf16[640,1024]{1,0:T(8,128)(2,1)}, u32[]{:S(2)}) copy-start(bf16[640,1024]{1,0:T(8,128)(2,1)} %get-tuple-element.70.normed_ref) | copy-start | bytes 3932164
  494.6 1.1 copy-start.7
  496.4 1.6 copy-start.5
  498.0 1.3 copy-start.8
  499.3 71.2 %copy-start.10 = (f32[4,32,1536]{2,1,0:T(8,128)S(1)}, f32[4,32,1536]{2,1,0:T(8,128)}, u32[]{:S(2)}) copy-start(f32[4,32,1536]{2,1,0:T(8,128)} %get-tuple-element.87) | copy-start | bytes 2359300
  499.3 71.2 %copy-start.12 = (f32[2,32,1536]{2,1,0:T(8,128)S(1)}, f32[2,32,1536]{2,1,0:T(8,128)}, u32[]{:S(2)}) copy-start(f32[2,32,1536]{2,1,0:T(8,128)} %get-tuple-element.88) | copy-start | bytes 1179652
  573.0 1.8 copy-start.9
  573.0 5.6 copy-start.1
  574.9 3.1 copy-start.13

commit v5 on v4

--- a/solution.py
+++ b/solution.py
@@ -24,7 +24,8 @@
 FF_CHUNK = 512
 PAIRS = KV_HEADS // 2
 FF_CHUNKS = FF // FF_CHUNK
-FF_EARLY = 4
+FF_EARLY = 3
+FF_FIRST = 4
 LOCAL_RUNS = 3
 MIB = 1024 * 1024
 
@@ -342,7 +343,10 @@
         total = self.sums[y, x, z].astype(F32)
         for p in range(self.got[2].shape[0]):
             total = total + self.got[2][p].astype(F32)
-        self.out[:, self.cols] = total
+        if callable(self.out):
+            self.out(total)
+        else:
+            self.out[:, self.cols] = total
 
     @staticmethod
     def copies(sizes):
@@ -362,41 +366,61 @@
 
 ORDERS = ("xy", "yx")
 
-FORWARD_START = [("swap", "tokens"), (0, 2), (0, 0), (1, 0), (0, 1), (1, 1), (1, 2), (0, 11), (2, 1), (1, 11), (2, 11), (0, 10), (2, 0), (0, 3), (3, 11), (0, 5), (3, 1), (0, 6), (3, 0), (2, 2), ("swapped", "tokens"), (4, 11), (0, 8)]
+FORWARD_START = [
+    (0, 9), (0, 0), (0, 1), (1, 9), (1, 0), ("swap", "tokens"), (2, 9), (2, 0), (1, 1), (3, 9), (4, 9), (3, 0),
+    (2, 1), (0, 2), ("swapped", "tokens"), (1, 2),
+]
 FORWARD_AFTER = {
-    0: [(1, 3), (3, 2), ("kv", 0), (2, 3), (1, 10)],
-    1: [(1, 5), (1, 8), (2, 10), (1, 6), ("kv", 1), ("use", 0), (3, 3), (0, 7)],
-    3: [(0, 4), (1, 7), (2, 6), ("got", 0)],
-    4: [("use", 1), (2, 8), ("kv", 2)],
-    5: [("got", 1), (1, 4)],
-    6: [("kv", 3), (3, 6), (2, 5), (0, 9), (2, 7), ("use", 2), (3, 10)],
-    7: [("got", 2)],
-    8: [(3, 8), (1, 9), (2, 4), ("swap", "cot")],
-    9: [("use", 3), (3, 7), ("got", 3)],
-    10: [(2, 9), (3, 5)],
-    11: [(3, 4), (3, 9), ("swapped", "cot")],
+    0: [("kv", 0), (3, 1), (2, 2), (0, 3), (0, 4)],
+    1: [("kv", 1), (3, 2), (1, 3), (1, 4), (0, 5)],
+    2: [("use", 0), (2, 3), (2, 4), (1, 5), (0, 6), (3, 3)],
+    3: [("got", 0), ("kv", 2), (3, 4), (2, 5), (1, 6)],
+    4: [("use", 1), ("got", 1), ("kv", 3), (3, 5), (2, 6), (0, 7)],
+    5: [(1, 7)],
+    6: [("use", 2), (3, 6), (2, 7), (0, 8)],
+    7: [("got", 2), (1, 8), ("swap", "cot")],
+    8: [("use", 3), (3, 7), (2, 8)],
+    9: [("got", 3)],
+    10: [(3, 8)],
+    11: [("swapped", "cot")],
 }
+FEED_START = [("fetch", 0), ("send", (0, 4)), ("fetch", 1)]
+FEED_NEXT = [("send", (1, 4)), ("send", (0, 5))]
 FEED_MIDDLE = {
+    0: [("send", (2, 4))],
+    1: [("send", (3, 4)), ("send", (2, 5)), ("fetch", 2)],
+    2: [("send", (3, 5)), ("fetch", 3)],
+    3: [(1, 0), ("fetch", 4)],
+    4: [(1, 1), ("fetch", 5)],
+    5: [(1, 2)],
+}
+FEED_AFTER = {
+    0: [("send", (1, 5)), ("core", 0)],
+    1: [("begin", 0), ("core", 1)],
+    2: [(0, 0), ("begin", 1), ("core", 2)],
+    3: [(0, 1), ("begin", 2)],
+    4: [(0, 2)],
+}
+FEED_LAST = []
+FINISH_MIDDLE = {
     1: [("begin", 0)],
     2: [("begin", 1), (1, 0)],
     3: [("begin", 2), (1, 1)],
-    4: [("begin", 3), (1, 2)],
-    5: [(1, 3)],
 }
-FEED_AFTER = {
+FINISH_AFTER = {
     0: [("core", 0)],
     1: [("core", 1), (0, 0)],
     2: [("core", 2), (0, 1)],
-    3: [("core", 3), (0, 2)],
-    4: [(0, 3)],
+    3: [("core", 3)],
 }
-FEED_LAST = []
 BACKWARD_AFTER = {
     0: [(0, 0)],
     1: [(1, 0), (0, 1)],
-    2: [(2, 0), (1, 1), (0, 2)],
-    3: [(2, 1), (1, 2)],
-    4: [(2, 2)],
+    2: [(2, 0), (1, 1)],
+    3: [(2, 1), (0, 2)],
+    4: [(1, 2), (0, 3)],
+    5: [(2, 2), (1, 3)],
+    6: [(2, 3)],
 }
 
 
@@ -406,98 +430,6 @@
 
 def roll_half(values):
     return pltpu.roll(values, HEAD_DIM // 2, 1)
-
-
-def project_back_kernel(
-    rows, dq_ref, dkv_ref, pre_ref, normed_ref, x_ref, hid_ref, gain_ref, wq_ref, wk_ref, wv_ref, qg_ref, kg_ref, cos_ref, sin_ref,
-    dwq_ref, dwk_ref, dwv_ref, dx_ref, in_ref, qk_ref, normed_t, grads,
-):
-    sub = rows // SUBS
-    head = pl.program_id(0)
-
-    @pl.when(head == 0)
-    def _():
-        normed_t[...] = normed_ref[...].astype(F32).T.astype(BF16)
-        grads[...] = jnp.zeros_like(grads)
-        qk_ref[...] = jnp.zeros_like(qk_ref)
-
-    cosine, sine = cos_ref[...], sin_ref[...]
-
-    def back(turned_grad, pre, gain):
-        grad = turned_grad * cosine - roll_half(turned_grad) * sine
-        factor = norm_factor(pre)
-        grad_pre, part = norm_backward(grad, gain, pre * factor, factor)
-        return grad_pre.astype(BF16), jnp.sum(part, axis=0, keepdims=True)
-
-    pieces = []
-    for h in range(2):
-        grad = jnp.concatenate(
-            [dq_ref[0, (2 * s + h) * sub : (2 * s + h + 1) * sub] for s in range(2 * SUBS)], axis=0
-        )
-        low, part = back(grad, pre_ref[0, :, h * HEAD_DIM : (h + 1) * HEAD_DIM], qg_ref[...])
-        qk_ref[0:1] += part
-        pieces.append(low)
-    low, part = back(dkv_ref[0, 0].reshape(2 * rows, HEAD_DIM), pre_ref[0, :, 2 * HEAD_DIM :], kg_ref[...])
-    qk_ref[1:2] += part
-    pieces.append(low)
-    pieces.append(dkv_ref[1, 0].reshape(2 * rows, HEAD_DIM).astype(BF16))
-    low = jnp.concatenate(pieces, axis=1)
-    weights = jnp.concatenate([wq_ref[0], wk_ref[0], wv_ref[0]], axis=1)
-    grads[...] += nt(low, weights)
-    part = matmul(normed_t[...], low).astype(BF16)
-    dwq_ref[...] = part[:, : 2 * HEAD_DIM]
-    dwk_ref[...] = part[:, 2 * HEAD_DIM : 3 * HEAD_DIM]
-    dwv_ref[...] = part[:, 3 * HEAD_DIM :]
-
-    @pl.when(head == KV_HEADS - 1)
-    def _():
-        values = x_ref[...].astype(F32)
-        factor = norm_factor(values)
-        grad_in, part = norm_backward(grads[...], gain_ref[...], values * factor, factor)
-        dx_ref[...] = (hid_ref[...] + grad_in).astype(BF16)
-        in_ref[...] = jnp.sum(part, axis=0, keepdims=True)
-
-
-def project_back(dq, dkv, pre, normed, x, grad_hidden, gain, qkv_full, query_gain, key_gain, cosine, sine):
-    count = x.shape[0]
-    rows = count // 2
-    full = pl.BlockSpec((count, D), lambda h: (0, 0))
-    row = lambda n: pl.BlockSpec((1, n), lambda h: (0, 0))
-    table = pl.BlockSpec((count, HEAD_DIM), lambda h: (0, 0))
-    wide = pl.BlockSpec((D, 2 * HEAD_DIM), lambda h: (0, h))
-    thin = pl.BlockSpec((D, HEAD_DIM), lambda h: (0, h))
-    return pl.pallas_call(
-        functools.partial(project_back_kernel, rows),
-        grid=(KV_HEADS,),
-        out_shape=[
-            jax.ShapeDtypeStruct((D, QD), BF16),
-            jax.ShapeDtypeStruct((D, KVD), BF16),
-            jax.ShapeDtypeStruct((D, KVD), BF16),
-            jax.ShapeDtypeStruct((count, D), BF16),
-            jax.ShapeDtypeStruct((1, D), F32),
-            jax.ShapeDtypeStruct((8, HEAD_DIM), F32),
-        ],
-        in_specs=[
-            pl.BlockSpec((1, 2 * count, HEAD_DIM), lambda h: (h, 0, 0)),
-            pl.BlockSpec((2, 1, 2, rows, HEAD_DIM), lambda h: (0, h, 0, 0, 0)),
-            pl.BlockSpec((1, count, 3 * HEAD_DIM), lambda h: (h, 0, 0)),
-            full,
-            full,
-            full,
-            row(D),
-            pl.BlockSpec((1, D, 2 * HEAD_DIM), lambda h: (h // 2, 0, h % 2)),
-            pl.BlockSpec((1, D, HEAD_DIM), lambda h: (h // 2, 0, 4 + h % 2)),
-            pl.BlockSpec((1, D, HEAD_DIM), lambda h: (h // 2, 0, 6 + h % 2)),
-            row(HEAD_DIM),
-            row(HEAD_DIM),
-            table,
-            table,
-        ],
-        out_specs=[wide, thin, thin, full, row(D), pl.BlockSpec((8, HEAD_DIM), lambda h: (0, 0))],
-        scratch_shapes=[pltpu.VMEM((D, count), BF16), pltpu.VMEM((count, D), F32)],
-        compiler_params=pltpu.CompilerParams(vmem_limit_bytes=48 * MIB),
-        name="project_back",
-    )(dq, dkv, pre, normed, x, grad_hidden, gain, qkv_full, qkv_full, qkv_full, query_gain, key_gain, cosine, sine)
 
 
 class KeyValues:
@@ -557,6 +489,16 @@
 def row_places(shape, dim, sub):
     t = lax.broadcasted_iota(jnp.int32, shape, dim)
     return (t // (2 * sub)) * sub + t % sub
+
+
+def block_copies(sizes, src, dst, sem):
+    ny, nx, nz = sizes
+    shard_rows = src.shape[-2]
+    found = []
+    for i in range(ny * nx * nz * 2):
+        block = src.at[i // (nx * nz * 2), i // (nz * 2) % nx, i // 2 % nz, i % 2]
+        found.append(pltpu.make_async_copy(block, dst.at[i * shard_rows : (i + 1) * shard_rows], sem))
+    return found
 
 
 def gather_parents(meta, lead, slot, pairs):
@@ -573,14 +515,14 @@
 
 
 def forward_kernel(sizes, rows, meta, cos_ref, sin_ref, tok_ref, cot_ref, *refs):
-    arrays = PAIRS + 2 + FF_CHUNKS
+    arrays = PAIRS + 2 + FF_FIRST
     shard = refs[:arrays]
     (mixed_ref, l_ref, pre_ref, normed_ref, gains_ref, qk_ref,
      placed, cot_placed, q_all, kv_all, qkv_whole, gain_whole, out_whole, feed_whole) = refs[arrays : arrays + 14]
     whole = (
         tuple(qkv_whole.at[c] for c in range(PAIRS))
         + (out_whole,)
-        + tuple(feed_whole.at[c] for c in range(FF_CHUNKS))
+        + tuple(feed_whole.at[c] for c in range(FF_FIRST))
         + (gain_whole,)
     )
     (qs, kvs, xs, ws, gs, acc, part, places, kp, vp, send_sem, recv_sem, local_sem) = refs[arrays + 14 :]
@@ -611,18 +553,6 @@
             pltpu.make_async_copy(kvs.at[:, pair], kv_all.at[:, pair], local_sem.at[2 + group]),
             pltpu.make_async_copy(qs.at[pair], q_all.at[pair], local_sem.at[6 + group]),
         ]
-
-    def fetch(src, dst):
-        ny, nx, nz = sizes
-        shard_rows = src.shape[4]
-        copies = []
-        for i in range(ny * nx * nz * 2):
-            block = src.at[i // (nx * nz * 2), i // (nz * 2) % nx, i // 2 % nz, i % 2]
-            copies.append(
-                pltpu.make_async_copy(block, dst.at[i * shard_rows : (i + 1) * shard_rows], local_sem.at[10])
-            )
-        run_all(copies, "start")
-        pltpu.make_async_copy(dst, dst, local_sem.at[10]).wait()
 
     def act(steps):
         for what, a in steps:
@@ -655,7 +585,8 @@
         act(FORWARD_START)
         l_ref[...] = jnp.zeros_like(l_ref)
         places[...] = row_places(places.shape, 0, sub)
-        fetch(gain_whole, gs)
+        run_all(block_copies(sizes, gain_whole, gs, local_sem.at[10]), "start")
+        pltpu.make_async_copy(gs, gs, local_sem.at[10]).wait()
         loaded = pltpu.make_async_copy(placed, xs, local_sem.at[11])
         loaded.start()
         gains_ref[...] = gs[:, :GAIN_COLS].astype(F32).T[:8]
@@ -670,7 +601,8 @@
         @pl.when(step == c)
         def _():
             act([(4, c)])
-            fetch(qkv_whole.at[c], ws)
+            run_all(block_copies(sizes, qkv_whole.at[c], ws, local_sem.at[10]), "start")
+            pltpu.make_async_copy(ws, ws, local_sem.at[10]).wait()
 
     @pl.when(step < PAIRS)
     def _():
@@ -785,7 +717,7 @@
 
     @pl.when(step == PAIRS + KV_HEADS - 1)
     def _():
-        for array in weights_[PAIRS : PAIRS + 1 + FF_CHUNKS]:
+        for array in weights_[PAIRS : PAIRS + 1 + FF_FIRST]:
             for g in array:
                 g.close()
         for group in range(4):
@@ -796,7 +728,7 @@
     ny, nx, nz = sizes
     rows = tokens.shape[1]
     count = 2 * rows
-    arrays = PAIRS + 2 + FF_CHUNKS
+    arrays = PAIRS + 2 + FF_FIRST
     shard_rows = shards_[0].shape[0]
     blocks = (ny, nx, nz, 2, shard_rows)
     widths = [w.shape[-1] for w in shards_]
@@ -821,7 +753,7 @@
             jax.ShapeDtypeStruct((PAIRS,) + blocks + (widths[0],), BF16),
             jax.ShapeDtypeStruct(blocks + (widths[-1],), BF16),
             jax.ShapeDtypeStruct(blocks + (widths[PAIRS],), BF16),
-            jax.ShapeDtypeStruct((FF_CHUNKS,) + blocks + (widths[PAIRS + 1],), BF16),
+            jax.ShapeDtypeStruct((FF_FIRST,) + blocks + (widths[PAIRS + 1],), BF16),
         ],
         grid_spec=pltpu.PrefetchScalarGridSpec(
             num_scalar_prefetch=1,
@@ -861,11 +793,13 @@
 
 
 def feed_kernel(
-    sizes, rows, x_ref, mixed_ref, cot_ref, out_ref, gain_ref, w_ref,
-    result_ref, hid_ref, stack_ref, delta_ref, post_ref, dout_ref, late_ref, early_ref, *refs,
+    sizes, rows, x_ref, mixed_ref, cot_ref, out_ref, gain_ref, first_ref, *refs,
 ):
-    hidden, second, second_t, cot_t, total, grads, inner, gate_up, low, stack, part = refs[:11]
-    buffers = refs[11:-3]
+    shard = refs[: FF_CHUNKS - FF_FIRST]
+    refs = refs[FF_CHUNKS - FF_FIRST :]
+    result_ref, hid_ref, stack_ref, delta_ref, post_ref, dout_ref, late_ref, rest_ref, early_ref = refs[:9]
+    hidden, second, second_t, cot_t, total, grads, inner, gate_up, low, stack, part, wbuf = refs[9:21]
+    buffers = refs[21:-3]
     send_sem, recv_sem, local_sem = refs[-3:]
     ny, nx, nz = sizes
     count = 2 * rows
@@ -894,8 +828,36 @@
                 )
             )
 
+    gathers = [
+        [
+            Gather(links, ("w", c, b), shard[c], rest_ref.at[c], ORDERS[b], cols, local_sem.at[8 + 2 * c + b])
+            for b, cols in enumerate(halves_of(width))
+        ]
+        for c in range(FF_CHUNKS - FF_FIRST)
+    ]
+
+    def fetch(c):
+        if c < FF_FIRST:
+            pltpu.make_async_copy(first_ref.at[c], wbuf.at[c % 2], local_sem.at[6 + c % 2]).start()
+        else:
+            for g in gathers[c - FF_FIRST]:
+                g.close()
+            run_all(
+                block_copies(sizes, rest_ref.at[c - FF_FIRST], wbuf.at[c % 2], local_sem.at[6 + c % 2]), "start"
+            )
+
     def act(steps):
         for what, c in steps:
+            if what == "fetch":
+                fetch(c)
+                continue
+            if what == "send":
+                for g in gathers[c[1] - FF_FIRST]:
+                    if c[0] == 0:
+                        g.start()
+                    else:
+                        g.step(c[0])
+                continue
             for s in scatters[2 * c : 2 * c + 2]:
                 if what == "core":
                     s.start()
@@ -920,6 +882,7 @@
     @pl.when(chunk == 0)
     def _():
         links.meet()
+        act(FEED_START)
 
         def project_out(t, carry):
             at = pl.multiple_of(t * tile, tile)
@@ -929,6 +892,7 @@
             return carry
 
         lax.fori_loop(0, D // tile, project_out, 0)
+        act(FEED_NEXT)
         values = hidden[...]
         values = values * norm_factor(values) * gain_ref[...]
         second[...] = values.astype(BF16)
@@ -938,12 +902,13 @@
         grads[...] = jnp.zeros_like(grads)
 
     slot = lax.rem(chunk, 2)
+    pltpu.make_async_copy(wbuf.at[slot], wbuf.at[slot], local_sem.at[6 + slot]).wait()
 
     def columns(t, carry):
         at = pl.multiple_of(t * tile, tile)
-        gate = matmul(second[...], w_ref[0, :, pl.ds(at, tile)])
-        up = matmul(second[...], w_ref[0, :, pl.ds(FF_CHUNK + at, tile)])
-        grad = matmul(cot_ref[...], w_ref[0, :, pl.ds(2 * FF_CHUNK + at, tile)])
+        gate = matmul(second[...], wbuf[slot, :, pl.ds(at, tile)])
+        up = matmul(second[...], wbuf[slot, :, pl.ds(FF_CHUNK + at, tile)])
+        grad = matmul(cot_ref[...], wbuf[slot, :, pl.ds(2 * FF_CHUNK + at, tile)])
         sigmoid = 1.0 / (1.0 + jnp.exp(-gate))
         active = gate * sigmoid
         inner[:, pl.ds(at, tile)] = (active * up).astype(BF16)
@@ -959,8 +924,8 @@
 
     def model(t, carry):
         at = pl.multiple_of(t * tile, tile)
-        total[:, pl.ds(at, tile)] += nt(inner[...], w_ref[0, pl.ds(at, tile), 2 * FF_CHUNK :])
-        grads[:, pl.ds(at, tile)] += nt(gate_up[...], w_ref[0, pl.ds(at, tile), : 2 * FF_CHUNK])
+        total[:, pl.ds(at, tile)] += nt(inner[...], wbuf[slot, pl.ds(at, tile), 2 * FF_CHUNK :])
+        grads[:, pl.ds(at, tile)] += nt(gate_up[...], wbuf[slot, pl.ds(at, tile), : 2 * FF_CHUNK])
         put(slot, at, slice(0, 2 * FF_CHUNK), matmul(second_t[pl.ds(at, tile)], gate_up[...]))
         put(slot, at, slice(2 * FF_CHUNK, width), matmul(cot_t[pl.ds(at, tile)], inner[...]))
         return carry
@@ -1028,7 +993,7 @@
         run_all(gone + [output, saved, stacked_], "wait")
 
 
-def feed(sizes, x, mixed, cot, out_t, gain, feed_whole):
+def feed(sizes, x, mixed, cot, out_t, gain, first, shards_):
     ny, nx, nz = sizes
     count = x.shape[0]
     rows = count // 2
@@ -1038,7 +1003,8 @@
     for c in range(FF_EARLY):
         for b, cols in enumerate(halves_of(width)):
             buffers += Scatter.scratch(sizes, ORDERS[b], shard_rows, cols.stop - cols.start)
-    rounds = 2 * FF_EARLY * Scatter.copies(sizes)
+    late = FF_CHUNKS - FF_FIRST
+    rounds = 2 * FF_EARLY * Scatter.copies(sizes) + 2 * late * Gather.copies(sizes)
 
     def whole_block(shape):
         return pl.BlockSpec(shape, lambda c: (0,) * len(shape), pipeline_mode=pl.Buffered(1))
@@ -1055,6 +1021,7 @@
             jax.ShapeDtypeStruct((1, D), F32),
             jax.ShapeDtypeStruct(blocks + (QD,), BF16),
             jax.ShapeDtypeStruct((FF_CHUNKS - FF_EARLY,) + blocks + (width,), BF16),
+            jax.ShapeDtypeStruct((late,) + blocks + (width,), BF16),
             jax.ShapeDtypeStruct((FF_EARLY, shard_rows, width), F32),
         ],
         in_specs=[
@@ -1063,14 +1030,16 @@
             whole_block((count, D)),
             whole_block((D, QD)),
             whole_block((1, D)),
-            pl.BlockSpec((1, D, width), lambda c: (c, 0, 0)),
-        ],
+            ANY,
+        ]
+        + [ANY] * late,
         out_specs=[
             ANY,
             ANY,
             ANY,
             pl.BlockSpec((HEAD_DIM, count), lambda c: (0, 0)),
             pl.BlockSpec((1, D), lambda c: (0, 0)),
+            ANY,
             ANY,
             ANY,
             pl.BlockSpec((FF_EARLY, shard_rows, width), lambda c: (0, 0, 0)),
@@ -1087,18 +1056,19 @@
             pltpu.VMEM((count, D), BF16),
             pltpu.VMEM((KV_HEADS, 2 * count, HEAD_DIM), BF16),
             pltpu.VMEM((2,) + blocks + (width,), BF16),
+            pltpu.VMEM((2, D, width), BF16),
         ]
         + buffers
         + [
             pltpu.SemaphoreType.DMA((rounds,)),
             pltpu.SemaphoreType.DMA((rounds,)),
-            pltpu.SemaphoreType.DMA((5,)),
+            pltpu.SemaphoreType.DMA((8 + 2 * late,)),
         ],
         compiler_params=pltpu.CompilerParams(
             collective_id=5, has_side_effects=True, vmem_limit_bytes=61 * MIB
         ),
         name="feed",
-    )(x, mixed, cot, out_t, gain, feed_whole)
+    )(x, mixed, cot, out_t, gain, first, *shards_)
 
 
 def backward_kernel(sizes, rows, widths, meta, q_ref, g_ref, k_ref, v_ref, lse_ref, del_ref, late_ref, dout_ref, done_ref, *refs):
@@ -1426,90 +1396,214 @@
     )
 
 
-def scatter_kernel(sizes, widths, *refs):
-    count = len(widths)
-    parts = refs[:count]
-    moved_ref = refs[count]
-    outs = refs[count + 1 : 2 * count + 1]
-    placed_ref = refs[2 * count + 1]
-    rest = refs[2 * count + 2 :]
-    send_sem, recv_sem, local_sem = rest[-3:]
+def finish_kernel(
+    sizes, rows, dq_ref, dkv_ref, pre_ref, w_ref, normed_ref, x_ref, hid_ref, gain_ref, post_ref, qg_ref, kg_ref, cos_ref, sin_ref,
+    q_out, k_out, v_out, g_out, dx_placed, *refs,
+):
+    normed_t, low, grads, qk, dx, part, part_g = refs[:7]
+    buffers = refs[7:-3]
+    send_sem, recv_sem, local_sem = refs[-3:]
+    ny, nx, nz = sizes
+    count = 2 * rows
+    sub = rows // SUBS
+    shard_rows = part.shape[5]
+    tile = 256
+    pair = pl.program_id(0)
     links = Links(sizes, send_sem, recv_sem)
+    _, _, _, core = links.place()
+    swap = Exchange(links, dx, dx_placed, local_sem.at[0])
+
+    def to_query(c):
+        def store(total):
+            q_out[:, 4 * HEAD_DIM * c : 4 * HEAD_DIM * (c + 1)] = total
+
+        return store
+
+    def to_key_value(c):
+        def store(total):
+            k_out[:, 2 * HEAD_DIM * c : 2 * HEAD_DIM * (c + 1)] = total[:, : 2 * HEAD_DIM]
+            v_out[:, 2 * HEAD_DIM * c : 2 * HEAD_DIM * (c + 1)] = total[:, 2 * HEAD_DIM :]
+
+        return store
+
     scatters = []
-    used = 0
-    for a in range(count):
-        for b, cols in enumerate(halves_of(widths[a])):
-            k = 5 * used
+    for c in range(PAIRS):
+        for b, cols in enumerate(halves_of(8 * HEAD_DIM)):
+            k = 4 * len(scatters)
             scatters.append(
                 Scatter(
                     links,
-                    (a, b),
-                    parts[a],
+                    (c, b),
+                    part.at[c % 2],
                     ORDERS[b],
                     cols,
-                    *rest[k : k + 4],
-                    rest[k + 4],
-                    local_sem.at[used],
-                    outs[a],
+                    *buffers[k : k + 4],
+                    part.at[c % 2, :, :, :, core, :, cols],
+                    None,
+                    to_key_value(c) if b else to_query(c),
                 )
             )
-            used += 1
-    for s in scatters:
-        s.load().start()
-    links.meet()
-    for s in scatters:
-        s.start()
-    _, _, z, _ = links.place()
-    half = z // (sizes[2] // 2)
-    keep = pltpu.make_async_copy(moved_ref.at[half], placed_ref.at[half], local_sem.at[used])
-    give = links.copy("moved", moved_ref.at[1 - half], placed_ref.at[half], links.across())
-    keep.start()
-    give.start()
-    depth = 2
-    for i, s in enumerate(scatters):
-        if i >= depth:
-            scatters[i - depth].middle(0)
-        s.begin()
-    for s in scatters[-depth:]:
-        s.middle(0)
-    for s in scatters:
-        s.middle(1)
-    for s in scatters:
-        s.finish()
-    keep.wait()
-    give.wait()
-
-
-def scatter_end(sizes, parts, moved):
+    k = 4 * len(scatters)
+    whole = slice(0, 3 * GAIN_COLS)
+    scatters.append(
+        Scatter(
+            links, "gains", part_g, ORDERS[0], whole, *buffers[k : k + 4], part_g.at[:, :, :, core], None, g_out
+        )
+    )
+
+    def act(steps):
+        for what, c in steps:
+            for s in scatters[2 * c : 2 * c + 2]:
+                if what == "core":
+                    s.start()
+                elif what == "begin":
+                    s.begin()
+                elif what == "finish":
+                    s.finish()
+                else:
+                    s.middle(what)
+
+    def rows_of(block):
+        return (block // (2 * nz * nx), lax.rem(block // (2 * nz), nx), lax.rem(block // 2, nz), lax.rem(block, 2))
+
+    @pl.when(pair == 0)
+    def _():
+        links.meet()
+        normed_t[...] = normed_ref[...].astype(F32).T.astype(BF16)
+        grads[...] = jnp.zeros_like(grads)
+        qk[...] = jnp.zeros_like(qk)
+
+    cosine, sine = cos_ref[...], sin_ref[...]
+
+    def back(turned_grad, pre, gain):
+        grad = turned_grad * cosine - roll_half(turned_grad) * sine
+        factor = norm_factor(pre)
+        grad_pre, share = norm_backward(grad, gain, pre * factor, factor)
+        return grad_pre.astype(BF16), jnp.sum(share, axis=0, keepdims=True)
+
+    for hh in range(2):
+        for h in range(2):
+            grad = jnp.concatenate(
+                [dq_ref[hh, (2 * s + h) * sub : (2 * s + h + 1) * sub] for s in range(2 * SUBS)], axis=0
+            )
+            value, share = back(grad, pre_ref[hh, :, h * HEAD_DIM : (h + 1) * HEAD_DIM], qg_ref[...])
+            qk[0:1] += share
+            at = 2 * hh + h
+            low[:, at * HEAD_DIM : (at + 1) * HEAD_DIM] = value
+        value, share = back(dkv_ref[0, hh].reshape(count, HEAD_DIM), pre_ref[hh, :, 2 * HEAD_DIM :], kg_ref[...])
+        qk[1:2] += share
+        low[:, (4 + hh) * HEAD_DIM : (5 + hh) * HEAD_DIM] = value
+        low[:, (6 + hh) * HEAD_DIM : (7 + hh) * HEAD_DIM] = dkv_ref[1, hh].reshape(count, HEAD_DIM).astype(BF16)
+    for moment, steps in FINISH_MIDDLE.items():
+        pl.when(pair == moment)(functools.partial(act, steps))
+    slot = lax.rem(pair, 2)
+
+    def model(t, carry):
+        at = pl.multiple_of(t * tile, tile)
+        grads[:, pl.ds(at, tile)] += nt(low[...], w_ref[0, pl.ds(at, tile), :])
+        value = matmul(normed_t[pl.ds(at, tile)], low[...])
+        for k in range(tile // shard_rows):
+            y, x, z, c = rows_of(at // shard_rows + k)
+            part[slot, y, x, z, c] = value[k * shard_rows : (k + 1) * shard_rows].astype(BF16)
+        return carry
+
+    lax.fori_loop(0, D // tile, model, 0)
+    for moment, steps in FINISH_AFTER.items():
+        pl.when(pair == moment)(functools.partial(act, steps))
+
+    @pl.when(pair == PAIRS - 1)
+    def _():
+        values = x_ref[...].astype(F32)
+        factor = norm_factor(values)
+        grad_in, share = norm_backward(grads[...], gain_ref[...], values * factor, factor)
+        dx[...] = (hid_ref[...] + grad_in).astype(BF16).reshape(2, rows, D)
+        swap.start()
+        act([(0, PAIRS - 2), ("begin", PAIRS - 1)])
+        lines = jnp.concatenate(
+            [jnp.sum(share, axis=0, keepdims=True), post_ref[...], jnp.zeros((GAIN_COLS - 2, D), F32)], axis=0
+        )
+        columns = lines.T.astype(BF16)
+        first = lax.broadcasted_iota(jnp.int32, (shard_rows, GAIN_COLS), 0) == 0
+        query_line = jnp.where(first, qk[0:1], 0.0).astype(BF16)
+        key_line = jnp.where(first, qk[1:2], 0.0).astype(BF16)
+        for k in range(D // shard_rows):
+            y, x, z, c = k // (2 * nz * nx), k // (2 * nz) % nx, k // 2 % nz, k % 2
+            part_g[y, x, z, c, :, :GAIN_COLS] = columns[k * shard_rows : (k + 1) * shard_rows]
+            part_g[y, x, z, c, :, GAIN_COLS : 2 * GAIN_COLS] = query_line
+            part_g[y, x, z, c, :, 2 * GAIN_COLS :] = key_line
+        act([("core", PAIRS), (1, PAIRS - 2), ("begin", PAIRS), (0, PAIRS - 1), (0, PAIRS), (1, PAIRS - 1), (1, PAIRS)])
+        for c in range(PAIRS + 1):
+            act([("finish", c)])
+        swap.wait()
+
+
+def finish(sizes, dq, dkv, pre, normed, x, grad_hidden, gain, post_part, qkv_full, query_gain, key_gain, cosine, sine):
     ny, nx, nz = sizes
+    count = x.shape[0]
+    rows = count // 2
     shard_rows = D // (ny * nx * nz * 2)
-    widths = tuple(p.shape[-1] for p in parts)
-    pieces = [p.reshape(ny, nx, nz, 2, shard_rows, p.shape[-1]) for p in parts]
-    buffers, count = [], 0
-    for w in widths:
-        for b, cols in enumerate(halves_of(w)):
+    blocks = (ny, nx, nz, 2, shard_rows)
+    width = 8 * HEAD_DIM
+
+    def whole_block(shape):
+        return pl.BlockSpec(shape, lambda c: (0,) * len(shape), pipeline_mode=pl.Buffered(1))
+
+    buffers = []
+    for c in range(PAIRS):
+        for b, cols in enumerate(halves_of(width)):
             buffers += Scatter.scratch(sizes, ORDERS[b], shard_rows, cols.stop - cols.start)
-            buffers.append(pltpu.VMEM((ny, nx, nz, shard_rows, cols.stop - cols.start), BF16))
-            count += 1
-    rounds = count * Scatter.copies(sizes) + 1
-    results = pl.pallas_call(
-        functools.partial(scatter_kernel, sizes, widths),
-        out_shape=[jax.ShapeDtypeStruct((shard_rows, w), F32) for w in widths]
-        + [jax.ShapeDtypeStruct(moved.shape, BF16)],
-        in_specs=[ANY] * (len(widths) + 1),
-        out_specs=[pl.BlockSpec(memory_space=pltpu.VMEM)] * len(widths) + [ANY],
-        scratch_shapes=buffers
+    buffers += Scatter.scratch(sizes, ORDERS[0], shard_rows, 3 * GAIN_COLS)
+    rounds = (2 * PAIRS + 1) * Scatter.copies(sizes) + 1
+
+    def out_block(n):
+        return pl.BlockSpec((shard_rows, n), lambda c: (0, 0))
+
+    return pl.pallas_call(
+        functools.partial(finish_kernel, sizes, rows),
+        grid=(PAIRS,),
+        out_shape=[
+            jax.ShapeDtypeStruct((shard_rows, QD), F32),
+            jax.ShapeDtypeStruct((shard_rows, KVD), F32),
+            jax.ShapeDtypeStruct((shard_rows, KVD), F32),
+            jax.ShapeDtypeStruct((shard_rows, 3 * GAIN_COLS), F32),
+            jax.ShapeDtypeStruct((2, rows, D), BF16),
+        ],
+        in_specs=[
+            pl.BlockSpec((2, 2 * count, HEAD_DIM), lambda c: (c, 0, 0)),
+            pl.BlockSpec((2, 2, 2, rows, HEAD_DIM), lambda c: (0, c, 0, 0, 0)),
+            pl.BlockSpec((2, count, 3 * HEAD_DIM), lambda c: (c, 0, 0)),
+            pl.BlockSpec((1, D, width), lambda c: (c, 0, 0)),
+            whole_block((count, D)),
+            whole_block((count, D)),
+            whole_block((count, D)),
+            whole_block((1, D)),
+            whole_block((1, D)),
+            whole_block((1, HEAD_DIM)),
+            whole_block((1, HEAD_DIM)),
+            whole_block((count, HEAD_DIM)),
+            whole_block((count, HEAD_DIM)),
+        ],
+        out_specs=[out_block(QD), out_block(KVD), out_block(KVD), out_block(3 * GAIN_COLS), ANY],
+        scratch_shapes=[
+            pltpu.VMEM((D, count), BF16),
+            pltpu.VMEM((count, width), BF16),
+            pltpu.VMEM((count, D), F32),
+            pltpu.VMEM((8, HEAD_DIM), F32),
+            pltpu.VMEM((2, rows, D), BF16),
+            pltpu.VMEM((2,) + blocks + (width,), BF16),
+            pltpu.VMEM(blocks + (3 * GAIN_COLS,), BF16),
+        ]
+        + buffers
         + [
             pltpu.SemaphoreType.DMA((rounds,)),
             pltpu.SemaphoreType.DMA((rounds,)),
-            pltpu.SemaphoreType.DMA((count + 1,)),
+            pltpu.SemaphoreType.DMA((1,)),
         ],
         compiler_params=pltpu.CompilerParams(
-            collective_id=4, has_side_effects=True, vmem_limit_bytes=48 * MIB
+            collective_id=4, has_side_effects=True, vmem_limit_bytes=58 * MIB
         ),
-        name="scatter_end",
-    )(*pieces, moved)
-    return results[:-1], results[-1]
+        name="finish",
+    )(dq, dkv, pre, qkv_full, normed, x, grad_hidden, gain, post_part, query_gain, key_gain, cosine, sine)
 
 
 def shards(
@@ -1581,7 +1675,7 @@
 
     (mixed, totals, pre, normed, gain_rows_, qk_gains, placed, cot, queries, kv_all,
      qkv_full, _, out_t, feed_whole) = forward(
-        sizes, meta, cosine, sine, tokens, cotangent, qkv_shards + [out_proj.T] + feed_shards + [gains]
+        sizes, meta, cosine, sine, tokens, cotangent, qkv_shards + [out_proj.T] + feed_shards[:FF_FIRST] + [gains]
     )
     x = placed.reshape(count, D)
     cot = cot.reshape(count, D)
@@ -1589,10 +1683,10 @@
     query_weight, key_weight = qk_gains[0:1], qk_gains[1:2]
     qkv_full = qkv_full.reshape(PAIRS, D, -1)
     out_t = out_t.reshape(D, QD)
-    feed_whole = feed_whole.reshape(FF_CHUNKS, D, -1)
+    feed_whole = feed_whole.reshape(FF_FIRST, D, -1)
     log_total = jnp.log2(totals[:, :KV_HEADS]).T
-    result, grad_hidden, grad_stack, delta, post_part, dout, late, early_grad = feed(
-        sizes, x, mixed, cot, out_t, post_weight, feed_whole
+    result, grad_hidden, grad_stack, delta, post_part, dout, late, _, early_grad = feed(
+        sizes, x, mixed, cot, out_t, post_weight, feed_whole, feed_shards[FF_FIRST:]
     )
     delta = delta[:HEADS].reshape(KV_HEADS, 2, 2 * SUBS, sub).transpose(0, 2, 1, 3)
     dq, dkv, late_grad, out_grad, output = backward(
@@ -1604,29 +1698,13 @@
         piece = feed_grad[:, :, k * FF_CHUNK : (k + 1) * FF_CHUNK]
         return piece.transpose(1, 0, 2).reshape(shard_rows, FF)
 
-    dwq, dwk, dwv, dx, in_part, qk_part = project_back(
-        dq, dkv, pre, normed, x, grad_hidden, in_weight, qkv_full, query_weight, key_weight, cosine, sine
+    query_grad, key_grad, value_grad, gain_grad, input_grad = finish(
+        sizes, dq, dkv, pre, normed, x, grad_hidden, in_weight, post_part, qkv_full, query_weight, key_weight, cosine, sine
     )
 
-    def gain_column(values):
-        if values.shape[0] == D:
-            return values[:, None]
-        spread = jnp.pad(values.reshape(-1, gain_rows), ((0, 0), (0, shard_rows - gain_rows)))
-        return spread.reshape(D, 1)
-
-    gain_parts = jnp.concatenate(
-        [
-            gain_column(in_part[0]),
-            gain_column(post_part[0]),
-            gain_column(qk_part[0]),
-            gain_column(qk_part[1]),
-        ],
-        axis=1,
-    )
-    gain_parts = jnp.pad(gain_parts, ((0, 0), (0, GAIN_COLS - 4))).astype(BF16)
-    (query_grad, key_grad, value_grad, gain_grad), input_grad = scatter_end(
-        sizes, [dwq, dwk, dwv, gain_parts], dx.reshape(2, rows, D)
-    )
+    def own(line):
+        return lax.dynamic_slice_in_dim(line, device * gain_rows, gain_rows)
+
     return (
         output,
         input_grad.astype(F32),
@@ -1634,8 +1712,8 @@
         query_grad,
         key_grad,
         value_grad,
-        gain_grad[:gain_rows, 2],
-        gain_grad[:gain_rows, 3],
+        own(gain_grad[0, GAIN_COLS : 2 * GAIN_COLS]),
+        own(gain_grad[0, 2 * GAIN_COLS :]),
         out_grad.T,
         gain_grad[:, 1],
         feed_columns(0),

time: 583 us -> 568 us (0.974)
  Pallas kernels: 542 us -> 530 us
    pallas_call x2 -> x1, Pallas kernels: 109 us -> 87.4 us  [finish(): pl.pallas_call(functools.partial(finish_kernel, sizes, rows), grid=(PAIRS...]
    pallas_call x1, Pallas kernels: 100 us -> 109 us  [feed(): pl.pallas_call(functools.partial(feed_kernel, sizes, rows), grid=(FF_CHUN...]
where the time goes in v5:
time: 568 us; the launch traced here: 564 us
  Pallas kernels  530 us (93%)
  local copies, waits for them, and re-layouts  22.5 us (4%)
  other arithmetic  10.7 us (2%)
    pallas_call x1, Pallas kernels, forward(): pl.pallas_call(functools.partial(forward_kernel, sizes, rows), out_shape=...  211 us
    pallas_call x1, Pallas kernels, backward(): pl.pallas_call(functools.partial(backward_kernel, sizes, rows, widths), o...  122 us
    pallas_call x1, Pallas kernels, feed(): pl.pallas_call(functools.partial(feed_kernel, sizes, rows), grid=(FF_CHUN...  109 us
    pallas_call x1, Pallas kernels, finish(): pl.pallas_call(functools.partial(finish_kernel, sizes, rows), grid=(PAIRS...  87.4 us

profile of v5, /device:TPU:0, one launch (start us, length us, event | category | flops | bytes accessed | tf_op | source)
XLA Modules:
  0.0 563.9 jit_solution(12681880537433298173)
XLA Ops:
  2.0 0.8 dynamic_update_slice.7
  2.8 0.8 dynamic_update_slice.6
  4.3 0.8 dynamic-slice_reduce_fusion
  7.3 0.8 fusion.16
  8.1 0.8 fusion.17
  8.8 0.8 fusion.15
  13.1 1.2 fusion
  14.3 0.9 pad_maximum_fusion.1.sin_ref
  15.2 0.9 pad_maximum_fusion.cos_ref
  16.1 210.6 %forward.1 = (bf16[640,2048]{1,0:T(8,128)(2,1)}, f32[1280,128]{1,0:T(8,128)}, f32[8,640,384]{2,1,0:T(8,128)}, bf16[640,1024]{1,0:T(8,128)(2,1)}, f32[8,1024]{1,0...) custom-call(s32[12]{0:T(128)} %compare_select_fusion.1.meta, ...), custom_call_target="tpu_custom_call" | custom-call | tf_op jit(solution)/shard_map/forward/pallas_call | solution.py:740
  226.7 1.3 fusion.20
  228.0 1.4 fusion.19
  229.4 1.3 copy.47
  231.4 109.3 %feed.1 = (bf16[640,1024]{1,0:T(8,128)(2,1)}, f32[640,1024]{1,0:T(8,128)}, bf16[8,1280,128]{2,1,0:T(8,128)(2,1)}, f32[128,640]{1,0:T(8,128)}, f32[1,1024]{1,0:T(...) custom-call(bf16[640,1024]{1,0:T(8,128)(2,1)} %bitcast.38, ...), custom_call_target="tpu_custom_call" | custom-call | tf_op jit(solution)/shard_map/feed/pallas_call | solution.py:1013
  340.7 0.8 slice.165
  342.4 122.2 %backward.1 = (f32[8,1280,128]{2,1,0:T(8,128)}, f32[2,8,2,320,128]{4,3,2,1,0:T(8,128)}, f32[3,32,1536]{2,1,0:T(8,128)}, f32[32,2048]{1,0:T(8,128)}, bf16[2,320,1024]{2,1,0:T(8,128)(2,1)}) custom-call(s32[12]{0:T(128)} %compare_select_fusion.1.meta, bf16[8,1280,128]{2,1,0:T(8,128)(2,1)} %get-tuple-element.46.q_ref, ...), custom_call_target="tpu_custom_call" | custom-call | tf_op jit(solution)/shard_map/backward/pallas_call | solution.py:1330
  464.6 87.4 %finish.1 = (f32[32,2048]{1,0:T(8,128)}, f32[32,1024]{1,0:T(8,128)}, f32[32,1024]{1,0:T(8,128)}, f32[32,384]{1,0:T(8,128)}, bf16[2,320,1024]{2,1,0:T(8,128)(2,1)}) custom-call(f32[8,1280,128]{2,1,0:T(8,128)} %get-tuple-element.61.dq_ref, f32[2,8,2,320,128]{4,3,2,1,0:T(8,128)} %get-tuple-element.62.dkv_ref, f32[8,640,384]{2,1,0:T(8,128)} %get-tuple-element.63.pre_ref, ...), custom_call_target="tpu_custom_call" | custom-call | tf_op jit(solution)/shard_map/finish/pallas_call | solution.py:1561
  552.0 0.7 fusion.18
  552.8 1.5 slice_reduce_fusion
  555.7 0.8 copy.54
  556.5 0.8 copy.53
  557.2 0.8 copy.52
  558.0 1.8 convert_element_type.20
  559.9 1.1 copy.63
  (64 shorter events, 13.3 us)
Async XLA Ops:
  0.6 0.7 copy-start
  0.7 10.3 %copy-start.9 = (bf16[32,3072]{1,0:T(8,128)(2,1)S(1)}, bf16[32,3072]{1,0:T(8,128)(2,1)}, u32[]{:S(2)}) copy-start(bf16[32,3072]{1,0:T(8,128)(2,1)} %param.30) | copy-start | bytes 589828
  0.7 10.3 %copy-start.8 = (bf16[32,3072]{1,0:T(8,128)(2,1)S(1)}, bf16[32,3072]{1,0:T(8,128)(2,1)}, u32[]{:S(2)}) copy-start(bf16[32,3072]{1,0:T(8,128)(2,1)} %param.29) | copy-start | bytes 589828
  0.7 10.3 %copy-start.10 = (bf16[3072,32]{0,1:T(8,128)(2,1)S(1)}, bf16[3072,32]{0,1:T(8,128)(2,1)}, u32[]{:S(2)}) copy-start(bf16[3072,32]{0,1:T(8,128)(2,1)} %param.31) | copy-start | bytes 589828
  464.6 90.9 %copy-start.4 = (f32[3,32,1536]{2,1,0:T(8,128)S(1)}, f32[3,32,1536]{2,1,0:T(8,128)}, u32[]{:S(2)}) copy-start(f32[3,32,1536]{2,1,0:T(8,128)} %get-tuple-element.75) | copy-start | bytes 1769476
  552.0 3.5 copy-start.5
  555.7 2.3 copy-start.3
  558.0 1.8 copy-start.2
  559.8 1.1 copy-start.7
  559.8 1.8 copy-start.12
  559.8 2.5 copy-start.11
  559.8 3.1 copy-start.6
  559.8 3.8 copy-start.1

commit v6 on v5

--- a/solution.py
+++ b/solution.py
@@ -24,7 +24,7 @@
 FF_CHUNK = 512
 PAIRS = KV_HEADS // 2
 FF_CHUNKS = FF // FF_CHUNK
-FF_EARLY = 3
+FF_EARLY = 2
 FF_FIRST = 4
 LOCAL_RUNS = 3
 MIB = 1024 * 1024
@@ -367,21 +367,20 @@
 ORDERS = ("xy", "yx")
 
 FORWARD_START = [
-    (0, 9), (0, 0), (0, 1), (1, 9), (1, 0), ("swap", "tokens"), (2, 9), (2, 0), (1, 1), (3, 9), (4, 9), (3, 0),
-    (2, 1), (0, 2), ("swapped", "tokens"), (1, 2),
+    ("swap", "tokens"), (0, 9), (0, 0), (1, 9), (1, 0), (2, 9), (2, 0), (0, 1), (0, 2), (3, 9), (4, 9), (3, 0),
+    (1, 1), (1, 2), (0, 3), (2, 1), (0, 4), ("swapped", "tokens"),
 ]
 FORWARD_AFTER = {
-    0: [("kv", 0), (3, 1), (2, 2), (0, 3), (0, 4)],
-    1: [("kv", 1), (3, 2), (1, 3), (1, 4), (0, 5)],
-    2: [("use", 0), (2, 3), (2, 4), (1, 5), (0, 6), (3, 3)],
-    3: [("got", 0), ("kv", 2), (3, 4), (2, 5), (1, 6)],
-    4: [("use", 1), ("got", 1), ("kv", 3), (3, 5), (2, 6), (0, 7)],
-    5: [(1, 7)],
-    6: [("use", 2), (3, 6), (2, 7), (0, 8)],
-    7: [("got", 2), (1, 8), ("swap", "cot")],
-    8: [("use", 3), (3, 7), (2, 8)],
-    9: [("got", 3)],
-    10: [(3, 8)],
+    0: [("kv", 0), (2, 2), (1, 3), (3, 1), (1, 4), (0, 5)],
+    1: [("kv", 1), (3, 2), (2, 3), (2, 4), (1, 5), (0, 6)],
+    2: [("use", 0), (3, 3), (3, 4), (2, 5), (1, 6), ("swap", "cot")],
+    3: [("got", 0), ("kv", 2), (0, 7), (3, 5), (2, 6)],
+    4: [("use", 1), ("got", 1), ("kv", 3), (1, 7), (0, 8)],
+    5: [(3, 6), (2, 7)],
+    6: [("use", 2), (1, 8)],
+    7: [("got", 2), (3, 7), (2, 8)],
+    8: [("use", 3)],
+    9: [("got", 3), (3, 8)],
     11: [("swapped", "cot")],
 }
 FEED_START = [("fetch", 0), ("send", (0, 4)), ("fetch", 1)]
@@ -390,16 +389,16 @@
     0: [("send", (2, 4))],
     1: [("send", (3, 4)), ("send", (2, 5)), ("fetch", 2)],
     2: [("send", (3, 5)), ("fetch", 3)],
-    3: [(1, 0), ("fetch", 4)],
-    4: [(1, 1), ("fetch", 5)],
-    5: [(1, 2)],
+    3: [("fetch", 4)],
+    4: [("fetch", 5)],
+    5: [(1, 1)],
 }
 FEED_AFTER = {
     0: [("send", (1, 5)), ("core", 0)],
     1: [("begin", 0), ("core", 1)],
-    2: [(0, 0), ("begin", 1), ("core", 2)],
-    3: [(0, 1), ("begin", 2)],
-    4: [(0, 2)],
+    2: [("begin", 1)],
+    3: [(0, 0), (0, 1)],
+    4: [(1, 0)],
 }
 FEED_LAST = []
 FINISH_MIDDLE = {
@@ -416,11 +415,11 @@
 BACKWARD_AFTER = {
     0: [(0, 0)],
     1: [(1, 0), (0, 1)],
-    2: [(2, 0), (1, 1)],
-    3: [(2, 1), (0, 2)],
-    4: [(1, 2), (0, 3)],
-    5: [(2, 2), (1, 3)],
-    6: [(2, 3)],
+    2: [(2, 0), (1, 1), (0, 2)],
+    3: [(2, 1), (1, 2), (0, 3)],
+    4: [(2, 2), (1, 3), (0, 4)],
+    5: [(2, 3), (1, 4)],
+    6: [(2, 4)],
 }
 
 
@@ -894,7 +893,7 @@
         lax.fori_loop(0, D // tile, project_out, 0)
         act(FEED_NEXT)
         values = hidden[...]
-        values = values * norm_factor(values) * gain_ref[...]
+        values = values * norm_factor(values) * gain_ref[1:2]
         second[...] = values.astype(BF16)
         second_t[...] = values.T.astype(BF16)
         cot_t[...] = cot_ref[...].astype(F32).T.astype(BF16)
@@ -943,7 +942,7 @@
         output = pltpu.make_async_copy(low, result_ref, local_sem.at[2])
         output.start()
         factor = norm_factor(values)
-        grad_in, share = norm_backward(grads[...], gain_ref[...], values * factor, factor)
+        grad_in, share = norm_backward(grads[...], gain_ref[1:2], values * factor, factor)
         post_ref[...] = jnp.sum(share, axis=0, keepdims=True)
         hidden[...] = cot_ref[...].astype(F32) + grad_in
         saved = pltpu.make_async_copy(hidden, hid_ref, local_sem.at[3])
@@ -1029,7 +1028,7 @@
             whole_block((count, QD)),
             whole_block((count, D)),
             whole_block((D, QD)),
-            whole_block((1, D)),
+            whole_block((8, D)),
             ANY,
         ]
         + [ANY] * late,
@@ -1397,7 +1396,7 @@
 
 
 def finish_kernel(
-    sizes, rows, dq_ref, dkv_ref, pre_ref, w_ref, normed_ref, x_ref, hid_ref, gain_ref, post_ref, qg_ref, kg_ref, cos_ref, sin_ref,
+    sizes, rows, dq_ref, dkv_ref, pre_ref, w_ref, normed_ref, x_ref, hid_ref, gain_ref, post_ref, qk_ref, cos_ref, sin_ref,
     q_out, k_out, v_out, g_out, dx_placed, *refs,
 ):
     normed_t, low, grads, qk, dx, part, part_g = refs[:7]
@@ -1486,11 +1485,11 @@
             grad = jnp.concatenate(
                 [dq_ref[hh, (2 * s + h) * sub : (2 * s + h + 1) * sub] for s in range(2 * SUBS)], axis=0
             )
-            value, share = back(grad, pre_ref[hh, :, h * HEAD_DIM : (h + 1) * HEAD_DIM], qg_ref[...])
+            value, share = back(grad, pre_ref[hh, :, h * HEAD_DIM : (h + 1) * HEAD_DIM], qk_ref[0:1])
             qk[0:1] += share
             at = 2 * hh + h
             low[:, at * HEAD_DIM : (at + 1) * HEAD_DIM] = value
-        value, share = back(dkv_ref[0, hh].reshape(count, HEAD_DIM), pre_ref[hh, :, 2 * HEAD_DIM :], kg_ref[...])
+        value, share = back(dkv_ref[0, hh].reshape(count, HEAD_DIM), pre_ref[hh, :, 2 * HEAD_DIM :], qk_ref[1:2])
         qk[1:2] += share
         low[:, (4 + hh) * HEAD_DIM : (5 + hh) * HEAD_DIM] = value
         low[:, (6 + hh) * HEAD_DIM : (7 + hh) * HEAD_DIM] = dkv_ref[1, hh].reshape(count, HEAD_DIM).astype(BF16)
@@ -1515,7 +1514,7 @@
     def _():
         values = x_ref[...].astype(F32)
         factor = norm_factor(values)
-        grad_in, share = norm_backward(grads[...], gain_ref[...], values * factor, factor)
+        grad_in, share = norm_backward(grads[...], gain_ref[0:1], values * factor, factor)
         dx[...] = (hid_ref[...] + grad_in).astype(BF16).reshape(2, rows, D)
         swap.start()
         act([(0, PAIRS - 2), ("begin", PAIRS - 1)])
@@ -1537,7 +1536,7 @@
         swap.wait()
 
 
-def finish(sizes, dq, dkv, pre, normed, x, grad_hidden, gain, post_part, qkv_full, query_gain, key_gain, cosine, sine):
+def finish(sizes, dq, dkv, pre, normed, x, grad_hidden, gain, post_part, qkv_full, qk_gain, cosine, sine):
     ny, nx, nz = sizes
     count = x.shape[0]
     rows = count // 2
@@ -1576,10 +1575,9 @@
             whole_block((count, D)),
             whole_block((count, D)),
             whole_block((count, D)),
+            whole_block((8, D)),
             whole_block((1, D)),
-            whole_block((1, D)),
-            whole_block((1, HEAD_DIM)),
-            whole_block((1, HEAD_DIM)),
+            whole_block((8, HEAD_DIM)),
             whole_block((count, HEAD_DIM)),
             whole_block((count, HEAD_DIM)),
         ],
@@ -1603,7 +1601,7 @@
             collective_id=4, has_side_effects=True, vmem_limit_bytes=58 * MIB
         ),
         name="finish",
-    )(dq, dkv, pre, qkv_full, normed, x, grad_hidden, gain, post_part, query_gain, key_gain, cosine, sine)
+    )(dq, dkv, pre, qkv_full, normed, x, grad_hidden, gain, post_part, qk_gain, cosine, sine)
 
 
 def shards(
@@ -1679,14 +1677,12 @@
     )
     x = placed.reshape(count, D)
     cot = cot.reshape(count, D)
-    in_weight, post_weight = gain_rows_[0:1], gain_rows_[1:2]
-    query_weight, key_weight = qk_gains[0:1], qk_gains[1:2]
     qkv_full = qkv_full.reshape(PAIRS, D, -1)
     out_t = out_t.reshape(D, QD)
     feed_whole = feed_whole.reshape(FF_FIRST, D, -1)
     log_total = jnp.log2(totals[:, :KV_HEADS]).T
     result, grad_hidden, grad_stack, delta, post_part, dout, late, _, early_grad = feed(
-        sizes, x, mixed, cot, out_t, post_weight, feed_whole, feed_shards[FF_FIRST:]
+        sizes, x, mixed, cot, out_t, gain_rows_, feed_whole, feed_shards[FF_FIRST:]
     )
     delta = delta[:HEADS].reshape(KV_HEADS, 2, 2 * SUBS, sub).transpose(0, 2, 1, 3)
     dq, dkv, late_grad, out_grad, output = backward(
@@ -1699,7 +1695,7 @@
         return piece.transpose(1, 0, 2).reshape(shard_rows, FF)
 
     query_grad, key_grad, value_grad, gain_grad, input_grad = finish(
-        sizes, dq, dkv, pre, normed, x, grad_hidden, in_weight, post_part, qkv_full, query_weight, key_weight, cosine, sine
+        sizes, dq, dkv, pre, normed, x, grad_hidden, gain_rows_, post_part, qkv_full, qk_gains, cosine, sine
     )
 
     def own(line):

time: 568 us -> 556 us (0.979)
  Pallas kernels: 530 us -> 521 us
    pallas_call x1, Pallas kernels: 109 us -> 98.8 us  [feed(): pl.pallas_call(functools.partial(feed_kernel, sizes, rows), grid=(FF_CHUN...]
where the time goes in v6:
time: 556 us; the launch traced here: 553 us
  Pallas kernels  521 us (94%)
  local copies, waits for them, and re-layouts  19.8 us (4%)
  other arithmetic  10.7 us (2%)
    pallas_call x1, Pallas kernels, forward(): pl.pallas_call(functools.partial(forward_kernel, sizes, rows), out_shape=...  208 us
    pallas_call x1, Pallas kernels, backward(): pl.pallas_call(functools.partial(backward_kernel, sizes, rows, widths), o...  124 us
    pallas_call x1, Pallas kernels, feed(): pl.pallas_call(functools.partial(feed_kernel, sizes, rows), grid=(FF_CHUN...  98.8 us
    pallas_call x1, Pallas kernels, finish(): pl.pallas_call(functools.partial(finish_kernel, sizes, rows), grid=(PAIRS...  90.4 us

profile of v6, /device:TPU:0, one launch (start us, length us, event | category | flops | bytes accessed | tf_op | source)
XLA Modules:
  0.0 552.6 jit_solution(11927777339750519657)
XLA Ops:
  2.0 0.8 dynamic_update_slice.7
  2.8 0.8 dynamic_update_slice.6
  4.3 0.8 dynamic-slice_reduce_fusion
  6.1 0.7 iota_reduce_fusion
  7.3 0.8 fusion.16
  8.1 0.8 fusion.17
  8.8 0.8 fusion.15
  13.1 1.2 fusion
  14.3 0.9 pad_maximum_fusion.1.sin_ref
  15.2 0.9 pad_maximum_fusion.cos_ref
  16.1 207.7 %forward.1 = (bf16[640,2048]{1,0:T(8,128)(2,1)}, f32[1280,128]{1,0:T(8,128)}, f32[8,640,384]{2,1,0:T(8,128)}, bf16[640,1024]{1,0:T(8,128)(2,1)}, f32[8,1024]{1,0...) custom-call(s32[12]{0:T(128)} %compare_select_fusion.1.meta, ...), custom_call_target="tpu_custom_call" | custom-call | tf_op jit(solution)/shard_map/forward/pallas_call | solution.py:739
  223.8 1.3 copy.47
  225.8 98.8 %feed.1 = (bf16[640,1024]{1,0:T(8,128)(2,1)}, f32[640,1024]{1,0:T(8,128)}, bf16[8,1280,128]{2,1,0:T(8,128)(2,1)}, f32[128,640]{1,0:T(8,128)}, f32[1,1024]{1,0:T(...) custom-call(bf16[640,1024]{1,0:T(8,128)(2,1)} %bitcast.38, ...), custom_call_target="tpu_custom_call" | custom-call | tf_op jit(solution)/shard_map/feed/pallas_call | solution.py:1012
  324.6 0.8 slice.152
  325.5 0.7 reshape.86.del_ref
  326.3 124.0 %backward.1 = (f32[8,1280,128]{2,1,0:T(8,128)}, f32[2,8,2,320,128]{4,3,2,1,0:T(8,128)}, f32[4,32,1536]{2,1,0:T(8,128)}, f32[32,2048]{1,0:T(8,128)}, bf16[2,320,1024]{2,1,0:T(8,128)(2,1)}) custom-call(s32[12]{0:T(128)} %compare_select_fusion.1.meta, bf16[8,1280,128]{2,1,0:T(8,128)(2,1)} %get-tuple-element.46.q_ref, ...), custom_call_target="tpu_custom_call" | custom-call | tf_op jit(solution)/shard_map/backward/pallas_call | solution.py:1329
  450.3 90.4 %finish.1 = (f32[32,2048]{1,0:T(8,128)}, f32[32,1024]{1,0:T(8,128)}, f32[32,1024]{1,0:T(8,128)}, f32[32,384]{1,0:T(8,128)}, bf16[2,320,1024]{2,1,0:T(8,128)(2,1)}) custom-call(f32[8,1280,128]{2,1,0:T(8,128)} %get-tuple-element.61.dq_ref, f32[2,8,2,320,128]{4,3,2,1,0:T(8,128)} %get-tuple-element.62.dkv_ref, f32[8,640,384]{2,1,0:T(8,128)} %get-tuple-element.63.pre_ref, ...), custom_call_target="tpu_custom_call" | custom-call | tf_op jit(solution)/shard_map/finish/pallas_call | solution.py:1560
  540.7 0.8 fusion.18
  541.5 1.5 slice_reduce_fusion
  544.3 0.8 copy.54
  545.1 0.8 copy.53
  545.9 0.8 copy.52
  546.7 1.8 convert_element_type.20
  548.5 1.1 copy.63
  (62 shorter events, 11.8 us)
Async XLA Ops:
  0.6 0.7 copy-start
  0.7 10.3 %copy-start.9 = (bf16[32,3072]{1,0:T(8,128)(2,1)S(1)}, bf16[32,3072]{1,0:T(8,128)(2,1)}, u32[]{:S(2)}) copy-start(bf16[32,3072]{1,0:T(8,128)(2,1)} %param.30) | copy-start | bytes 589828
  0.7 10.3 %copy-start.8 = (bf16[32,3072]{1,0:T(8,128)(2,1)S(1)}, bf16[32,3072]{1,0:T(8,128)(2,1)}, u32[]{:S(2)}) copy-start(bf16[32,3072]{1,0:T(8,128)(2,1)} %param.29) | copy-start | bytes 589828
  0.7 10.3 %copy-start.10 = (bf16[3072,32]{0,1:T(8,128)(2,1)S(1)}, bf16[3072,32]{0,1:T(8,128)(2,1)}, u32[]{:S(2)}) copy-start(bf16[3072,32]{0,1:T(8,128)(2,1)} %param.31) | copy-start | bytes 589828
  450.3 93.9 %copy-start.5 = (f32[2,32,1536]{2,1,0:T(8,128)S(1)}, f32[2,32,1536]{2,1,0:T(8,128)}, u32[]{:S(2)}) copy-start(f32[2,32,1536]{2,1,0:T(8,128)} %get-tuple-element.75) | copy-start | bytes 1179652
  540.7 3.5 copy-start.4
  544.3 2.3 copy-start.3
  546.7 1.8 copy-start.2
  548.5 1.1 copy-start.7
  548.5 1.8 copy-start.12
  548.5 2.5 copy-start.11
  548.5 3.1 copy-start.6
  548.5 3.8 copy-start.1

commit v7 on v6

--- a/solution.py
+++ b/solution.py
@@ -372,12 +372,12 @@
 ]
 FORWARD_AFTER = {
     0: [("kv", 0), (2, 2), (1, 3), (3, 1), (1, 4), (0, 5)],
-    1: [("kv", 1), (3, 2), (2, 3), (2, 4), (1, 5), (0, 6)],
-    2: [("use", 0), (3, 3), (3, 4), (2, 5), (1, 6), ("swap", "cot")],
-    3: [("got", 0), ("kv", 2), (0, 7), (3, 5), (2, 6)],
-    4: [("use", 1), ("got", 1), ("kv", 3), (1, 7), (0, 8)],
-    5: [(3, 6), (2, 7)],
-    6: [("use", 2), (1, 8)],
+    1: [("kv", 1), (3, 2), (2, 3), (2, 4), (1, 5)],
+    2: [("use", 0), (3, 3), (3, 4), (2, 5), (0, 6), ("kv", 2)],
+    3: [("got", 0), (1, 6), (0, 7), (3, 5)],
+    4: [("use", 1), ("got", 1), ("kv", 3), (2, 6), (1, 7)],
+    5: [(3, 6), (2, 7), (0, 8)],
+    6: [("use", 2), ("swap", "cot"), (1, 8)],
     7: [("got", 2), (3, 7), (2, 8)],
     8: [("use", 3)],
     9: [("got", 3), (3, 8)],
@@ -1399,8 +1399,8 @@
     sizes, rows, dq_ref, dkv_ref, pre_ref, w_ref, normed_ref, x_ref, hid_ref, gain_ref, post_ref, qk_ref, cos_ref, sin_ref,
     q_out, k_out, v_out, g_out, dx_placed, *refs,
 ):
-    normed_t, low, grads, qk, dx, part, part_g = refs[:7]
-    buffers = refs[7:-3]
+    normed_t, low, grads, qk, sums, dx, part, part_g = refs[:8]
+    buffers = refs[8:-3]
     send_sem, recv_sem, local_sem = refs[-3:]
     ny, nx, nz = sizes
     count = 2 * rows
@@ -1493,22 +1493,12 @@
         qk[1:2] += share
         low[:, (4 + hh) * HEAD_DIM : (5 + hh) * HEAD_DIM] = value
         low[:, (6 + hh) * HEAD_DIM : (7 + hh) * HEAD_DIM] = dkv_ref[1, hh].reshape(count, HEAD_DIM).astype(BF16)
-    for moment, steps in FINISH_MIDDLE.items():
-        pl.when(pair == moment)(functools.partial(act, steps))
-    slot = lax.rem(pair, 2)
-
-    def model(t, carry):
+    def inward(t, carry):
         at = pl.multiple_of(t * tile, tile)
         grads[:, pl.ds(at, tile)] += nt(low[...], w_ref[0, pl.ds(at, tile), :])
-        value = matmul(normed_t[pl.ds(at, tile)], low[...])
-        for k in range(tile // shard_rows):
-            y, x, z, c = rows_of(at // shard_rows + k)
-            part[slot, y, x, z, c] = value[k * shard_rows : (k + 1) * shard_rows].astype(BF16)
         return carry
 
-    lax.fori_loop(0, D // tile, model, 0)
-    for moment, steps in FINISH_AFTER.items():
-        pl.when(pair == moment)(functools.partial(act, steps))
+    lax.fori_loop(0, D // tile, inward, 0)
 
     @pl.when(pair == PAIRS - 1)
     def _():
@@ -1517,9 +1507,28 @@
         grad_in, share = norm_backward(grads[...], gain_ref[0:1], values * factor, factor)
         dx[...] = (hid_ref[...] + grad_in).astype(BF16).reshape(2, rows, D)
         swap.start()
-        act([(0, PAIRS - 2), ("begin", PAIRS - 1)])
+        sums[...] = jnp.sum(share, axis=0, keepdims=True)
+
+    for moment, steps in FINISH_MIDDLE.items():
+        pl.when(pair == moment)(functools.partial(act, steps))
+    slot = lax.rem(pair, 2)
+
+    def model(t, carry):
+        at = pl.multiple_of(t * tile, tile)
+        value = matmul(normed_t[pl.ds(at, tile)], low[...])
+        for k in range(tile // shard_rows):
+            y, x, z, c = rows_of(at // shard_rows + k)
+            part[slot, y, x, z, c] = value[k * shard_rows : (k + 1) * shard_rows].astype(BF16)
+        return carry
+
+    lax.fori_loop(0, D // tile, model, 0)
+    for moment, steps in FINISH_AFTER.items():
+        pl.when(pair == moment)(functools.partial(act, steps))
+
+    @pl.when(pair == PAIRS - 1)
+    def _():
         lines = jnp.concatenate(
-            [jnp.sum(share, axis=0, keepdims=True), post_ref[...], jnp.zeros((GAIN_COLS - 2, D), F32)], axis=0
+            [sums[...], post_ref[...], jnp.zeros((GAIN_COLS - 2, D), F32)], axis=0
         )
         columns = lines.T.astype(BF16)
         first = lax.broadcasted_iota(jnp.int32, (shard_rows, GAIN_COLS), 0) == 0
@@ -1530,7 +1539,8 @@
             part_g[y, x, z, c, :, :GAIN_COLS] = columns[k * shard_rows : (k + 1) * shard_rows]
             part_g[y, x, z, c, :, GAIN_COLS : 2 * GAIN_COLS] = query_line
             part_g[y, x, z, c, :, 2 * GAIN_COLS :] = key_line
-        act([("core", PAIRS), (1, PAIRS - 2), ("begin", PAIRS), (0, PAIRS - 1), (0, PAIRS), (1, PAIRS - 1), (1, PAIRS)])
+        act([("core", PAIRS), (0, PAIRS - 2), ("begin", PAIRS - 1), ("begin", PAIRS), (1, PAIRS - 2)])
+        act([(0, PAIRS - 1), (0, PAIRS), (1, PAIRS - 1), (1, PAIRS)])
         for c in range(PAIRS + 1):
             act([("finish", c)])
         swap.wait()
@@ -1587,6 +1597,7 @@
             pltpu.VMEM((count, width), BF16),
             pltpu.VMEM((count, D), F32),
             pltpu.VMEM((8, HEAD_DIM), F32),
+            pltpu.VMEM((1, D), F32),
             pltpu.VMEM((2, rows, D), BF16),
             pltpu.VMEM((2,) + blocks + (width,), BF16),
             pltpu.VMEM(blocks + (3 * GAIN_COLS,), BF16),

time: 556 us -> 545 us (0.980)
  Pallas kernels: 521 us -> 509 us
    pallas_call x1, Pallas kernels: 208 us -> 190 us  [forward(): pl.pallas_call(functools.partial(forward_kernel, sizes, rows), out_shape=...]
where the time goes in v7:
time: 545 us; the launch traced here: 541 us
  Pallas kernels  509 us (93%)
  local copies, waits for them, and re-layouts  19.8 us (4%)
  other arithmetic  10.7 us (2%)
    pallas_call x1, Pallas kernels, forward(): pl.pallas_call(functools.partial(forward_kernel, sizes, rows), out_shape=...  190 us
    pallas_call x1, Pallas kernels, backward(): pl.pallas_call(functools.partial(backward_kernel, sizes, rows, widths), o...  127 us
    pallas_call x1, Pallas kernels, feed(): pl.pallas_call(functools.partial(feed_kernel, sizes, rows), grid=(FF_CHUN...  97.6 us
    pallas_call x1, Pallas kernels, finish(): pl.pallas_call(functools.partial(finish_kernel, sizes, rows), grid=(PAIRS...  94.6 us

profile of v7, /device:TPU:0, one launch (start us, length us, event | category | flops | bytes accessed | tf_op | source)
XLA Modules:
  0.0 541.1 jit_solution(13264246886519731258)
XLA Ops:
  2.0 0.8 dynamic_update_slice.7
  2.8 0.8 dynamic_update_slice.6
  4.3 0.8 dynamic-slice_reduce_fusion
  6.1 0.7 iota_reduce_fusion
  7.3 0.8 fusion.16
  8.1 0.8 fusion.17
  8.8 0.8 fusion.15
  13.1 1.2 fusion
  14.3 0.9 pad_maximum_fusion.1.sin_ref
  15.2 0.9 pad_maximum_fusion.cos_ref
  16.1 190.1 %forward.1 = (bf16[640,2048]{1,0:T(8,128)(2,1)}, f32[1280,128]{1,0:T(8,128)}, f32[8,640,384]{2,1,0:T(8,128)}, bf16[640,1024]{1,0:T(8,128)(2,1)}, f32[8,1024]{1,0...) custom-call(s32[12]{0:T(128)} %compare_select_fusion.1.meta, ...), custom_call_target="tpu_custom_call" | custom-call | tf_op jit(solution)/shard_map/forward/pallas_call | solution.py:739
  206.2 1.3 copy.47
  208.2 97.6 %feed.1 = (bf16[640,1024]{1,0:T(8,128)(2,1)}, f32[640,1024]{1,0:T(8,128)}, bf16[8,1280,128]{2,1,0:T(8,128)(2,1)}, f32[128,640]{1,0:T(8,128)}, f32[1,1024]{1,0:T(...) custom-call(bf16[640,1024]{1,0:T(8,128)(2,1)} %bitcast.38, ...), custom_call_target="tpu_custom_call" | custom-call | tf_op jit(solution)/shard_map/feed/pallas_call | solution.py:1012
  305.8 0.8 slice.152
  306.7 0.7 reshape.86.del_ref
  307.4 127.2 %backward.1 = (f32[8,1280,128]{2,1,0:T(8,128)}, f32[2,8,2,320,128]{4,3,2,1,0:T(8,128)}, f32[4,32,1536]{2,1,0:T(8,128)}, f32[32,2048]{1,0:T(8,128)}, bf16[2,320,1024]{2,1,0:T(8,128)(2,1)}) custom-call(s32[12]{0:T(128)} %compare_select_fusion.1.meta, bf16[8,1280,128]{2,1,0:T(8,128)(2,1)} %get-tuple-element.46.q_ref, ...), custom_call_target="tpu_custom_call" | custom-call | tf_op jit(solution)/shard_map/backward/pallas_call | solution.py:1329
  434.7 94.6 %finish.1 = (f32[32,2048]{1,0:T(8,128)}, f32[32,1024]{1,0:T(8,128)}, f32[32,1024]{1,0:T(8,128)}, f32[32,384]{1,0:T(8,128)}, bf16[2,320,1024]{2,1,0:T(8,128)(2,1)}) custom-call(f32[8,1280,128]{2,1,0:T(8,128)} %get-tuple-element.61.dq_ref, f32[2,8,2,320,128]{4,3,2,1,0:T(8,128)} %get-tuple-element.62.dkv_ref, f32[8,640,384]{2,1,0:T(8,128)} %get-tuple-element.63.pre_ref, ...), custom_call_target="tpu_custom_call" | custom-call | tf_op jit(solution)/shard_map/finish/pallas_call | solution.py:1570
  529.3 0.8 fusion.18
  530.0 1.5 slice_reduce_fusion
  532.9 0.8 copy.54
  533.7 0.8 copy.53
  534.5 0.8 copy.52
  535.2 1.8 convert_element_type.20
  537.1 1.1 copy.63
  (62 shorter events, 11.8 us)
Async XLA Ops:
  0.6 0.7 copy-start
  0.7 10.3 %copy-start.9 = (bf16[32,3072]{1,0:T(8,128)(2,1)S(1)}, bf16[32,3072]{1,0:T(8,128)(2,1)}, u32[]{:S(2)}) copy-start(bf16[32,3072]{1,0:T(8,128)(2,1)} %param.30) | copy-start | bytes 589828
  0.7 10.3 %copy-start.8 = (bf16[32,3072]{1,0:T(8,128)(2,1)S(1)}, bf16[32,3072]{1,0:T(8,128)(2,1)}, u32[]{:S(2)}) copy-start(bf16[32,3072]{1,0:T(8,128)(2,1)} %param.29) | copy-start | bytes 589828
  0.7 10.3 %copy-start.10 = (bf16[3072,32]{0,1:T(8,128)(2,1)S(1)}, bf16[3072,32]{0,1:T(8,128)(2,1)}, u32[]{:S(2)}) copy-start(bf16[3072,32]{0,1:T(8,128)(2,1)} %param.31) | copy-start | bytes 589828
  434.7 98.0 %copy-start.5 = (f32[2,32,1536]{2,1,0:T(8,128)S(1)}, f32[2,32,1536]{2,1,0:T(8,128)}, u32[]{:S(2)}) copy-start(f32[2,32,1536]{2,1,0:T(8,128)} %get-tuple-element.75) | copy-start | bytes 1179652
  529.2 3.5 copy-start.4
  532.9 2.3 copy-start.3
  535.2 1.8 copy-start.2
  537.1 1.1 copy-start.7
  537.1 1.8 copy-start.12
  537.1 2.5 copy-start.11
  537.1 3.1 copy-start.6
  537.1 3.8 copy-start.1

commit v8 on v6

--- a/solution.py
+++ b/solution.py
@@ -372,12 +372,12 @@
 ]
 FORWARD_AFTER = {
     0: [("kv", 0), (2, 2), (1, 3), (3, 1), (1, 4), (0, 5)],
-    1: [("kv", 1), (3, 2), (2, 3), (2, 4), (1, 5), (0, 6)],
-    2: [("use", 0), (3, 3), (3, 4), (2, 5), (1, 6), ("swap", "cot")],
-    3: [("got", 0), ("kv", 2), (0, 7), (3, 5), (2, 6)],
-    4: [("use", 1), ("got", 1), ("kv", 3), (1, 7), (0, 8)],
-    5: [(3, 6), (2, 7)],
-    6: [("use", 2), (1, 8)],
+    1: [("kv", 1), (3, 2), (2, 3), (2, 4), (1, 5)],
+    2: [("use", 0), (3, 3), (3, 4), (2, 5), (0, 6), ("kv", 2)],
+    3: [("got", 0), (1, 6), (0, 7), (3, 5)],
+    4: [("use", 1), ("got", 1), ("kv", 3), (2, 6), (1, 7)],
+    5: [(3, 6), (2, 7), (0, 8)],
+    6: [("use", 2), ("swap", "cot"), (1, 8)],
     7: [("got", 2), (3, 7), (2, 8)],
     8: [("use", 3)],
     9: [("got", 3), (3, 8)],

time: 556 us -> 539 us (0.969)
  Pallas kernels: 521 us -> 504 us
    pallas_call x1, Pallas kernels: 208 us -> 190 us  [forward(): pl.pallas_call(functools.partial(forward_kernel, sizes, rows), out_shape=...]
where the time goes in v8:
time: 539 us; the launch traced here: 535 us
  Pallas kernels  504 us (94%)
  local copies, waits for them, and re-layouts  19.8 us (4%)
  other arithmetic  10.7 us (2%)
    pallas_call x1, Pallas kernels, forward(): pl.pallas_call(functools.partial(forward_kernel, sizes, rows), out_shape=...  190 us
    pallas_call x1, Pallas kernels, backward(): pl.pallas_call(functools.partial(backward_kernel, sizes, rows, widths), o...  127 us
    pallas_call x1, Pallas kernels, feed(): pl.pallas_call(functools.partial(feed_kernel, sizes, rows), grid=(FF_CHUN...  97.6 us
    pallas_call x1, Pallas kernels, finish(): pl.pallas_call(functools.partial(finish_kernel, sizes, rows), grid=(PAIRS...  88.9 us

profile of v8, /device:TPU:0, one launch (start us, length us, event | category | flops | bytes accessed | tf_op | source)
XLA Modules:
  0.0 535.5 jit_solution(11392469999389198031)
XLA Ops:
  2.0 0.8 dynamic_update_slice.7
  2.8 0.8 dynamic_update_slice.6
  4.3 0.8 dynamic-slice_reduce_fusion
  6.1 0.7 iota_reduce_fusion
  7.3 0.8 fusion.16
  8.1 0.8 fusion.17
  8.8 0.8 fusion.15
  13.1 1.2 fusion
  14.3 0.9 pad_maximum_fusion.1.sin_ref
  15.2 0.9 pad_maximum_fusion.cos_ref
  16.1 190.1 %forward.1 = (bf16[640,2048]{1,0:T(8,128)(2,1)}, f32[1280,128]{1,0:T(8,128)}, f32[8,640,384]{2,1,0:T(8,128)}, bf16[640,1024]{1,0:T(8,128)(2,1)}, f32[8,1024]{1,0...) custom-call(s32[12]{0:T(128)} %compare_select_fusion.1.meta, ...), custom_call_target="tpu_custom_call" | custom-call | tf_op jit(solution)/shard_map/forward/pallas_call | solution.py:739
  206.2 1.3 copy.47
  208.2 97.6 %feed.1 = (bf16[640,1024]{1,0:T(8,128)(2,1)}, f32[640,1024]{1,0:T(8,128)}, bf16[8,1280,128]{2,1,0:T(8,128)(2,1)}, f32[128,640]{1,0:T(8,128)}, f32[1,1024]{1,0:T(...) custom-call(bf16[640,1024]{1,0:T(8,128)(2,1)} %bitcast.38, ...), custom_call_target="tpu_custom_call" | custom-call | tf_op jit(solution)/shard_map/feed/pallas_call | solution.py:1012
  305.8 0.8 slice.152
  306.7 0.7 reshape.86.del_ref
  307.4 127.2 %backward.1 = (f32[8,1280,128]{2,1,0:T(8,128)}, f32[2,8,2,320,128]{4,3,2,1,0:T(8,128)}, f32[4,32,1536]{2,1,0:T(8,128)}, f32[32,2048]{1,0:T(8,128)}, bf16[2,320,1024]{2,1,0:T(8,128)(2,1)}) custom-call(s32[12]{0:T(128)} %compare_select_fusion.1.meta, bf16[8,1280,128]{2,1,0:T(8,128)(2,1)} %get-tuple-element.46.q_ref, ...), custom_call_target="tpu_custom_call" | custom-call | tf_op jit(solution)/shard_map/backward/pallas_call | solution.py:1329
  434.7 88.9 %finish.1 = (f32[32,2048]{1,0:T(8,128)}, f32[32,1024]{1,0:T(8,128)}, f32[32,1024]{1,0:T(8,128)}, f32[32,384]{1,0:T(8,128)}, bf16[2,320,1024]{2,1,0:T(8,128)(2,1)}) custom-call(f32[8,1280,128]{2,1,0:T(8,128)} %get-tuple-element.61.dq_ref, f32[2,8,2,320,128]{4,3,2,1,0:T(8,128)} %get-tuple-element.62.dkv_ref, f32[8,640,384]{2,1,0:T(8,128)} %get-tuple-element.63.pre_ref, ...), custom_call_target="tpu_custom_call" | custom-call | tf_op jit(solution)/shard_map/finish/pallas_call | solution.py:1560
  523.6 0.8 fusion.18
  524.4 1.5 slice_reduce_fusion
  527.3 0.8 copy.54
  528.0 0.8 copy.53
  528.8 0.8 copy.52
  529.6 1.8 convert_element_type.20
  531.4 1.1 copy.63
  (62 shorter events, 11.8 us)
Async XLA Ops:
  0.6 0.7 copy-start
  0.7 10.3 %copy-start.9 = (bf16[32,3072]{1,0:T(8,128)(2,1)S(1)}, bf16[32,3072]{1,0:T(8,128)(2,1)}, u32[]{:S(2)}) copy-start(bf16[32,3072]{1,0:T(8,128)(2,1)} %param.30) | copy-start | bytes 589828
  0.7 10.3 %copy-start.8 = (bf16[32,3072]{1,0:T(8,128)(2,1)S(1)}, bf16[32,3072]{1,0:T(8,128)(2,1)}, u32[]{:S(2)}) copy-start(bf16[32,3072]{1,0:T(8,128)(2,1)} %param.29) | copy-start | bytes 589828
  0.7 10.3 %copy-start.10 = (bf16[3072,32]{0,1:T(8,128)(2,1)S(1)}, bf16[3072,32]{0,1:T(8,128)(2,1)}, u32[]{:S(2)}) copy-start(bf16[3072,32]{0,1:T(8,128)(2,1)} %param.31) | copy-start | bytes 589828
  434.7 92.4 %copy-start.5 = (f32[2,32,1536]{2,1,0:T(8,128)S(1)}, f32[2,32,1536]{2,1,0:T(8,128)}, u32[]{:S(2)}) copy-start(f32[2,32,1536]{2,1,0:T(8,128)} %get-tuple-element.75) | copy-start | bytes 1179652
  523.6 3.5 copy-start.4
  527.2 2.3 copy-start.3
  529.6 1.8 copy-start.2
  531.4 1.1 copy-start.7
  531.4 1.8 copy-start.12
  531.4 2.5 copy-start.11
  531.4 3.1 copy-start.6
  531.4 3.8 copy-start.1

commit v9 on v8

--- a/solution.py
+++ b/solution.py
@@ -515,16 +515,23 @@
 
 def forward_kernel(sizes, rows, meta, cos_ref, sin_ref, tok_ref, cot_ref, *refs):
     arrays = PAIRS + 2 + FF_FIRST
-    shard = refs[:arrays]
+    qkv_width, feed_width = 8 * HEAD_DIM, 3 * FF_CHUNK
+    shard = (
+        tuple(refs[0].at[:, qkv_width * c : qkv_width * (c + 1)] for c in range(PAIRS))
+        + (refs[1],)
+        + tuple(refs[2].at[:, feed_width * c : feed_width * (c + 1)] for c in range(FF_FIRST))
+        + (refs[3],)
+    )
+    refs = refs[4:]
     (mixed_ref, l_ref, pre_ref, normed_ref, gains_ref, qk_ref,
-     placed, cot_placed, q_all, kv_all, qkv_whole, gain_whole, out_whole, feed_whole) = refs[arrays : arrays + 14]
+     placed, cot_placed, q_all, kv_all, qkv_whole, gain_whole, out_whole, feed_whole) = refs[:14]
     whole = (
         tuple(qkv_whole.at[c] for c in range(PAIRS))
         + (out_whole,)
         + tuple(feed_whole.at[c] for c in range(FF_FIRST))
         + (gain_whole,)
     )
-    (qs, kvs, xs, ws, gs, acc, part, places, kp, vp, send_sem, recv_sem, local_sem) = refs[arrays + 14 :]
+    (qs, kvs, xs, ws, gs, acc, part, places, kp, vp, send_sem, recv_sem, local_sem) = refs[14:]
     members = sizes[2]
     sub = rows // SUBS
     count = 2 * rows
@@ -730,7 +737,7 @@
     arrays = PAIRS + 2 + FF_FIRST
     shard_rows = shards_[0].shape[0]
     blocks = (ny, nx, nz, 2, shard_rows)
-    widths = [w.shape[-1] for w in shards_]
+    widths = [8 * HEAD_DIM] * PAIRS + [QD] + [3 * FF_CHUNK] * FF_FIRST + [3 * GAIN_COLS]
     rounds = KeyValues.copies(sizes) + 2 * arrays * Gather.copies(sizes) + 2
 
     def at_head(s):
@@ -757,7 +764,7 @@
         grid_spec=pltpu.PrefetchScalarGridSpec(
             num_scalar_prefetch=1,
             grid=(PAIRS + KV_HEADS,),
-            in_specs=[pl.BlockSpec((count, HEAD_DIM), lambda s, meta: (0, 0))] * 2 + [ANY] * (2 + arrays),
+            in_specs=[pl.BlockSpec((count, HEAD_DIM), lambda s, meta: (0, 0))] * 2 + [ANY] * 6,
             out_specs=[
                 pl.BlockSpec((count, 2 * HEAD_DIM), lambda s, meta: (0, at_head(s))),
                 pl.BlockSpec((2 * count, HEAD_DIM), lambda s, meta: (0, 0)),
@@ -1644,24 +1651,20 @@
         jnp.stack([input_norm, post_norm], axis=1), ((0, 0), (0, GAIN_COLS - 2))
     )
     gains = jnp.concatenate([gains, spread(query_norm), spread(key_norm)], axis=1)
-    qkv_shards = [
-        jnp.concatenate(
-            [
-                query_proj[:, 4 * HEAD_DIM * c : 4 * HEAD_DIM * (c + 1)],
-                key_proj[:, 2 * HEAD_DIM * c : 2 * HEAD_DIM * (c + 1)],
-                value_proj[:, 2 * HEAD_DIM * c : 2 * HEAD_DIM * (c + 1)],
-            ],
-            axis=1,
+    qkv_shard = jnp.concatenate(
+        [
+            w[:, n * HEAD_DIM * c : n * HEAD_DIM * (c + 1)]
+            for c in range(PAIRS)
+            for w, n in ((query_proj, 4), (key_proj, 2), (value_proj, 2))
+        ],
+        axis=1,
+    )
+    down_t = down_proj.T
+
+    def feed_shard(chunks):
+        return jnp.concatenate(
+            [w[:, c * FF_CHUNK : (c + 1) * FF_CHUNK] for c in chunks for w in (gate_proj, up_proj, down_t)], axis=1
         )
-        for c in range(PAIRS)
-    ]
-    down_t = down_proj.T
-    feed_shards = [
-        jnp.concatenate(
-            [w[:, c * FF_CHUNK : (c + 1) * FF_CHUNK] for w in (gate_proj, up_proj, down_t)], axis=1
-        )
-        for c in range(FF_CHUNKS)
-    ]
 
     run_seg = segment_ids[half][TRUNK::SEG]
     run_parent = parents[half][run_seg]
@@ -1673,7 +1676,7 @@
 
     (mixed, totals, pre, normed, gain_rows_, qk_gains, placed, cot, queries, kv_all,
      qkv_full, _, out_t, feed_whole) = forward(
-        sizes, meta, cosine, sine, tokens, cotangent, qkv_shards + [out_proj.T] + feed_shards[:FF_FIRST] + [gains]
+        sizes, meta, cosine, sine, tokens, cotangent, [qkv_shard, out_proj.T, feed_shard(range(FF_FIRST)), gains]
     )
     x = placed.reshape(count, D)
     cot = cot.reshape(count, D)
@@ -1682,7 +1685,7 @@
     feed_whole = feed_whole.reshape(FF_FIRST, D, -1)
     log_total = jnp.log2(totals[:, :KV_HEADS]).T
     result, grad_hidden, grad_stack, delta, post_part, dout, late, _, early_grad = feed(
-        sizes, x, mixed, cot, out_t, gain_rows_, feed_whole, feed_shards[FF_FIRST:]
+        sizes, x, mixed, cot, out_t, gain_rows_, feed_whole, [feed_shard([c]) for c in range(FF_FIRST, FF_CHUNKS)]
     )
     delta = delta[:HEADS].reshape(KV_HEADS, 2, 2 * SUBS, sub).transpose(0, 2, 1, 3)
     dq, dkv, late_grad, out_grad, output = backward(

time: 539 us -> 544 us (level)
  local copies, waits for them, and re-layouts: 19.8 us -> 26.2 us
    unnamed x33 -> x57, local copies, waits for them, and re-layouts: 4.58 us -> 12.7 us
where the time goes in v9:
time: 544 us; the launch traced here: 540 us
  Pallas kernels  504 us (93%)
  local copies, waits for them, and re-layouts  26.2 us (5%)
  other arithmetic  8.16 us (2%)
    pallas_call x1, Pallas kernels, forward(): pl.pallas_call(functools.partial(forward_kernel, sizes, rows), out_shape=...  190 us
    pallas_call x1, Pallas kernels, backward(): pl.pallas_call(functools.partial(backward_kernel, sizes, rows, widths), o...  127 us
    pallas_call x1, Pallas kernels, feed(): pl.pallas_call(functools.partial(feed_kernel, sizes, rows), grid=(FF_CHUN...  97.6 us
    pallas_call x1, Pallas kernels, finish(): pl.pallas_call(functools.partial(finish_kernel, sizes, rows), grid=(PAIRS...  89.1 us
    unnamed x57, local copies, waits for them, and re-layouts  12.7 us

profile of v9, /device:TPU:0, one launch (start us, length us, event | category | flops | bytes accessed | tf_op | source)
XLA Modules:
  0.0 539.7 jit_solution(11237179866009906204)
XLA Ops:
  2.0 0.8 dynamic_update_slice.7
  2.8 0.8 dynamic_update_slice.6
  4.3 0.8 dynamic-slice_reduce_fusion
  7.3 0.8 constant_dynamic-update-slice_fusion.11
  9.5 0.8 constant_dynamic-update-slice_fusion.8
  11.7 0.8 constant_dynamic-update-slice_fusion.5
  13.9 0.8 constant_dynamic-update-slice_fusion.2
  16.3 0.8 pad_maximum_fusion.2
  17.1 1.2 fusion
  18.3 0.9 pad_maximum_fusion.1.sin_ref
  19.2 0.9 pad_maximum_fusion.cos_ref
  20.1 190.1 %forward.1 = (bf16[640,2048]{1,0:T(8,128)(2,1)}, f32[1280,128]{1,0:T(8,128)}, f32[8,640,384]{2,1,0:T(8,128)}, bf16[640,1024]{1,0:T(8,128)(2,1)}, f32[8,1024]{1,0...) custom-call(s32[12]{0:T(128)} %compare_select_fusion.1.meta, ...), custom_call_target="tpu_custom_call" | custom-call | tf_op jit(solution)/shard_map/forward/pallas_call | solution.py:746
  210.2 1.3 copy.47
  212.2 97.6 %feed.1 = (bf16[640,1024]{1,0:T(8,128)(2,1)}, f32[640,1024]{1,0:T(8,128)}, bf16[8,1280,128]{2,1,0:T(8,128)(2,1)}, f32[128,640]{1,0:T(8,128)}, f32[1,1024]{1,0:T(...) custom-call(bf16[640,1024]{1,0:T(8,128)(2,1)} %bitcast.38, ...), custom_call_target="tpu_custom_call" | custom-call | tf_op jit(solution)/shard_map/feed/pallas_call | solution.py:1019
  309.8 0.8 slice.152
  311.5 127.2 %backward.1 = (f32[8,1280,128]{2,1,0:T(8,128)}, f32[2,8,2,320,128]{4,3,2,1,0:T(8,128)}, f32[4,32,1536]{2,1,0:T(8,128)}, f32[32,2048]{1,0:T(8,128)}, bf16[2,320,1024]{2,1,0:T(8,128)(2,1)}) custom-call(s32[12]{0:T(128)} %compare_select_fusion.1.meta, bf16[8,1280,128]{2,1,0:T(8,128)(2,1)} %get-tuple-element.46.q_ref, ...), custom_call_target="tpu_custom_call" | custom-call | tf_op jit(solution)/shard_map/backward/pallas_call | solution.py:1336
  438.7 89.1 %finish.1 = (f32[32,2048]{1,0:T(8,128)}, f32[32,1024]{1,0:T(8,128)}, f32[32,1024]{1,0:T(8,128)}, f32[32,384]{1,0:T(8,128)}, bf16[2,320,1024]{2,1,0:T(8,128)(2,1)}) custom-call(f32[8,1280,128]{2,1,0:T(8,128)} %get-tuple-element.61.dq_ref, f32[2,8,2,320,128]{4,3,2,1,0:T(8,128)} %get-tuple-element.62.dkv_ref, f32[8,640,384]{2,1,0:T(8,128)} %get-tuple-element.63.pre_ref, ...), custom_call_target="tpu_custom_call" | custom-call | tf_op jit(solution)/shard_map/finish/pallas_call | solution.py:1567
  527.8 0.8 fusion.15
  528.5 1.5 slice_reduce_fusion
  531.4 0.8 copy.54
  532.2 0.8 copy.53
  533.0 0.8 copy.52
  533.7 1.8 convert_element_type.20
  535.6 1.1 copy.85
  (80 shorter events, 15.7 us)
Async XLA Ops:
  0.6 0.7 copy-start
  0.7 15.4 %copy-start.11 = (bf16[32,3072]{1,0:T(8,128)(2,1)S(1)}, bf16[32,3072]{1,0:T(8,128)(2,1)}, u32[]{:S(2)}) copy-start(bf16[32,3072]{1,0:T(8,128)(2,1)} %param.30) | copy-start | bytes 589828
  0.7 15.4 %copy-start.10 = (bf16[32,3072]{1,0:T(8,128)(2,1)S(1)}, bf16[32,3072]{1,0:T(8,128)(2,1)}, u32[]{:S(2)}) copy-start(bf16[32,3072]{1,0:T(8,128)(2,1)} %param.29) | copy-start | bytes 589828
  0.7 15.4 %copy-start.12 = (bf16[3072,32]{0,1:T(8,128)(2,1)S(1)}, bf16[3072,32]{0,1:T(8,128)(2,1)}, u32[]{:S(2)}) copy-start(bf16[3072,32]{0,1:T(8,128)(2,1)} %param.31) | copy-start | bytes 589828
  16.1 3.1 copy-start.7
  16.3 3.8 copy-start.5
  438.7 92.5 %copy-start.6 = (f32[2,32,1536]{2,1,0:T(8,128)S(1)}, f32[2,32,1536]{2,1,0:T(8,128)}, u32[]{:S(2)}) copy-start(f32[2,32,1536]{2,1,0:T(8,128)} %get-tuple-element.75) | copy-start | bytes 1179652
  527.8 3.5 copy-start.4
  531.4 2.3 copy-start.3
  533.7 1.8 copy-start.2
  535.6 1.1 copy-start.9
  535.6 1.8 copy-start.14
  535.6 2.5 copy-start.13
  535.6 3.1 copy-start.8
  535.6 3.8 copy-start.1
